TPU v7x, 128 devices: a whole 4x4x4 slice. The times are simulated.
128 devices in a mesh: thinker: 4 (over z), seq: 32 (over y, x, core).
Axes of the slice: x: 4, y: 4, z: 4, core: 2. Of those that a mesh axis runs over, the one named last changes fastest.
Arguments:
- queries: bfloat16 [4, 4096, 2048], P('thinker', 'seq'), may hold values from -6 to 6
- keys: bfloat16 [4, 4096, 512], P('thinker', 'seq'), may hold values from -6 to 6
- values: bfloat16 [4, 4096, 512], P('thinker', 'seq'), may hold values from -6 to 6
- forward_out: bfloat16 [4, 4096, 2048], P('thinker', 'seq'), may hold values from -2 to 2
- logsumexp: float32 [4, 16, 4096], P('thinker', None, 'seq'), may hold values from -1 to 16, as said below
- upstream: bfloat16 [128, 128, 2048], P(None, ('thinker', 'seq')), may hold values from -6 to 6
- lengths: int32 [4], replicated, may hold values from 512 to 4096, as said below
- sibling_mask: int32 [4, 3, 32], P('thinker', None, 'seq'), may hold values from 0 to 1, as said below
Outputs:
- query_grad: bfloat16 [4, 4096, 2048], P('thinker', 'seq')
- key_grad: bfloat16 [4, 4096, 512], P('thinker', 'seq')
- value_grad: bfloat16 [4, 4096, 512], P('thinker', 'seq')
Inputs may be any that keep to these rules, and one draw needn't show every extreme that they name: lengths[t] valid positions stand at the start of thinker t's trace; two thinkers have exactly 4096, one exactly 512. sibling_mask[t, r, b] = 1 where query block b of thinker t reads the recent tokens of thinker (t + r + 1) % 4; the two thinkers of length 4096 read each other in the blocks of the last 128 positions. `logsumexp`: rows of positions past a trace's length carry arbitrary values.
All inputs are finite; a program needn't handle non-finite values.
Results may differ from a plain program's by a relative error of at most 0.014.
Values may be sent and summed in bfloat16 or wider, within the bound.
No kernel may reach another device: no remote copies, remote signals or barrier semaphores. Data moves between devices by JAX's collectives and lax.ppermute only.
A program may use at most 128 MiB of HBM per device.

v0:
```python
import jax
import jax.numpy as jnp
from jax import lax
from jax.experimental import pallas as pl
from jax.experimental.pallas import tpu as pltpu
from jax.sharding import Mesh, PartitionSpec as P


B = 128
HD = 128
GROUP = 4
HEADS = 4
ROWS = GROUP * B
QO = 2 * ROWS + 16
FACTOR = HD**-0.5
LOG2E = 1.4426950408889634
SCALE = FACTOR * LOG2E
DEAD = 1e30
F32 = jnp.float32
BF16 = jnp.bfloat16
SEQ = ("y", "x", "c")
VMEM = pl.BlockSpec(memory_space=pltpu.VMEM)
SMEM = pl.BlockSpec(memory_space=pltpu.SMEM)


def nt(a, b):
    return lax.dot_general(a, b, (((1,), (1,)), ((), ())), preferred_element_type=F32)


def nn(a, b):
    return jnp.dot(a, b, preferred_element_type=F32)


def call(kernel, outs, n_smem, n_vmem, scratch=(), aliases=None):
    return pl.pallas_call(
        kernel,
        out_shape=outs,
        in_specs=[SMEM] * n_smem + [VMEM] * n_vmem,
        out_specs=jax.tree.map(lambda _: VMEM, outs),
        scratch_shapes=list(scratch),
        input_output_aliases=aliases or {},
        compiler_params=pltpu.CompilerParams(vmem_limit_bytes=48 << 20),
    )


def shape(dims, dtype):
    return jax.ShapeDtypeStruct(dims, dtype)


def prep_kv(k_ref, v_ref, *outs):
    y = lax.axis_index("y")
    for d in range(HEADS):
        cols = pl.ds(pl.multiple_of(lax.rem(y + d, 4) * HD, HD), HD)
        outs[d][0] = k_ref[:, cols]
        outs[d][1] = v_ref[:, cols]


def three(x):
    high = x.astype(BF16)
    rest = x - high.astype(F32)
    mid = rest.astype(BF16)
    low = (rest - mid.astype(F32)).astype(BF16)
    return [high.astype(F32), mid.astype(F32), low.astype(F32)]


def prep_qo(mask_ref, q_ref, o_ref, lse_ref, *outs):
    y = lax.axis_index("y")
    marks = [jnp.full((1, HD), mask_ref[n].astype(F32)) for n in range(3)] + [jnp.zeros((1, HD), F32)]
    for d in range(HEADS):
        head = lax.rem(y + d, 4)
        for g in range(GROUP):
            cols = pl.ds(pl.multiple_of((head * GROUP + g) * HD, HD), HD)
            outs[d][g * B : (g + 1) * B, :] = q_ref[:, cols]
            outs[d][ROWS + g * B : ROWS + (g + 1) * B, :] = o_ref[:, cols]
        outs[d][2 * ROWS : QO, :] = jnp.concatenate(three(lse_ref[head]) + marks, axis=0).astype(BF16)


def deal(up_ref, out_ref, wide_ref):
    for t in range(4):
        for c in range(4):
            for i in range(4):
                for g in range(GROUP):
                    cols = slice((c * GROUP + g) * HD, (c * GROUP + g + 1) * HD)
                    block = up_ref[(t * 4 + i) * 8 : (t * 4 + i + 1) * 8, cols]
                    wide_ref[(t * 4 + c) * 8 : (t * 4 + c + 1) * 8, i * GROUP + g, :] = block.astype(F32)
    out_ref[...] = wide_ref[...].astype(BF16)


def prepare(len_ref, g_ref, *refs):
    pieces, (p_ref, stat_ref, mark_ref, wide_ref) = refs[:4], refs[4:]
    y = lax.axis_index("y")
    length = len_ref[lax.axis_index("z")]
    shard = 2 * lax.axis_index("x") + lax.axis_index("c")
    lane = lax.broadcasted_iota(jnp.int32, (GROUP, B), 1)
    wide_ref[...] = g_ref[...].astype(F32)
    for n in range(16):
        p_ref[n // GROUP, ROWS + (n % GROUP) * B : ROWS + (n % GROUP + 1) * B, :] = wide_ref[:, n, :].astype(BF16)
    for d in range(4):
        i = lax.rem(y + 4 - d, 4)
        p_ref[i, 0:ROWS, :] = pieces[d][0:ROWS, :]
        raw = pieces[d][2 * ROWS : QO, :].astype(F32)
        lse = raw[0:4] + raw[4:8] + raw[8:12]
        lse = jnp.where((8 * i + shard) * B + lane < length, lse * LOG2E, DEAD)
        mark_ref[i] = raw[8:16]
        for g in range(GROUP):
            grad = p_ref[i, ROWS + g * B : ROWS + (g + 1) * B, :]
            out = pieces[d][ROWS + g * B : ROWS + (g + 1) * B, :]
            prod = grad.astype(F32) * out.astype(F32)
            stat_ref[i, 0:1, g * B : (g + 1) * B] = jnp.sum(prod.T, axis=0, keepdims=True)
            stat_ref[i, 1:2, g * B : (g + 1) * B] = lse[g : g + 1]


def weigh(keys, vals, p_ref, stat_ref, i, allow, prob_ref, ds_ref):
    q = p_ref[i, 0:ROWS, :]
    grad = p_ref[i, ROWS : 2 * ROWS, :]
    prob = jnp.exp2(nt(keys, q) * SCALE - stat_ref[i, 1:2, :])
    if allow is not None:
        prob = jnp.where(allow, prob, 0.0)
    diff = nt(vals, grad) - stat_ref[i, 0:1, :]
    prob_ref[...] = prob.astype(BF16)
    ds_ref[...] = (prob * diff).astype(BF16)


MS = sum(m << (2 * t) for t, m in enumerate((0, 0, 0, 1, 1, 2, 0, 1, 2, 3)))
QS = sum(i << (2 * t) for t, i in enumerate((1, 2, 3, 2, 3, 3, 0, 1, 2, 3)))


def make_own(dist, first, last):
    def kernel(p_ref, stat_ref, km_ref, ko_ref, *refs):
        if not first:
            dq_in, refs = refs[0], refs[1:]
        dm_ref, do_ref, refs = refs[0], refs[1], refs[2:]
        if last:
            dq_outs, refs = refs[:4], refs[4:]
            kt_ref, dk_ref, dv_ref, p0, s0, p1, s1, acc_ref = refs
        else:
            acc_ref, kt_ref, dk_ref, dv_ref, p0, s0, p1, s1 = refs
        chip = lax.axis_index("x")
        core = lax.axis_index("c")
        y = lax.axis_index("y")
        if first:
            acc_ref[...] = jnp.zeros_like(acc_ref)
        else:
            acc_ref[...] = dq_in[...]
        dk_ref[...] = jnp.zeros_like(dk_ref)
        dv_ref[...] = jnp.zeros_like(dv_ref)
        for m in range(4):
            kt_ref[m] = jnp.concatenate([km_ref[m, 0], ko_ref[m, 0]], axis=0).T
        if dist == 0:
            count = 10
        else:
            count = jnp.where(lax.rem(chip + 4 - dist, 4) < chip, 10, 6)

        def which(t):
            t = jnp.minimum(t, count - 1)
            m = lax.shift_right_logical(jnp.int32(MS), 2 * t) & 3
            i = lax.shift_right_logical(jnp.int32(QS), 2 * t) & 3
            return m, i, (y - m) & 3

        def before(t, prob_ref, ds_ref):
            m, i, slot = which(t)
            keys = jnp.concatenate([km_ref[slot, 0], ko_ref[slot, 0]], axis=0)
            vals = jnp.concatenate([km_ref[slot, 1], ko_ref[slot, 1]], axis=0)
            allow = None
            if dist == 0:
                row = lax.broadcasted_iota(jnp.int32, (2 * B, ROWS), 0)
                col = lax.broadcasted_iota(jnp.int32, (1, ROWS), 1)
                row = jnp.where(core == 0, row, row ^ B)
                allow = row <= core * B + col % B + jnp.where(i > m, 4 * B, 0)
            weigh(keys, vals, p_ref, stat_ref, i, allow, prob_ref, ds_ref)

        def after(t, prob_ref, ds_ref):
            _, i, slot = which(t)
            dv_ref[slot] += nn(prob_ref[...], p_ref[i, ROWS : 2 * ROWS, :])
            dk_ref[slot] += nn(ds_ref[...], p_ref[i, 0:ROWS, :])
            acc_ref[i] += nn(kt_ref[slot], ds_ref[...])

        before(0, p0, s0)

        def two(u, carry):
            before(2 * u + 1, p1, s1)
            after(2 * u, p0, s0)
            before(2 * u + 2, p0, s0)
            after(2 * u + 1, p1, s1)
            return carry

        lax.fori_loop(0, count // 2, two, 0)
        for m in range(4):
            dk = (dk_ref[m] * FACTOR).astype(BF16)
            dv = dv_ref[m].astype(BF16)
            dm_ref[m, 0] = dk[:B]
            dm_ref[m, 1] = dv[:B]
            do_ref[m, 0] = dk[B:]
            do_ref[m, 1] = dv[B:]
        if last:
            for d in range(4):
                dq_outs[d][...] = (acc_ref[(y - d) & 3].T * FACTOR).astype(BF16)

    kv = shape((4, 2, B, HD), BF16)
    dq = [shape((ROWS, HD), BF16)] * 4 if last else [shape((4, HD, ROWS), F32)]
    scratch = [
        pltpu.VMEM((4, HD, 2 * B), BF16),
        pltpu.VMEM((4, 2 * B, HD), F32),
        pltpu.VMEM((4, 2 * B, HD), F32),
    ] + [pltpu.VMEM((2 * B, ROWS), BF16)] * 4
    if last:
        scratch.append(pltpu.VMEM((4, HD, ROWS), F32))
    return call(kernel, (kv, kv, *dq), 0, 4 if first else 5, scratch)


def sibling_kernel(len_ref, p_ref, stat_ref, mark_ref, dq_in, *refs):
    cur, prev, refs = refs[0:3], refs[3:6], refs[6:]
    dcur, dprev, acc_ref, k_ref, v_ref, list_ref, p0, s0, p1, s1 = refs
    thinker = lax.axis_index("z")
    y = lax.axis_index("y")
    shard = 2 * lax.axis_index("x") + lax.axis_index("c")
    length = len_ref[thinker]
    acc_ref[...] = dq_in[...]
    dcur[...] = jnp.zeros_like(dcur)
    dprev[...] = jnp.zeros_like(dprev)
    step = (shard == 0).astype(jnp.int32)
    count = jnp.int32(0)
    for i in range(4):
        slot = (y - i) & 3
        old = (slot + step) & 3
        block = 8 * i + shard
        for n in range(3):
            code = i * 4 + n
            k_ref[code, :B] = prev[n][old, 0]
            k_ref[code, B:] = cur[n][slot, 0]
            v_ref[code, :B] = prev[n][old, 1]
            v_ref[code, B:] = cur[n][slot, 1]
            top = len_ref[(thinker - 1 - n) & 3] - (block - 1) * B
            wanted = jnp.max(mark_ref[i, 6 - n : 7 - n, :]) > 0.5
            list_ref[count] = code
            count = count + (wanted & (block * B < length) & (top > 0)).astype(jnp.int32)
    list_ref[count] = 0
    list_ref[count + 1] = 0
    list_ref[count + 2] = 0

    def before(t, prob_ref, ds_ref):
        code = list_ref[t]
        i, n = code // 4, code & 3
        block = 8 * i + shard
        top = len_ref[(thinker - 1 - n) & 3] - (block - 1) * B
        low = jnp.where(block == 0, B, 0)
        top = jnp.where(t < count, top, 0)
        row = lax.broadcasted_iota(jnp.int32, (2 * B, ROWS), 0)
        col = lax.broadcasted_iota(jnp.int32, (1, ROWS), 1) % B
        allow = (row > jnp.maximum(col, low - 1)) & (row <= jnp.minimum(col + B, top - 1))
        weigh(k_ref[code], v_ref[code], p_ref, stat_ref, i, allow, prob_ref, ds_ref)

    def after(t, prob_ref, ds_ref):
        code = list_ref[t]
        i, n = code // 4, code & 3
        slot = (y - i) & 3
        old = (slot + step) & 3
        dv = nn(prob_ref[...], p_ref[i, ROWS : 2 * ROWS, :])
        dk = nn(ds_ref[...], p_ref[i, 0:ROWS, :]) * FACTOR
        acc_ref[i] += nn(k_ref[code].T, ds_ref[...])
        for kind, grad in ((0, dk), (1, dv)):
            dprev[n, old, kind] = (dprev[n, old, kind].astype(F32) + grad[:B]).astype(BF16)
            dcur[n, slot, kind] = (dcur[n, slot, kind].astype(F32) + grad[B:]).astype(BF16)

    @pl.when(count > 0)
    def _():
        before(0, p0, s0)

        def two(u, carry):
            before(2 * u + 1, p1, s1)
            after(2 * u, p0, s0)
            before(2 * u + 2, p0, s0)
            after(2 * u + 1, p1, s1)
            return carry

        lax.fori_loop(0, (count + 1) // 2, two, 0)


def merge(cur_ref, late_ref, *outs):
    for n in range(3):
        outs[n][...] = (cur_ref[n].astype(F32) + late_ref[n].astype(F32)).astype(BF16)


def gather_terms(*refs):
    terms, outs = refs[:-4], refs[-4:]
    for slot in range(4):
        total = terms[0][slot].astype(F32)
        for term in terms[1:]:
            total = total + term[slot].astype(F32)
        outs[slot][...] = total.astype(BF16)


def finish_q(d0, d1, d2, d3, out):
    y = lax.axis_index("y")
    for d, ref in enumerate((d0, d1, d2, d3)):
        head = lax.rem(y + d, 4)
        for g in range(GROUP):
            cols = pl.ds(pl.multiple_of((head * GROUP + g) * HD, HD), HD)
            out[:, cols] = ref[g * B : (g + 1) * B, :]


def finish_kv(d0, d1, d2, d3, k_out, v_out):
    y = lax.axis_index("y")
    for d, ref in enumerate((d0, d1, d2, d3)):
        cols = pl.ds(pl.multiple_of(lax.rem(y + d, 4) * HD, HD), HD)
        k_out[:, cols] = ref[0]
        v_out[:, cols] = ref[1]


def ring(x, axis, step, count):
    return lax.ppermute(x, axis, [(j, (j + step) % count) for j in range(count)])


def step(queries, keys, values, forward_out, logsumexp, upstream, lengths, sibling_mask):
    kv = shape((4, 2, B, HD), BF16)
    piece = shape((2, B, HD), BF16)
    row = shape((B, 512), BF16)
    core = ("x", "c")
    dists = (1, 2, 3)
    kv_sent = call(prep_kv, (piece,) * 4, 0, 2)(keys[0], values[0])
    kv_own = jnp.stack([kv_sent[0]] + [ring(kv_sent[d], "y", d, 4) for d in dists])
    qo_sent = call(prep_qo, (shape((QO, HD), BF16),) * 4, 1, 3)(
        sibling_mask.reshape(3), queries[0], forward_out[0], logsumexp.reshape(4, GROUP, B)
    )
    qo = [qo_sent[0]] + [ring(qo_sent[d], "y", d, 4) for d in dists]
    near = [kv_own] + [ring(kv_own, "x", d, 4) for d in dists]
    cur = [ring(kv_own, "z", d, 4) for d in dists]
    dealt = call(deal, shape((128, 16, HD), BF16), 0, 1, [pltpu.VMEM((128, 16, HD), F32)])(
        upstream.reshape(128, 2048)
    )
    arrived = lax.all_to_all(dealt, ("z", "y", "x", "c"), 0, 0, tiled=True)
    far = [ring(near[d], "c", 1, 2) for d in range(4)]
    prev = [ring(k, core, 1, 8) for k in cur]
    pay, stat, mark = call(
        prepare,
        (shape((4, 2 * ROWS, HD), BF16), shape((4, 2, ROWS), F32), shape((4, 8, HD), F32)),
        1,
        5,
        [pltpu.VMEM((128, 16, HD), F32)],
    )(lengths, arrived, *qo)
    mine, other, dq = {}, {}, None
    mine[2], other[2], dq = make_own(2, True, False)(pay, stat, near[2], far[2])
    trio = shape((3, 4, 2, B, HD), BF16)
    scratch = [pltpu.VMEM((16, 2 * B, HD), BF16)] * 2 + [pltpu.SMEM((16,), jnp.int32)]
    scratch += [pltpu.VMEM((2 * B, ROWS), BF16)] * 4
    sibling = call(sibling_kernel, (trio, trio, shape((4, HD, ROWS), F32)), 1, 10, scratch)
    dcur, dprev, dq = sibling(lengths, pay, stat, mark, dq, *cur, *prev)
    mine[3], other[3], dq = make_own(3, False, False)(pay, stat, near[3], far[3], dq)
    mine[1], other[1], dq = make_own(1, False, False)(pay, stat, near[1], far[1], dq)
    mine[0], other[0], *dq_sent = make_own(0, False, True)(pay, stat, near[0], far[0], dq)
    terms = [mine[0], ring(other[0], "c", 1, 2)]
    for d in (2, 1, 3):
        both = mine[d].astype(F32) + ring(other[d], "c", 1, 2).astype(F32)
        terms.append(ring(both.astype(BF16), "x", -d, 4))
    late = ring(dprev, core, -1, 8)
    merged = call(merge, (kv,) * 3, 0, 2)(dcur, late)
    terms += [ring(merged[d - 1], "z", -d, 4) for d in dists]
    dq_got = [dq_sent[0]] + [ring(dq_sent[d], "y", -d, 4) for d in dists]
    q_grad = call(finish_q, (shape((B, 2048), BF16),), 0, 4)(*dq_got)[0]
    kv_out = call(gather_terms, (piece,) * 4, 0, 8)(*terms)
    kv_got = [kv_out[0]] + [ring(kv_out[d], "y", -d, 4) for d in dists]
    k_grad, v_grad = call(finish_kv, (row, row), 0, 4)(*kv_got)
    return q_grad[None], k_grad[None], v_grad[None]


def solution(mesh):
    grid = Mesh(mesh.devices.reshape(4, 4, 4, 2), ("z",) + SEQ)
    rows = P("z", SEQ, None)
    return jax.shard_map(
        step,
        mesh=grid,
        in_specs=(
            rows,
            rows,
            rows,
            rows,
            P("z", None, SEQ),
            P(None, ("z",) + SEQ, None),
            P(),
            P("z", None, SEQ),
        ),
        out_specs=(rows, rows, rows),
        check_vma=False,
    )
```

profile of v0, /device:TPU:0, one launch (start us, length us, event | category | flops | bytes accessed | tf_op | source)
XLA Modules:
  0.0 114.2 jit_solution(3178913193901998903)
XLA Ops:
  2.5 3.2 %collective-permute-start.5 = (bf16[2,128,128]{2,1,0:T(8,128)(2,1)S(1)}, bf16[2,128,128]{2,1,0:T(8,128)(2,1)S(1)}, u32[]{:S(2)}, u32[]{:S(2)}) collective-permute-start(bf16[2,128,128]{2,1,0:T(8,128)(2,1)S(1)} %get-tuple-element.50), channel_id=1, source_target_pairs={{0,24},{8,0},{16,8},{24,16},{1,25},{9,1},{17,9},{25,17},{2,26},{10... | collective-permute-start | bytes 196616 | tf_op jit(solution)/shard_map/ppermute | solution.py:311
  5.7 2.2 %collective-permute-start.4 = (bf16[2,128,128]{2,1,0:T(8,128)(2,1)S(1)}, bf16[2,128,128]{2,1,0:T(8,128)(2,1)S(1)}, u32[]{:S(2)}, u32[]{:S(2)}) collective-permute-start(bf16[2,128,128]{2,1,0:T(8,128)(2,1)S(1)} %get-tuple-element.49), channel_id=1, source_target_pairs={{0,16},{8,24},{16,0},{24,8},{1,17},{9,25},{17,1},{25,9},{2,18},{10... | collective-permute-start | bytes 196616 | tf_op jit(solution)/shard_map/ppermute | solution.py:311
  11.5 2.0 %collective-permute-start = (bf16[1040,128]{1,0:T(8,128)(2,1)S(1)}, bf16[1040,128]{1,0:T(8,128)(2,1)S(1)}, u32[]{:S(2)}, u32[]{:S(2)}) collective-permute-start(bf16[1040,128]{1,0:T(8,128)(2,1)S(1)} %get-tuple-element.42), channel_id=1, source_target_pairs={{0,8},{8,16},{16,24},{24,0},{1,9},{9,17},{17,25},{25,1},{2,10},{10... | collective-permute-start | bytes 798728 | tf_op jit(solution)/shard_map/ppermute | solution.py:311
  14.1 2.1 %collective-permute-start.2 = (bf16[1040,128]{1,0:T(8,128)(2,1)S(1)}, bf16[1040,128]{1,0:T(8,128)(2,1)S(1)}, u32[]{:S(2)}, u32[]{:S(2)}) collective-permute-start(bf16[1040,128]{1,0:T(8,128)(2,1)S(1)} %get-tuple-element.44), channel_id=1, source_target_pairs={{0,24},{8,0},{16,8},{24,16},{1,25},{9,1},{17,9},{25,17},{2,26},{10... | collective-permute-start | bytes 798728 | tf_op jit(solution)/shard_map/ppermute | solution.py:311
  16.3 3.1 %collective-permute-start.11 = (bf16[4,2,128,128]{3,2,1,0:T(8,128)(2,1)S(1)}, bf16[4,2,128,128]{3,2,1,0:T(8,128)(2,1)S(1)}, u32[]{:S(2)}, u32[]{:S(2)}) collective-permute-start(bf16[4,2,128,128]{3,2,1,0:T(8,128)(2,1)S(1)} %pad_maximum_fusion.km_ref), channel_id=1, source_target_pairs={{0,4},{2,6},{4,0},{6,2},{1,5},{3,7},{5,1},{7,3},{8,12},{10,14},{12... | collective-permute-start | bytes 786440 | tf_op jit(solution)/shard_map/ppermute | solution.py:311
  19.4 1.9 %collective-permute-start.13 = (bf16[4,2,128,128]{3,2,1,0:T(8,128)(2,1)S(1)}, bf16[4,2,128,128]{3,2,1,0:T(8,128)(2,1)S(1)}, u32[]{:S(2)}, u32[]{:S(2)}) collective-permute-start(bf16[4,2,128,128]{3,2,1,0:T(8,128)(2,1)S(1)} %pad_maximum_fusion.km_ref), channel_id=1, source_target_pairs={{0,32},{32,64},{64,96},{96,0},{1,33},{33,65},{65,97},{97,1},{2,34}... | collective-permute-start | bytes 786440 | tf_op jit(solution)/shard_map/ppermute | solution.py:311
  21.3 4.5 %collective-permute-done.refs_1_ = bf16[1040,128]{1,0:T(8,128)(2,1)S(1)} collective-permute-done((bf16[1040,128]{1,0:T(8,128)(2,1)S(1)}, bf16[1040,128]{1,0:T(8,128)(2,1)S(1)}, u32[]{:S(2)}, u32[]{:S(2)}) %collective-permute-start) | collective-permute-done | bytes 266272 | tf_op jit(solution)/shard_map/ppermute | solution.py:311
  25.8 3.9 %collective-permute-start.14 = (bf16[4,2,128,128]{3,2,1,0:T(8,128)(2,1)S(1)}, bf16[4,2,128,128]{3,2,1,0:T(8,128)(2,1)S(1)}, u32[]{:S(2)}, u32[]{:S(2)}) collective-permute-start(bf16[4,2,128,128]{3,2,1,0:T(8,128)(2,1)S(1)} %pad_maximum_fusion.km_ref), channel_id=1, source_target_pairs={{0,64},{32,96},{64,0},{96,32},{1,65},{33,97},{65,1},{97,33},{2,66}... | collective-permute-start | bytes 786440 | tf_op jit(solution)/shard_map/ppermute | solution.py:311
  30.4 2.8 %collective-permute-start.9 = (bf16[4,2,128,128]{3,2,1,0:T(8,128)(2,1)S(1)}, bf16[4,2,128,128]{3,2,1,0:T(8,128)(2,1)S(1)}, u32[]{:S(2)}, u32[]{:S(2)}) collective-permute-start(bf16[4,2,128,128]{3,2,1,0:T(8,128)(2,1)S(1)} %pad_maximum_fusion.km_ref), channel_id=1, source_target_pairs={{0,6},{2,0},{4,2},{6,4},{1,7},{3,1},{5,3},{7,5},{8,14},{10,8},{12,... | collective-permute-start | bytes 786440 | tf_op jit(solution)/shard_map/ppermute | solution.py:311
  34.6 7.0 %all-to-all-start = ((bf16[128,16,128]{2,1,0:T(8,128)(2,1)}), bf16[128,16,128]{2,1,0:T(8,128)(2,1)S(1)}, u32[]{:S(2)}, u32[]{:S(2)}) async-start(bf16[128,16,128]{2,1,0:T(8,128)(2,1)} %shard_map.103), calls=%async_computation | async-start | bytes 1048576 | tf_op jit(solution)/shard_map/all_to_all | solution.py:331
  45.1 10.5 %all-to-all-done.g_ref = bf16[128,16,128]{2,1,0:T(8,128)(2,1)S(1)} async-done(((bf16[128,16,128]{2,1,0:T(8,128)(2,1)}), bf16[128,16,128]{2,1,0:T(8,128)(2,1)S(1)}, u32[]{:S(2)}, u32[]{:S(2)}) %all-to-all-start) | async-done | bytes 524320 | tf_op jit(solution)/shard_map/all_to_all | solution.py:331
  55.6 2.0 %shard_map.105 = (bf16[4,1024,128]{2,1,0:T(8,128)(2,1)S(1)}, f32[4,2,512]{2,1,0:T(2,128)S(1)}, f32[4,8,128]{2,1,0:T(8,128)S(1)}) custom-call(s32[4]{0:T(128)S(1)} %copy-done.9, bf16[128,16,128]{2,1,0:T(8,128)(2,1)S(1)} %all-to-all-done.g_ref, bf16[1040,128]{1,0:T(8,128)(2,1)S(1)} %get-tuple-element.41.refs_0_, ...), custom_call_target="tpu_custom_call" | custom-call | tf_op jit(solution)/shard_map/pallas_call | solution.py:334
  57.6 2.8 %shard_map.107 = (bf16[4,2,128,128]{3,2,1,0:T(8,128)(2,1)S(1)}, bf16[4,2,128,128]{3,2,1,0:T(8,128)(2,1)S(1)}, f32[4,128,512]{2,1,0:T(8,128)S(1)}) custom-call(bf16[4,1024,128]{2,1,0:T(8,128)(2,1)S(1)} %get-tuple-element.45.p_ref, f32[4,2,512]{2,1,0:T(2,128)S(1)} %get-tuple-element.46.stat_ref, bf16[4,2,128,128]{3,2,1,0:T(8,128)(2,1)S(1)} %collective-permute-done.11.km_ref, ...), custom_call_target="tpu_custom_call" | custom-call | tf_op jit(solution)/shard_map/pallas_call | solution.py:342
  63.4 4.0 %shard_map.109 = (bf16[4,2,128,128]{3,2,1,0:T(8,128)(2,1)S(1)}, bf16[4,2,128,128]{3,2,1,0:T(8,128)(2,1)S(1)}, f32[4,128,512]{2,1,0:T(8,128)S(1)}) custom-call(bf16[4,1024,128]{2,1,0:T(8,128)(2,1)S(1)} %get-tuple-element.45.p_ref, f32[4,2,512]{2,1,0:T(2,128)S(1)} %get-tuple-element.46.stat_ref, bf16[4,2,128,128]{3,2,1,0:T(8,128)(2,1)S(1)} %collective-permute-done.9.km_ref, ...), custom_call_target="tpu_custom_call" | custom-call | tf_op jit(solution)/shard_map/pallas_call | solution.py:348
  67.4 1.9 %collective-permute-start.27 = (bf16[4,2,128,128]{3,2,1,0:T(8,128)(2,1)S(1)}, bf16[4,2,128,128]{3,2,1,0:T(8,128)(2,1)S(1)}, u32[]{:S(2)}, u32[]{:S(2)}) collective-permute-start(bf16[4,2,128,128]{3,2,1,0:T(8,128)(2,1)S(1)} %get-tuple-element.67), channel_id=1, source_target_pairs={{0,1},{1,0},{2,3},{3,2},{4,5},{5,4},{6,7},{7,6},{8,9},{9,8},{10,11... | collective-permute-start | bytes 786440 | tf_op jit(solution)/shard_map/ppermute | solution.py:311
  69.3 2.0 %collective-permute-start.29 = (bf16[3,4,2,128,128]{4,3,2,1,0:T(8,128)(2,1)S(1)}, bf16[3,4,2,128,128]{4,3,2,1,0:T(8,128)(2,1)S(1)}, u32[]{:S(2)}, u32[]{:S(2)}) collective-permute-start(bf16[3,4,2,128,128]{4,3,2,1,0:T(8,128)(2,1)S(1)} %get-tuple-element.69), channel_id=1, source_target_pairs={{0,7},{1,0},{2,1},{3,2},{4,3},{5,4},{6,5},{7,6},{8,15},{9,8},{10,9... | collective-permute-start | bytes 2359304 | tf_op jit(solution)/shard_map/ppermute | solution.py:311
  71.3 3.9 %shard_map.110 = (bf16[4,2,128,128]{3,2,1,0:T(8,128)(2,1)S(1)}, bf16[4,2,128,128]{3,2,1,0:T(8,128)(2,1)S(1)}, f32[4,128,512]{2,1,0:T(8,128)S(1)}) custom-call(bf16[4,1024,128]{2,1,0:T(8,128)(2,1)S(1)} %get-tuple-element.45.p_ref, f32[4,2,512]{2,1,0:T(2,128)S(1)} %get-tuple-element.46.stat_ref, bf16[4,2,128,128]{3,2,1,0:T(8,128)(2,1)S(1)} %collective-permute-done.7.km_ref, ...), custom_call_target="tpu_custom_call" | custom-call | tf_op jit(solution)/shard_map/pallas_call | solution.py:349
  75.3 5.0 %shard_map.111 = (bf16[4,2,128,128]{3,2,1,0:T(8,128)(2,1)S(1)}, bf16[4,2,128,128]{3,2,1,0:T(8,128)(2,1)S(1)}, bf16[512,128]{1,0:T(8,128)(2,1)S(1)}, bf16[512,128...) custom-call(bf16[4,1024,128]{2,1,0:T(8,128)(2,1)S(1)} %get-tuple-element.45.p_ref, ...), custom_call_target="tpu_custom_call" | custom-call | tf_op jit(solution)/shard_map/pallas_call | solution.py:350
  82.5 2.1 %collective-permute-start.26 = (bf16[4,2,128,128]{3,2,1,0:T(8,128)(2,1)S(1)}, bf16[4,2,128,128]{3,2,1,0:T(8,128)(2,1)S(1)}, u32[]{:S(2)}, u32[]{:S(2)}) collective-permute-start(bf16[4,2,128,128]{3,2,1,0:T(8,128)(2,1)S(1)} %add_convert_fusion.1), channel_id=1, source_target_pairs={{0,6},{2,0},{4,2},{6,4},{1,7},{3,1},{5,3},{7,5},{8,14},{10,8},{12,... | collective-permute-start | bytes 786440 | tf_op jit(solution)/shard_map/ppermute | solution.py:311
  85.6 3.7 %collective-permute-start.30 = (bf16[4,2,128,128]{3,2,1,0:T(8,128)(2,1)S(1)}, bf16[4,2,128,128]{3,2,1,0:T(8,128)(2,1)S(1)}, u32[]{:S(2)}, u32[]{:S(2)}) collective-permute-start(bf16[4,2,128,128]{3,2,1,0:T(8,128)(2,1)S(1)} %get-tuple-element.70), channel_id=1, source_target_pairs={{0,96},{32,0},{64,32},{96,64},{1,97},{33,1},{65,33},{97,65},{2,98}... | collective-permute-start | bytes 786440 | tf_op jit(solution)/shard_map/ppermute | solution.py:311
  89.3 2.5 %collective-permute-start.31 = (bf16[4,2,128,128]{3,2,1,0:T(8,128)(2,1)S(1)}, bf16[4,2,128,128]{3,2,1,0:T(8,128)(2,1)S(1)}, u32[]{:S(2)}, u32[]{:S(2)}) collective-permute-start(bf16[4,2,128,128]{3,2,1,0:T(8,128)(2,1)S(1)} %get-tuple-element.71), channel_id=1, source_target_pairs={{0,64},{32,96},{64,0},{96,32},{1,65},{33,97},{65,1},{97,33},{2,66}... | collective-permute-start | bytes 786440 | tf_op jit(solution)/shard_map/ppermute | solution.py:311
  91.8 3.9 %collective-permute-start.32 = (bf16[4,2,128,128]{3,2,1,0:T(8,128)(2,1)S(1)}, bf16[4,2,128,128]{3,2,1,0:T(8,128)(2,1)S(1)}, u32[]{:S(2)}, u32[]{:S(2)}) collective-permute-start(bf16[4,2,128,128]{3,2,1,0:T(8,128)(2,1)S(1)} %get-tuple-element.72), channel_id=1, source_target_pairs={{0,32},{32,64},{64,96},{96,0},{1,33},{33,65},{65,97},{97,1},{2,34}... | collective-permute-start | bytes 786440 | tf_op jit(solution)/shard_map/ppermute | solution.py:311
  99.6 5.5 %collective-permute-done.32.refs_7_ = bf16[4,2,128,128]{3,2,1,0:T(8,128)(2,1)S(1)} collective-permute-done((bf16[4,2,128,128]{3,2,1,0:T(8,128)(2,1)S(1)}, bf16[4,2,128,128]{3,2,1,0:T(8,128)(2,1)S(1)}, u32[]{:S(2)}, u32[]{:S(2)}) %collective-permute-start.32) | collective-permute-done | bytes 262176 | tf_op jit(solution)/shard_map/ppermute | solution.py:311
  109.7 2.2 %collective-permute-done.34.d2 = bf16[2,128,128]{2,1,0:T(8,128)(2,1)S(1)} collective-permute-done((bf16[2,128,128]{2,1,0:T(8,128)(2,1)S(1)}, bf16[2,128,128]{2,1,0:T(8,128)(2,1)S(1)}, u32[]{:S(2)}, u32[]{:S(2)}) %collective-permute-start.34) | collective-permute-done | bytes 65568 | tf_op jit(solution)/shard_map/ppermute | solution.py:311
  (89 shorter events, 28.6 us)
Async XLA Ops:
  2.5 11.6 %collective-permute-start.5 = (bf16[2,128,128]{2,1,0:T(8,128)(2,1)S(1)}, bf16[2,128,128]{2,1,0:T(8,128)(2,1)S(1)}, u32[]{:S(2)}, u32[]{:S(2)}) collective-permute-start(bf16[2,128,128]{2,1,0:T(8,128)(2,1)S(1)} %get-tuple-element.50), channel_id=1, source_target_pairs={{0,24},{8,0},{16,8},{24,16},{1,25},{9,1},{17,9},{25,17},{2,26},{10... | collective-permute-start | bytes 196616 | tf_op jit(solution)/shard_map/ppermute | solution.py:311
  11.5 14.3 %collective-permute-start = (bf16[1040,128]{1,0:T(8,128)(2,1)S(1)}, bf16[1040,128]{1,0:T(8,128)(2,1)S(1)}, u32[]{:S(2)}, u32[]{:S(2)}) collective-permute-start(bf16[1040,128]{1,0:T(8,128)(2,1)S(1)} %get-tuple-element.42), channel_id=1, source_target_pairs={{0,8},{8,16},{16,24},{24,0},{1,9},{9,17},{17,25},{25,1},{2,10},{10... | collective-permute-start | bytes 798728 | tf_op jit(solution)/shard_map/ppermute | solution.py:311
  13.5 16.2 %collective-permute-start.1 = (bf16[1040,128]{1,0:T(8,128)(2,1)S(1)}, bf16[1040,128]{1,0:T(8,128)(2,1)S(1)}, u32[]{:S(2)}, u32[]{:S(2)}) collective-permute-start(bf16[1040,128]{1,0:T(8,128)(2,1)S(1)} %get-tuple-element.43), channel_id=1, source_target_pairs={{0,16},{8,24},{16,0},{24,8},{1,17},{9,25},{17,1},{25,9},{2,18},{10... | collective-permute-start | bytes 798728 | tf_op jit(solution)/shard_map/ppermute | solution.py:311
  14.1 16.3 %collective-permute-start.2 = (bf16[1040,128]{1,0:T(8,128)(2,1)S(1)}, bf16[1040,128]{1,0:T(8,128)(2,1)S(1)}, u32[]{:S(2)}, u32[]{:S(2)}) collective-permute-start(bf16[1040,128]{1,0:T(8,128)(2,1)S(1)} %get-tuple-element.44), channel_id=1, source_target_pairs={{0,24},{8,0},{16,8},{24,16},{1,25},{9,1},{17,9},{25,17},{2,26},{10... | collective-permute-start | bytes 798728 | tf_op jit(solution)/shard_map/ppermute | solution.py:311
  16.3 16.9 %collective-permute-start.11 = (bf16[4,2,128,128]{3,2,1,0:T(8,128)(2,1)S(1)}, bf16[4,2,128,128]{3,2,1,0:T(8,128)(2,1)S(1)}, u32[]{:S(2)}, u32[]{:S(2)}) collective-permute-start(bf16[4,2,128,128]{3,2,1,0:T(8,128)(2,1)S(1)} %pad_maximum_fusion.km_ref), channel_id=1, source_target_pairs={{0,4},{2,6},{4,0},{6,2},{1,5},{3,7},{5,1},{7,3},{8,12},{10,14},{12... | collective-permute-start | bytes 786440 | tf_op jit(solution)/shard_map/ppermute | solution.py:311
  19.4 22.2 %collective-permute-start.13 = (bf16[4,2,128,128]{3,2,1,0:T(8,128)(2,1)S(1)}, bf16[4,2,128,128]{3,2,1,0:T(8,128)(2,1)S(1)}, u32[]{:S(2)}, u32[]{:S(2)}) collective-permute-start(bf16[4,2,128,128]{3,2,1,0:T(8,128)(2,1)S(1)} %pad_maximum_fusion.km_ref), channel_id=1, source_target_pairs={{0,32},{32,64},{64,96},{96,0},{1,33},{33,65},{65,97},{97,1},{2,34}... | collective-permute-start | bytes 786440 | tf_op jit(solution)/shard_map/ppermute | solution.py:311
  25.8 15.9 %collective-permute-start.14 = (bf16[4,2,128,128]{3,2,1,0:T(8,128)(2,1)S(1)}, bf16[4,2,128,128]{3,2,1,0:T(8,128)(2,1)S(1)}, u32[]{:S(2)}, u32[]{:S(2)}) collective-permute-start(bf16[4,2,128,128]{3,2,1,0:T(8,128)(2,1)S(1)} %pad_maximum_fusion.km_ref), channel_id=1, source_target_pairs={{0,64},{32,96},{64,0},{96,32},{1,65},{33,97},{65,1},{97,33},{2,66}... | collective-permute-start | bytes 786440 | tf_op jit(solution)/shard_map/ppermute | solution.py:311
  29.7 12.5 %collective-permute-start.15 = (bf16[4,2,128,128]{3,2,1,0:T(8,128)(2,1)S(1)}, bf16[4,2,128,128]{3,2,1,0:T(8,128)(2,1)S(1)}, u32[]{:S(2)}, u32[]{:S(2)}) collective-permute-start(bf16[4,2,128,128]{3,2,1,0:T(8,128)(2,1)S(1)} %pad_maximum_fusion.km_ref), channel_id=1, source_target_pairs={{0,96},{32,0},{64,32},{96,64},{1,97},{33,1},{65,33},{97,65},{2,98}... | collective-permute-start | bytes 786440 | tf_op jit(solution)/shard_map/ppermute | solution.py:311
  30.4 12.5 %collective-permute-start.9 = (bf16[4,2,128,128]{3,2,1,0:T(8,128)(2,1)S(1)}, bf16[4,2,128,128]{3,2,1,0:T(8,128)(2,1)S(1)}, u32[]{:S(2)}, u32[]{:S(2)}) collective-permute-start(bf16[4,2,128,128]{3,2,1,0:T(8,128)(2,1)S(1)} %pad_maximum_fusion.km_ref), channel_id=1, source_target_pairs={{0,6},{2,0},{4,2},{6,4},{1,7},{3,1},{5,3},{7,5},{8,14},{10,8},{12,... | collective-permute-start | bytes 786440 | tf_op jit(solution)/shard_map/ppermute | solution.py:311
  34.6 21.1 %all-to-all-start = ((bf16[128,16,128]{2,1,0:T(8,128)(2,1)}), bf16[128,16,128]{2,1,0:T(8,128)(2,1)S(1)}, u32[]{:S(2)}, u32[]{:S(2)}) async-start(bf16[128,16,128]{2,1,0:T(8,128)(2,1)} %shard_map.103), calls=%async_computation | async-start | bytes 1048576 | tf_op jit(solution)/shard_map/all_to_all | solution.py:331
  41.7 19.8 %collective-permute-start.16 = (bf16[4,2,128,128]{3,2,1,0:T(8,128)(2,1)S(1)}, bf16[4,2,128,128]{3,2,1,0:T(8,128)(2,1)}, u32[]{:S(2)}, u32[]{:S(2)}) collective-permute-start(bf16[4,2,128,128]{3,2,1,0:T(8,128)(2,1)S(1)} %collective-permute-done.13.refs_0_), channel_id=1, source_target_pairs={{0,1},{1,2},{2,3},{3,4},{4,5},{5,6},{6,7},{7,0},{8,9},{9,10},{10,1... | collective-permute-start | bytes 786440 | tf_op jit(solution)/shard_map/ppermute | solution.py:311
  42.2 19.3 %collective-permute-start.17 = (bf16[4,2,128,128]{3,2,1,0:T(8,128)(2,1)S(1)}, bf16[4,2,128,128]{3,2,1,0:T(8,128)(2,1)}, u32[]{:S(2)}, u32[]{:S(2)}) collective-permute-start(bf16[4,2,128,128]{3,2,1,0:T(8,128)(2,1)S(1)} %collective-permute-done.14.refs_1_), channel_id=1, source_target_pairs={{0,1},{1,2},{2,3},{3,4},{4,5},{5,6},{6,7},{7,0},{8,9},{9,10},{10,1... | collective-permute-start | bytes 786440 | tf_op jit(solution)/shard_map/ppermute | solution.py:311
  42.8 18.7 %collective-permute-start.18 = (bf16[4,2,128,128]{3,2,1,0:T(8,128)(2,1)S(1)}, bf16[4,2,128,128]{3,2,1,0:T(8,128)(2,1)}, u32[]{:S(2)}, u32[]{:S(2)}) collective-permute-start(bf16[4,2,128,128]{3,2,1,0:T(8,128)(2,1)S(1)} %collective-permute-done.15.refs_2_), channel_id=1, source_target_pairs={{0,1},{1,2},{2,3},{3,4},{4,5},{5,6},{6,7},{7,0},{8,9},{9,10},{10,1... | collective-permute-start | bytes 786440 | tf_op jit(solution)/shard_map/ppermute | solution.py:311
  43.2 20.1 %collective-permute-start.10 = (bf16[4,2,128,128]{3,2,1,0:T(8,128)(2,1)S(1)}, bf16[4,2,128,128]{3,2,1,0:T(8,128)(2,1)}, u32[]{:S(2)}, u32[]{:S(2)}) collective-permute-start(bf16[4,2,128,128]{3,2,1,0:T(8,128)(2,1)S(1)} %collective-permute-done.9.km_ref), channel_id=1, source_target_pairs={{0,1},{1,0},{2,3},{3,2},{4,5},{5,4},{6,7},{7,6},{8,9},{9,8},{10,11... | collective-permute-start | bytes 786440 | tf_op jit(solution)/shard_map/ppermute | solution.py:311
  45.1 26.2 %collective-permute-start.8 = (bf16[4,2,128,128]{3,2,1,0:T(8,128)(2,1)S(1)}, bf16[4,2,128,128]{3,2,1,0:T(8,128)(2,1)}, u32[]{:S(2)}, u32[]{:S(2)}) collective-permute-start(bf16[4,2,128,128]{3,2,1,0:T(8,128)(2,1)S(1)} %collective-permute-done.7.km_ref), channel_id=1, source_target_pairs={{0,1},{1,0},{2,3},{3,2},{4,5},{5,4},{6,7},{7,6},{8,9},{9,8},{10,11... | collective-permute-start | bytes 786440 | tf_op jit(solution)/shard_map/ppermute | solution.py:311
  61.5 13.8 %collective-permute-start.6 = (bf16[4,2,128,128]{3,2,1,0:T(8,128)(2,1)S(1)}, bf16[4,2,128,128]{3,2,1,0:T(8,128)(2,1)S(1)}, u32[]{:S(2)}, u32[]{:S(2)}) collective-permute-start(bf16[4,2,128,128]{3,2,1,0:T(8,128)(2,1)S(1)} %pad_maximum_fusion.km_ref), channel_id=1, source_target_pairs={{0,1},{1,0},{2,3},{3,2},{4,5},{5,4},{6,7},{7,6},{8,9},{9,8},{10,11... | collective-permute-start | bytes 786440 | tf_op jit(solution)/shard_map/ppermute | solution.py:311
  67.4 13.6 %collective-permute-start.27 = (bf16[4,2,128,128]{3,2,1,0:T(8,128)(2,1)S(1)}, bf16[4,2,128,128]{3,2,1,0:T(8,128)(2,1)S(1)}, u32[]{:S(2)}, u32[]{:S(2)}) collective-permute-start(bf16[4,2,128,128]{3,2,1,0:T(8,128)(2,1)S(1)} %get-tuple-element.67), channel_id=1, source_target_pairs={{0,1},{1,0},{2,3},{3,2},{4,5},{5,4},{6,7},{7,6},{8,9},{9,8},{10,11... | collective-permute-start | bytes 786440 | tf_op jit(solution)/shard_map/ppermute | solution.py:311
  69.3 16.1 %collective-permute-start.29 = (bf16[3,4,2,128,128]{4,3,2,1,0:T(8,128)(2,1)S(1)}, bf16[3,4,2,128,128]{4,3,2,1,0:T(8,128)(2,1)S(1)}, u32[]{:S(2)}, u32[]{:S(2)}) collective-permute-start(bf16[3,4,2,128,128]{4,3,2,1,0:T(8,128)(2,1)S(1)} %get-tuple-element.69), channel_id=1, source_target_pairs={{0,7},{1,0},{2,1},{3,2},{4,3},{5,4},{6,5},{7,6},{8,15},{9,8},{10,9... | collective-permute-start | bytes 2359304 | tf_op jit(solution)/shard_map/ppermute | solution.py:311
  82.5 13.6 %collective-permute-start.26 = (bf16[4,2,128,128]{3,2,1,0:T(8,128)(2,1)S(1)}, bf16[4,2,128,128]{3,2,1,0:T(8,128)(2,1)S(1)}, u32[]{:S(2)}, u32[]{:S(2)}) collective-permute-start(bf16[4,2,128,128]{3,2,1,0:T(8,128)(2,1)S(1)} %add_convert_fusion.1), channel_id=1, source_target_pairs={{0,6},{2,0},{4,2},{6,4},{1,7},{3,1},{5,3},{7,5},{8,14},{10,8},{12,... | collective-permute-start | bytes 786440 | tf_op jit(solution)/shard_map/ppermute | solution.py:311
  84.6 12.3 %collective-permute-start.24 = (bf16[4,2,128,128]{3,2,1,0:T(8,128)(2,1)S(1)}, bf16[4,2,128,128]{3,2,1,0:T(8,128)(2,1)S(1)}, u32[]{:S(2)}, u32[]{:S(2)}) collective-permute-start(bf16[4,2,128,128]{3,2,1,0:T(8,128)(2,1)S(1)} %add_convert_fusion.2), channel_id=1, source_target_pairs={{0,4},{2,6},{4,0},{6,2},{1,5},{3,7},{5,1},{7,3},{8,12},{10,14},{12... | collective-permute-start | bytes 786440 | tf_op jit(solution)/shard_map/ppermute | solution.py:311
  85.6 13.0 %collective-permute-start.30 = (bf16[4,2,128,128]{3,2,1,0:T(8,128)(2,1)S(1)}, bf16[4,2,128,128]{3,2,1,0:T(8,128)(2,1)S(1)}, u32[]{:S(2)}, u32[]{:S(2)}) collective-permute-start(bf16[4,2,128,128]{3,2,1,0:T(8,128)(2,1)S(1)} %get-tuple-element.70), channel_id=1, source_target_pairs={{0,96},{32,0},{64,32},{96,64},{1,97},{33,1},{65,33},{97,65},{2,98}... | collective-permute-start | bytes 786440 | tf_op jit(solution)/shard_map/ppermute | solution.py:311
  91.8 13.3 %collective-permute-start.32 = (bf16[4,2,128,128]{3,2,1,0:T(8,128)(2,1)S(1)}, bf16[4,2,128,128]{3,2,1,0:T(8,128)(2,1)S(1)}, u32[]{:S(2)}, u32[]{:S(2)}) collective-permute-start(bf16[4,2,128,128]{3,2,1,0:T(8,128)(2,1)S(1)} %get-tuple-element.72), channel_id=1, source_target_pairs={{0,32},{32,64},{64,96},{96,0},{1,33},{33,65},{65,97},{97,1},{2,34}... | collective-permute-start | bytes 786440 | tf_op jit(solution)/shard_map/ppermute | solution.py:311
  96.1 11.9 %collective-permute-start.19 = (bf16[512,128]{1,0:T(8,128)(2,1)S(1)}, bf16[512,128]{1,0:T(8,128)(2,1)S(1)}, u32[]{:S(2)}, u32[]{:S(2)}) collective-permute-start(bf16[512,128]{1,0:T(8,128)(2,1)S(1)} %get-tuple-element.57), channel_id=1, source_target_pairs={{0,24},{8,0},{16,8},{24,16},{1,25},{9,1},{17,9},{25,17},{2,26},{10... | collective-permute-start | bytes 393224 | tf_op jit(solution)/shard_map/ppermute | solution.py:311
  97.0 11.0 %collective-permute-start.20 = (bf16[512,128]{1,0:T(8,128)(2,1)S(1)}, bf16[512,128]{1,0:T(8,128)(2,1)S(1)}, u32[]{:S(2)}, u32[]{:S(2)}) collective-permute-start(bf16[512,128]{1,0:T(8,128)(2,1)S(1)} %get-tuple-element.58), channel_id=1, source_target_pairs={{0,16},{8,24},{16,0},{24,8},{1,17},{9,25},{17,1},{25,9},{2,18},{10... | collective-permute-start | bytes 393224 | tf_op jit(solution)/shard_map/ppermute | solution.py:311
  (24 other events, 149.2 us)
where the time goes:
time: 115 us; the launch traced here: 114 us
  starting transfers between devices  56.5 us (49%)
  waiting for transfers between devices  26.3 us (23%)
  Pallas kernels  24 us (21%)
  local copies, waits for them, and re-layouts  6.27 us (5%)
    ppermute x36, starting transfers between devices, ring(): lax.ppermute(x, axis, [(j, (j + step) % count) for j in range(count)])  49.5 us
    ppermute x36, waiting for transfers between devices, ring(): lax.ppermute(x, axis, [(j, (j + step) % count) for j in range(count)])  15.8 us
    all_to_all x1, waiting for transfers between devices, step(): arrived = lax.all_to_all(dealt, ('z', 'y', 'x', 'c'), 0, 0, tiled=True)  10.5 us
    all_to_all x1, starting transfers between devices, step(): arrived = lax.all_to_all(dealt, ('z', 'y', 'x', 'c'), 0, 0, tiled=True)  6.97 us
    unnamed x22, local copies, waits for them, and re-layouts  6.27 us
    pallas_call x1, Pallas kernels, step(): make_own(0, False, True)(pay, stat, near[0], far[0], dq)  5.03 us
    pallas_call x1, Pallas kernels, step(): make_own(3, False, False)(pay, stat, near[3], far[3], dq)  4.05 us
    pallas_call x1, Pallas kernels, step(): make_own(1, False, False)(pay, stat, near[1], far[1], dq)  3.87 us
  transfers between devices with their start and end apart: 37, of which 8 were waited for; matrix products, arithmetic and copies ran while one was open for 0% of the time, Pallas kernels for 20%

commit v1 on v0

--- a/solution.py
+++ b/solution.py
@@ -339,15 +339,15 @@
         [pltpu.VMEM((128, 16, HD), F32)],
     )(lengths, arrived, *qo)
     mine, other, dq = {}, {}, None
-    mine[2], other[2], dq = make_own(2, True, False)(pay, stat, near[2], far[2])
+    mine[0], other[0], dq = make_own(0, True, False)(pay, stat, near[0], far[0])
+    mine[2], other[2], dq = make_own(2, False, False)(pay, stat, near[2], far[2], dq)
     trio = shape((3, 4, 2, B, HD), BF16)
     scratch = [pltpu.VMEM((16, 2 * B, HD), BF16)] * 2 + [pltpu.SMEM((16,), jnp.int32)]
     scratch += [pltpu.VMEM((2 * B, ROWS), BF16)] * 4
     sibling = call(sibling_kernel, (trio, trio, shape((4, HD, ROWS), F32)), 1, 10, scratch)
     dcur, dprev, dq = sibling(lengths, pay, stat, mark, dq, *cur, *prev)
     mine[3], other[3], dq = make_own(3, False, False)(pay, stat, near[3], far[3], dq)
-    mine[1], other[1], dq = make_own(1, False, False)(pay, stat, near[1], far[1], dq)
-    mine[0], other[0], *dq_sent = make_own(0, False, True)(pay, stat, near[0], far[0], dq)
+    mine[1], other[1], *dq_sent = make_own(1, False, True)(pay, stat, near[1], far[1], dq)
     terms = [mine[0], ring(other[0], "c", 1, 2)]
     for d in (2, 1, 3):
         both = mine[d].astype(F32) + ring(other[d], "c", 1, 2).astype(F32)

time: 115 us -> 116 us (level)
  waiting for transfers between devices: 26.3 us -> 33.7 us
  starting transfers between devices: 56.5 us -> 50.4 us
    ppermute x36, waiting for transfers between devices: 15.8 us -> 23.3 us  [ring(): lax.ppermute(x, axis, [(j, (j + step) % count) for j in range(count)])]
    ppermute x36, starting transfers between devices: 49.5 us -> 43.8 us  [ring(): lax.ppermute(x, axis, [(j, (j + step) % count) for j in range(count)])]
  transfers between devices with their start and end apart: 37 -> 37, of which waited for: 8 -> 11; matrix products, arithmetic and copies ran while one was open for 0% -> 0% of each run, Pallas kernels for 20% -> 20%
where the time goes in v1:
time: 116 us
  starting transfers between devices  50.4 us (43%)
  waiting for transfers between devices  33.7 us (29%)
  Pallas kernels  24.1 us (21%)
  local copies, waits for them, and re-layouts  6.27 us (5%)
    ppermute x36, starting transfers between devices, ring(): lax.ppermute(x, axis, [(j, (j + step) % count) for j in range(count)])  43.8 us
    ppermute x36, waiting for transfers between devices, ring(): lax.ppermute(x, axis, [(j, (j + step) % count) for j in range(count)])  23.3 us
    all_to_all x1, waiting for transfers between devices, step(): arrived = lax.all_to_all(dealt, ('z', 'y', 'x', 'c'), 0, 0, tiled=True)  10.5 us
    all_to_all x1, starting transfers between devices, step(): arrived = lax.all_to_all(dealt, ('z', 'y', 'x', 'c'), 0, 0, tiled=True)  6.67 us
    unnamed x22, local copies, waits for them, and re-layouts  6.27 us
    pallas_call x1, Pallas kernels, step(): mine[0], other[0], dq = make_own(0, True, False)(pay, stat, near[0], far[0])  4.65 us
    pallas_call x1, Pallas kernels, step(): make_own(1, False, True)(pay, stat, near[1], far[1], dq)  4.14 us
    pallas_call x1, Pallas kernels, step(): make_own(3, False, False)(pay, stat, near[3], far[3], dq)  3.86 us
  transfers between devices with their start and end apart: 37, of which 11 were waited for; matrix products, arithmetic and copies ran while one was open for 0% of the time, Pallas kernels for 20%

profile of v1, /device:TPU:0, one launch (start us, length us, event | category | flops | bytes accessed | tf_op | source)
XLA Modules:
  0.0 115.7 jit_solution(13501911447767618555)
XLA Ops:
  2.5 3.2 %collective-permute-start.5 = (bf16[2,128,128]{2,1,0:T(8,128)(2,1)S(1)}, bf16[2,128,128]{2,1,0:T(8,128)(2,1)S(1)}, u32[]{:S(2)}, u32[]{:S(2)}) collective-permute-start(bf16[2,128,128]{2,1,0:T(8,128)(2,1)S(1)} %get-tuple-element.50), channel_id=1, source_target_pairs={{0,24},{8,0},{16,8},{24,16},{1,25},{9,1},{17,9},{25,17},{2,26},{10... | collective-permute-start | bytes 196616 | tf_op jit(solution)/shard_map/ppermute | solution.py:311
  5.7 2.2 %collective-permute-start.4 = (bf16[2,128,128]{2,1,0:T(8,128)(2,1)S(1)}, bf16[2,128,128]{2,1,0:T(8,128)(2,1)S(1)}, u32[]{:S(2)}, u32[]{:S(2)}) collective-permute-start(bf16[2,128,128]{2,1,0:T(8,128)(2,1)S(1)} %get-tuple-element.49), channel_id=1, source_target_pairs={{0,16},{8,24},{16,0},{24,8},{1,17},{9,25},{17,1},{25,9},{2,18},{10... | collective-permute-start | bytes 196616 | tf_op jit(solution)/shard_map/ppermute | solution.py:311
  11.5 2.0 %collective-permute-start = (bf16[1040,128]{1,0:T(8,128)(2,1)S(1)}, bf16[1040,128]{1,0:T(8,128)(2,1)S(1)}, u32[]{:S(2)}, u32[]{:S(2)}) collective-permute-start(bf16[1040,128]{1,0:T(8,128)(2,1)S(1)} %get-tuple-element.42), channel_id=1, source_target_pairs={{0,8},{8,16},{16,24},{24,0},{1,9},{9,17},{17,25},{25,1},{2,10},{10... | collective-permute-start | bytes 798728 | tf_op jit(solution)/shard_map/ppermute | solution.py:311
  14.1 2.1 %collective-permute-start.2 = (bf16[1040,128]{1,0:T(8,128)(2,1)S(1)}, bf16[1040,128]{1,0:T(8,128)(2,1)S(1)}, u32[]{:S(2)}, u32[]{:S(2)}) collective-permute-start(bf16[1040,128]{1,0:T(8,128)(2,1)S(1)} %get-tuple-element.44), channel_id=1, source_target_pairs={{0,24},{8,0},{16,8},{24,16},{1,25},{9,1},{17,9},{25,17},{2,26},{10... | collective-permute-start | bytes 798728 | tf_op jit(solution)/shard_map/ppermute | solution.py:311
  16.4 3.1 %collective-permute-start.10 = (bf16[4,2,128,128]{3,2,1,0:T(8,128)(2,1)S(1)}, bf16[4,2,128,128]{3,2,1,0:T(8,128)(2,1)S(1)}, u32[]{:S(2)}, u32[]{:S(2)}) collective-permute-start(bf16[4,2,128,128]{3,2,1,0:T(8,128)(2,1)S(1)} %pad_maximum_fusion.km_ref), channel_id=1, source_target_pairs={{0,4},{2,6},{4,0},{6,2},{1,5},{3,7},{5,1},{7,3},{8,12},{10,14},{12... | collective-permute-start | bytes 786440 | tf_op jit(solution)/shard_map/ppermute | solution.py:311
  19.5 6.3 %collective-permute-done.refs_1_ = bf16[1040,128]{1,0:T(8,128)(2,1)S(1)} collective-permute-done((bf16[1040,128]{1,0:T(8,128)(2,1)S(1)}, bf16[1040,128]{1,0:T(8,128)(2,1)S(1)}, u32[]{:S(2)}, u32[]{:S(2)}) %collective-permute-start) | collective-permute-done | bytes 266272 | tf_op jit(solution)/shard_map/ppermute | solution.py:311
  25.8 1.9 %collective-permute-start.13 = (bf16[4,2,128,128]{3,2,1,0:T(8,128)(2,1)S(1)}, bf16[4,2,128,128]{3,2,1,0:T(8,128)(2,1)S(1)}, u32[]{:S(2)}, u32[]{:S(2)}) collective-permute-start(bf16[4,2,128,128]{3,2,1,0:T(8,128)(2,1)S(1)} %pad_maximum_fusion.km_ref), channel_id=1, source_target_pairs={{0,32},{32,64},{64,96},{96,0},{1,33},{33,65},{65,97},{97,1},{2,34}... | collective-permute-start | bytes 786440 | tf_op jit(solution)/shard_map/ppermute | solution.py:311
  27.7 3.6 %collective-permute-start.14 = (bf16[4,2,128,128]{3,2,1,0:T(8,128)(2,1)S(1)}, bf16[4,2,128,128]{3,2,1,0:T(8,128)(2,1)S(1)}, u32[]{:S(2)}, u32[]{:S(2)}) collective-permute-start(bf16[4,2,128,128]{3,2,1,0:T(8,128)(2,1)S(1)} %pad_maximum_fusion.km_ref), channel_id=1, source_target_pairs={{0,64},{32,96},{64,0},{96,32},{1,65},{33,97},{65,1},{97,33},{2,66}... | collective-permute-start | bytes 786440 | tf_op jit(solution)/shard_map/ppermute | solution.py:311
  32.3 2.8 %collective-permute-start.8 = (bf16[4,2,128,128]{3,2,1,0:T(8,128)(2,1)S(1)}, bf16[4,2,128,128]{3,2,1,0:T(8,128)(2,1)S(1)}, u32[]{:S(2)}, u32[]{:S(2)}) collective-permute-start(bf16[4,2,128,128]{3,2,1,0:T(8,128)(2,1)S(1)} %pad_maximum_fusion.km_ref), channel_id=1, source_target_pairs={{0,6},{2,0},{4,2},{6,4},{1,7},{3,1},{5,3},{7,5},{8,14},{10,8},{12,... | collective-permute-start | bytes 786440 | tf_op jit(solution)/shard_map/ppermute | solution.py:311
  36.5 6.7 %all-to-all-start = ((bf16[128,16,128]{2,1,0:T(8,128)(2,1)}), bf16[128,16,128]{2,1,0:T(8,128)(2,1)S(1)}, u32[]{:S(2)}, u32[]{:S(2)}) async-start(bf16[128,16,128]{2,1,0:T(8,128)(2,1)} %shard_map.103), calls=%async_computation | async-start | bytes 1048576 | tf_op jit(solution)/shard_map/all_to_all | solution.py:331
  46.8 10.5 %all-to-all-done.g_ref = bf16[128,16,128]{2,1,0:T(8,128)(2,1)S(1)} async-done(((bf16[128,16,128]{2,1,0:T(8,128)(2,1)}), bf16[128,16,128]{2,1,0:T(8,128)(2,1)S(1)}, u32[]{:S(2)}, u32[]{:S(2)}) %all-to-all-start) | async-done | bytes 524320 | tf_op jit(solution)/shard_map/all_to_all | solution.py:331
  57.2 2.0 %shard_map.105 = (bf16[4,1024,128]{2,1,0:T(8,128)(2,1)S(1)}, f32[4,2,512]{2,1,0:T(2,128)S(1)}, f32[4,8,128]{2,1,0:T(8,128)S(1)}) custom-call(s32[4]{0:T(128)S(1)} %copy-done.9, bf16[128,16,128]{2,1,0:T(8,128)(2,1)S(1)} %all-to-all-done.g_ref, bf16[1040,128]{1,0:T(8,128)(2,1)S(1)} %get-tuple-element.41.refs_0_, ...), custom_call_target="tpu_custom_call" | custom-call | tf_op jit(solution)/shard_map/pallas_call | solution.py:334
  59.2 4.6 %shard_map.107 = (bf16[4,2,128,128]{3,2,1,0:T(8,128)(2,1)S(1)}, bf16[4,2,128,128]{3,2,1,0:T(8,128)(2,1)S(1)}, f32[4,128,512]{2,1,0:T(8,128)S(1)}) custom-call(bf16[4,1024,128]{2,1,0:T(8,128)(2,1)S(1)} %get-tuple-element.45.p_ref, f32[4,2,512]{2,1,0:T(2,128)S(1)} %get-tuple-element.46.stat_ref, bf16[4,2,128,128]{3,2,1,0:T(8,128)(2,1)S(1)} %pad_maximum_fusion.km_ref, ...), custom_call_target="tpu_custom_call" | custom-call | tf_op jit(solution)/shard_map/pallas_call | solution.py:342
  63.9 2.9 %shard_map.108 = (bf16[4,2,128,128]{3,2,1,0:T(8,128)(2,1)S(1)}, bf16[4,2,128,128]{3,2,1,0:T(8,128)(2,1)S(1)}, f32[4,128,512]{2,1,0:T(8,128)S(1)}) custom-call(bf16[4,1024,128]{2,1,0:T(8,128)(2,1)S(1)} %get-tuple-element.45.p_ref, f32[4,2,512]{2,1,0:T(2,128)S(1)} %get-tuple-element.46.stat_ref, bf16[4,2,128,128]{3,2,1,0:T(8,128)(2,1)S(1)} %collective-permute-done.10.km_ref, ...), custom_call_target="tpu_custom_call" | custom-call | tf_op jit(solution)/shard_map/pallas_call | solution.py:343
  67.9 2.1 %shard_map.109 = (bf16[3,4,2,128,128]{4,3,2,1,0:T(8,128)(2,1)S(1)}, bf16[3,4,2,128,128]{4,3,2,1,0:T(8,128)(2,1)S(1)}, f32[4,128,512]{2,1,0:T(8,128)S(1)}) custom-call(s32[4]{0:T(128)S(1)} %copy-done.9, bf16[4,1024,128]{2,1,0:T(8,128)(2,1)S(1)} %get-tuple-element.45.p_ref, f32[4,2,512]{2,1,0:T(2,128)S(1)} %get-tuple-element.46.stat_ref, ...), custom_call_target="tpu_custom_call" | custom-call | tf_op jit(solution)/shard_map/pallas_call | solution.py:348
  70.0 3.9 %shard_map.110 = (bf16[4,2,128,128]{3,2,1,0:T(8,128)(2,1)S(1)}, bf16[4,2,128,128]{3,2,1,0:T(8,128)(2,1)S(1)}, f32[4,128,512]{2,1,0:T(8,128)S(1)}) custom-call(bf16[4,1024,128]{2,1,0:T(8,128)(2,1)S(1)} %get-tuple-element.45.p_ref, f32[4,2,512]{2,1,0:T(2,128)S(1)} %get-tuple-element.46.stat_ref, bf16[4,2,128,128]{3,2,1,0:T(8,128)(2,1)S(1)} %collective-permute-done.8.km_ref, ...), custom_call_target="tpu_custom_call" | custom-call | tf_op jit(solution)/shard_map/pallas_call | solution.py:349
  74.6 3.2 %collective-permute-start.29 = (bf16[3,4,2,128,128]{4,3,2,1,0:T(8,128)(2,1)S(1)}, bf16[3,4,2,128,128]{4,3,2,1,0:T(8,128)(2,1)S(1)}, u32[]{:S(2)}, u32[]{:S(2)}) collective-permute-start(bf16[3,4,2,128,128]{4,3,2,1,0:T(8,128)(2,1)S(1)} %get-tuple-element.69), channel_id=1, source_target_pairs={{0,7},{1,0},{2,1},{3,2},{4,3},{5,4},{6,5},{7,6},{8,15},{9,8},{10,9... | collective-permute-start | bytes 2359304 | tf_op jit(solution)/shard_map/ppermute | solution.py:311
  77.8 4.1 %shard_map.111 = (bf16[4,2,128,128]{3,2,1,0:T(8,128)(2,1)S(1)}, bf16[4,2,128,128]{3,2,1,0:T(8,128)(2,1)S(1)}, bf16[512,128]{1,0:T(8,128)(2,1)S(1)}, bf16[512,128...) custom-call(bf16[4,1024,128]{2,1,0:T(8,128)(2,1)S(1)} %get-tuple-element.45.p_ref, ...), custom_call_target="tpu_custom_call" | custom-call | tf_op jit(solution)/shard_map/pallas_call | solution.py:350
  83.6 2.5 %collective-permute-start.26 = (bf16[4,2,128,128]{3,2,1,0:T(8,128)(2,1)S(1)}, bf16[4,2,128,128]{3,2,1,0:T(8,128)(2,1)S(1)}, u32[]{:S(2)}, u32[]{:S(2)}) collective-permute-start(bf16[4,2,128,128]{3,2,1,0:T(8,128)(2,1)S(1)} %add_convert_fusion.1), channel_id=1, source_target_pairs={{0,6},{2,0},{4,2},{6,4},{1,7},{3,1},{5,3},{7,5},{8,14},{10,8},{12,... | collective-permute-start | bytes 786440 | tf_op jit(solution)/shard_map/ppermute | solution.py:311
  88.4 4.2 %collective-permute-start.30 = (bf16[4,2,128,128]{3,2,1,0:T(8,128)(2,1)S(1)}, bf16[4,2,128,128]{3,2,1,0:T(8,128)(2,1)S(1)}, u32[]{:S(2)}, u32[]{:S(2)}) collective-permute-start(bf16[4,2,128,128]{3,2,1,0:T(8,128)(2,1)S(1)} %get-tuple-element.70), channel_id=1, source_target_pairs={{0,96},{32,0},{64,32},{96,64},{1,97},{33,1},{65,33},{97,65},{2,98}... | collective-permute-start | bytes 786440 | tf_op jit(solution)/shard_map/ppermute | solution.py:311
  93.9 4.3 %collective-permute-done.28.refs_4_ = bf16[4,2,128,128]{3,2,1,0:T(8,128)(2,1)S(1)} collective-permute-done((bf16[4,2,128,128]{3,2,1,0:T(8,128)(2,1)S(1)}, bf16[4,2,128,128]{3,2,1,0:T(8,128)(2,1)S(1)}, u32[]{:S(2)}, u32[]{:S(2)}) %collective-permute-start.28) | collective-permute-done | bytes 262176 | tf_op jit(solution)/shard_map/ppermute | solution.py:311
  102.4 4.3 %collective-permute-done.32.refs_7_ = bf16[4,2,128,128]{3,2,1,0:T(8,128)(2,1)S(1)} collective-permute-done((bf16[4,2,128,128]{3,2,1,0:T(8,128)(2,1)S(1)}, bf16[4,2,128,128]{3,2,1,0:T(8,128)(2,1)S(1)}, u32[]{:S(2)}, u32[]{:S(2)}) %collective-permute-start.32) | collective-permute-done | bytes 262176 | tf_op jit(solution)/shard_map/ppermute | solution.py:311
  107.5 1.9 %collective-permute-start.34 = (bf16[2,128,128]{2,1,0:T(8,128)(2,1)S(1)}, bf16[2,128,128]{2,1,0:T(8,128)(2,1)S(1)}, u32[]{:S(2)}, u32[]{:S(2)}) collective-permute-start(bf16[2,128,128]{2,1,0:T(8,128)(2,1)S(1)} %get-tuple-element.75), channel_id=1, source_target_pairs={{0,16},{8,24},{16,0},{24,8},{1,17},{9,25},{17,1},{25,9},{2,18},{10... | collective-permute-start | bytes 196616 | tf_op jit(solution)/shard_map/ppermute | solution.py:311
  111.3 2.0 %collective-permute-done.34.d2 = bf16[2,128,128]{2,1,0:T(8,128)(2,1)S(1)} collective-permute-done((bf16[2,128,128]{2,1,0:T(8,128)(2,1)S(1)}, bf16[2,128,128]{2,1,0:T(8,128)(2,1)S(1)}, u32[]{:S(2)}, u32[]{:S(2)}) %collective-permute-start.34) | collective-permute-done | bytes 65568 | tf_op jit(solution)/shard_map/ppermute | solution.py:311
  (89 shorter events, 28.4 us)
Async XLA Ops:
  2.5 11.6 %collective-permute-start.5 = (bf16[2,128,128]{2,1,0:T(8,128)(2,1)S(1)}, bf16[2,128,128]{2,1,0:T(8,128)(2,1)S(1)}, u32[]{:S(2)}, u32[]{:S(2)}) collective-permute-start(bf16[2,128,128]{2,1,0:T(8,128)(2,1)S(1)} %get-tuple-element.50), channel_id=1, source_target_pairs={{0,24},{8,0},{16,8},{24,16},{1,25},{9,1},{17,9},{25,17},{2,26},{10... | collective-permute-start | bytes 196616 | tf_op jit(solution)/shard_map/ppermute | solution.py:311
  5.7 10.5 %collective-permute-start.3 = (bf16[2,128,128]{2,1,0:T(8,128)(2,1)S(1)}, bf16[2,128,128]{2,1,0:T(8,128)(2,1)S(1)}, u32[]{:S(2)}, u32[]{:S(2)}) collective-permute-start(bf16[2,128,128]{2,1,0:T(8,128)(2,1)S(1)} %get-tuple-element.48), channel_id=1, source_target_pairs={{0,8},{8,16},{16,24},{24,0},{1,9},{9,17},{17,25},{25,1},{2,10},{10... | collective-permute-start | bytes 196616 | tf_op jit(solution)/shard_map/ppermute | solution.py:311
  11.5 14.3 %collective-permute-start = (bf16[1040,128]{1,0:T(8,128)(2,1)S(1)}, bf16[1040,128]{1,0:T(8,128)(2,1)S(1)}, u32[]{:S(2)}, u32[]{:S(2)}) collective-permute-start(bf16[1040,128]{1,0:T(8,128)(2,1)S(1)} %get-tuple-element.42), channel_id=1, source_target_pairs={{0,8},{8,16},{16,24},{24,0},{1,9},{9,17},{17,25},{25,1},{2,10},{10... | collective-permute-start | bytes 798728 | tf_op jit(solution)/shard_map/ppermute | solution.py:311
  13.5 14.2 %collective-permute-start.1 = (bf16[1040,128]{1,0:T(8,128)(2,1)S(1)}, bf16[1040,128]{1,0:T(8,128)(2,1)S(1)}, u32[]{:S(2)}, u32[]{:S(2)}) collective-permute-start(bf16[1040,128]{1,0:T(8,128)(2,1)S(1)} %get-tuple-element.43), channel_id=1, source_target_pairs={{0,16},{8,24},{16,0},{24,8},{1,17},{9,25},{17,1},{25,9},{2,18},{10... | collective-permute-start | bytes 798728 | tf_op jit(solution)/shard_map/ppermute | solution.py:311
  14.1 17.2 %collective-permute-start.2 = (bf16[1040,128]{1,0:T(8,128)(2,1)S(1)}, bf16[1040,128]{1,0:T(8,128)(2,1)S(1)}, u32[]{:S(2)}, u32[]{:S(2)}) collective-permute-start(bf16[1040,128]{1,0:T(8,128)(2,1)S(1)} %get-tuple-element.44), channel_id=1, source_target_pairs={{0,24},{8,0},{16,8},{24,16},{1,25},{9,1},{17,9},{25,17},{2,26},{10... | collective-permute-start | bytes 798728 | tf_op jit(solution)/shard_map/ppermute | solution.py:311
  16.3 16.0 %collective-permute-start.12 = (bf16[4,2,128,128]{3,2,1,0:T(8,128)(2,1)S(1)}, bf16[4,2,128,128]{3,2,1,0:T(8,128)(2,1)S(1)}, u32[]{:S(2)}, u32[]{:S(2)}) collective-permute-start(bf16[4,2,128,128]{3,2,1,0:T(8,128)(2,1)S(1)} %pad_maximum_fusion.km_ref), channel_id=1, source_target_pairs={{0,1},{1,0},{2,3},{3,2},{4,5},{5,4},{6,7},{7,6},{8,9},{9,8},{10,11... | collective-permute-start | bytes 786440 | tf_op jit(solution)/shard_map/ppermute | solution.py:311
  16.4 18.7 %collective-permute-start.10 = (bf16[4,2,128,128]{3,2,1,0:T(8,128)(2,1)S(1)}, bf16[4,2,128,128]{3,2,1,0:T(8,128)(2,1)S(1)}, u32[]{:S(2)}, u32[]{:S(2)}) collective-permute-start(bf16[4,2,128,128]{3,2,1,0:T(8,128)(2,1)S(1)} %pad_maximum_fusion.km_ref), channel_id=1, source_target_pairs={{0,4},{2,6},{4,0},{6,2},{1,5},{3,7},{5,1},{7,3},{8,12},{10,14},{12... | collective-permute-start | bytes 786440 | tf_op jit(solution)/shard_map/ppermute | solution.py:311
  25.8 17.4 %collective-permute-start.13 = (bf16[4,2,128,128]{3,2,1,0:T(8,128)(2,1)S(1)}, bf16[4,2,128,128]{3,2,1,0:T(8,128)(2,1)S(1)}, u32[]{:S(2)}, u32[]{:S(2)}) collective-permute-start(bf16[4,2,128,128]{3,2,1,0:T(8,128)(2,1)S(1)} %pad_maximum_fusion.km_ref), channel_id=1, source_target_pairs={{0,32},{32,64},{64,96},{96,0},{1,33},{33,65},{65,97},{97,1},{2,34}... | collective-permute-start | bytes 786440 | tf_op jit(solution)/shard_map/ppermute | solution.py:311
  27.7 15.6 %collective-permute-start.14 = (bf16[4,2,128,128]{3,2,1,0:T(8,128)(2,1)S(1)}, bf16[4,2,128,128]{3,2,1,0:T(8,128)(2,1)S(1)}, u32[]{:S(2)}, u32[]{:S(2)}) collective-permute-start(bf16[4,2,128,128]{3,2,1,0:T(8,128)(2,1)S(1)} %pad_maximum_fusion.km_ref), channel_id=1, source_target_pairs={{0,64},{32,96},{64,0},{96,32},{1,65},{33,97},{65,1},{97,33},{2,66}... | collective-permute-start | bytes 786440 | tf_op jit(solution)/shard_map/ppermute | solution.py:311
  31.3 12.5 %collective-permute-start.15 = (bf16[4,2,128,128]{3,2,1,0:T(8,128)(2,1)S(1)}, bf16[4,2,128,128]{3,2,1,0:T(8,128)(2,1)}, u32[]{:S(2)}, u32[]{:S(2)}) collective-permute-start(bf16[4,2,128,128]{3,2,1,0:T(8,128)(2,1)S(1)} %pad_maximum_fusion.km_ref), channel_id=1, source_target_pairs={{0,96},{32,0},{64,32},{96,64},{1,97},{33,1},{65,33},{97,65},{2,98}... | collective-permute-start | bytes 786440 | tf_op jit(solution)/shard_map/ppermute | solution.py:311
  32.3 12.2 %collective-permute-start.8 = (bf16[4,2,128,128]{3,2,1,0:T(8,128)(2,1)S(1)}, bf16[4,2,128,128]{3,2,1,0:T(8,128)(2,1)S(1)}, u32[]{:S(2)}, u32[]{:S(2)}) collective-permute-start(bf16[4,2,128,128]{3,2,1,0:T(8,128)(2,1)S(1)} %pad_maximum_fusion.km_ref), channel_id=1, source_target_pairs={{0,6},{2,0},{4,2},{6,4},{1,7},{3,1},{5,3},{7,5},{8,14},{10,8},{12,... | collective-permute-start | bytes 786440 | tf_op jit(solution)/shard_map/ppermute | solution.py:311
  36.5 20.7 %all-to-all-start = ((bf16[128,16,128]{2,1,0:T(8,128)(2,1)}), bf16[128,16,128]{2,1,0:T(8,128)(2,1)S(1)}, u32[]{:S(2)}, u32[]{:S(2)}) async-start(bf16[128,16,128]{2,1,0:T(8,128)(2,1)} %shard_map.103), calls=%async_computation | async-start | bytes 1048576 | tf_op jit(solution)/shard_map/all_to_all | solution.py:331
  43.3 24.6 %collective-permute-start.16 = (bf16[4,2,128,128]{3,2,1,0:T(8,128)(2,1)S(1)}, bf16[4,2,128,128]{3,2,1,0:T(8,128)(2,1)}, u32[]{:S(2)}, u32[]{:S(2)}) collective-permute-start(bf16[4,2,128,128]{3,2,1,0:T(8,128)(2,1)S(1)} %collective-permute-done.13.refs_0_), channel_id=1, source_target_pairs={{0,1},{1,2},{2,3},{3,4},{4,5},{5,6},{6,7},{7,0},{8,9},{9,10},{10,1... | collective-permute-start | bytes 786440 | tf_op jit(solution)/shard_map/ppermute | solution.py:311
  43.8 24.1 %collective-permute-start.17 = (bf16[4,2,128,128]{3,2,1,0:T(8,128)(2,1)S(1)}, bf16[4,2,128,128]{3,2,1,0:T(8,128)(2,1)}, u32[]{:S(2)}, u32[]{:S(2)}) collective-permute-start(bf16[4,2,128,128]{3,2,1,0:T(8,128)(2,1)S(1)} %collective-permute-done.14.refs_1_), channel_id=1, source_target_pairs={{0,1},{1,2},{2,3},{3,4},{4,5},{5,6},{6,7},{7,0},{8,9},{9,10},{10,1... | collective-permute-start | bytes 786440 | tf_op jit(solution)/shard_map/ppermute | solution.py:311
  44.5 23.4 %collective-permute-start.18 = (bf16[4,2,128,128]{3,2,1,0:T(8,128)(2,1)}, bf16[4,2,128,128]{3,2,1,0:T(8,128)(2,1)}, u32[]{:S(2)}, u32[]{:S(2)}) collective-permute-start(bf16[4,2,128,128]{3,2,1,0:T(8,128)(2,1)} %collective-permute-done.15.refs_2_), channel_id=1, source_target_pairs={{0,1},{1,2},{2,3},{3,4},{4,5},{5,6},{6,7},{7,0},{8,9},{9,10},{10,1... | collective-permute-start | bytes 786440 | tf_op jit(solution)/shard_map/ppermute | solution.py:311
  44.9 25.1 %collective-permute-start.9 = (bf16[4,2,128,128]{3,2,1,0:T(8,128)(2,1)S(1)}, bf16[4,2,128,128]{3,2,1,0:T(8,128)(2,1)}, u32[]{:S(2)}, u32[]{:S(2)}) collective-permute-start(bf16[4,2,128,128]{3,2,1,0:T(8,128)(2,1)S(1)} %collective-permute-done.8.km_ref), channel_id=1, source_target_pairs={{0,1},{1,0},{2,3},{3,2},{4,5},{5,4},{6,7},{7,6},{8,9},{9,8},{10,11... | collective-permute-start | bytes 786440 | tf_op jit(solution)/shard_map/ppermute | solution.py:311
  46.7 31.0 %collective-permute-start.7 = (bf16[4,2,128,128]{3,2,1,0:T(8,128)(2,1)S(1)}, bf16[4,2,128,128]{3,2,1,0:T(8,128)(2,1)}, u32[]{:S(2)}, u32[]{:S(2)}) collective-permute-start(bf16[4,2,128,128]{3,2,1,0:T(8,128)(2,1)S(1)} %collective-permute-done.6.km_ref), channel_id=1, source_target_pairs={{0,1},{1,0},{2,3},{3,2},{4,5},{5,4},{6,7},{7,6},{8,9},{9,8},{10,11... | collective-permute-start | bytes 786440 | tf_op jit(solution)/shard_map/ppermute | solution.py:311
  74.6 13.6 %collective-permute-start.29 = (bf16[3,4,2,128,128]{4,3,2,1,0:T(8,128)(2,1)S(1)}, bf16[3,4,2,128,128]{4,3,2,1,0:T(8,128)(2,1)S(1)}, u32[]{:S(2)}, u32[]{:S(2)}) collective-permute-start(bf16[3,4,2,128,128]{4,3,2,1,0:T(8,128)(2,1)S(1)} %get-tuple-element.69), channel_id=1, source_target_pairs={{0,7},{1,0},{2,1},{3,2},{4,3},{5,4},{6,5},{7,6},{8,15},{9,8},{10,9... | collective-permute-start | bytes 2359304 | tf_op jit(solution)/shard_map/ppermute | solution.py:311
  82.0 10.6 %collective-permute-start.22 = (bf16[4,2,128,128]{3,2,1,0:T(8,128)(2,1)S(1)}, bf16[4,2,128,128]{3,2,1,0:T(8,128)(2,1)S(1)}, u32[]{:S(2)}, u32[]{:S(2)}) collective-permute-start(bf16[4,2,128,128]{3,2,1,0:T(8,128)(2,1)S(1)} %get-tuple-element.61), channel_id=1, source_target_pairs={{0,1},{1,0},{2,3},{3,2},{4,5},{5,4},{6,7},{7,6},{8,9},{9,8},{10,11... | collective-permute-start | bytes 786440 | tf_op jit(solution)/shard_map/ppermute | solution.py:311
  82.7 15.5 %collective-permute-start.28 = (bf16[4,2,128,128]{3,2,1,0:T(8,128)(2,1)S(1)}, bf16[4,2,128,128]{3,2,1,0:T(8,128)(2,1)S(1)}, u32[]{:S(2)}, u32[]{:S(2)}) collective-permute-start(bf16[4,2,128,128]{3,2,1,0:T(8,128)(2,1)S(1)} %add_convert_fusion), channel_id=1, source_target_pairs={{0,2},{2,4},{4,6},{6,0},{1,3},{3,5},{5,7},{7,1},{8,10},{10,12},{12... | collective-permute-start | bytes 786440 | tf_op jit(solution)/shard_map/ppermute | solution.py:311
  83.6 14.9 %collective-permute-start.26 = (bf16[4,2,128,128]{3,2,1,0:T(8,128)(2,1)S(1)}, bf16[4,2,128,128]{3,2,1,0:T(8,128)(2,1)S(1)}, u32[]{:S(2)}, u32[]{:S(2)}) collective-permute-start(bf16[4,2,128,128]{3,2,1,0:T(8,128)(2,1)S(1)} %add_convert_fusion.1), channel_id=1, source_target_pairs={{0,6},{2,0},{4,2},{6,4},{1,7},{3,1},{5,3},{7,5},{8,14},{10,8},{12,... | collective-permute-start | bytes 786440 | tf_op jit(solution)/shard_map/ppermute | solution.py:311
  86.2 13.1 %collective-permute-start.24 = (bf16[4,2,128,128]{3,2,1,0:T(8,128)(2,1)S(1)}, bf16[4,2,128,128]{3,2,1,0:T(8,128)(2,1)S(1)}, u32[]{:S(2)}, u32[]{:S(2)}) collective-permute-start(bf16[4,2,128,128]{3,2,1,0:T(8,128)(2,1)S(1)} %add_convert_fusion.2), channel_id=1, source_target_pairs={{0,4},{2,6},{4,0},{6,2},{1,5},{3,7},{5,1},{7,3},{8,12},{10,14},{12... | collective-permute-start | bytes 786440 | tf_op jit(solution)/shard_map/ppermute | solution.py:311
  88.4 13.6 %collective-permute-start.30 = (bf16[4,2,128,128]{3,2,1,0:T(8,128)(2,1)S(1)}, bf16[4,2,128,128]{3,2,1,0:T(8,128)(2,1)S(1)}, u32[]{:S(2)}, u32[]{:S(2)}) collective-permute-start(bf16[4,2,128,128]{3,2,1,0:T(8,128)(2,1)S(1)} %get-tuple-element.70), channel_id=1, source_target_pairs={{0,96},{32,0},{64,32},{96,64},{1,97},{33,1},{65,33},{97,65},{2,98}... | collective-permute-start | bytes 786440 | tf_op jit(solution)/shard_map/ppermute | solution.py:311
  98.5 10.9 %collective-permute-start.19 = (bf16[512,128]{1,0:T(8,128)(2,1)S(1)}, bf16[512,128]{1,0:T(8,128)(2,1)S(1)}, u32[]{:S(2)}, u32[]{:S(2)}) collective-permute-start(bf16[512,128]{1,0:T(8,128)(2,1)S(1)} %get-tuple-element.57), channel_id=1, source_target_pairs={{0,24},{8,0},{16,8},{24,16},{1,25},{9,1},{17,9},{25,17},{2,26},{10... | collective-permute-start | bytes 393224 | tf_op jit(solution)/shard_map/ppermute | solution.py:311
  (24 other events, 142.7 us)

commit v2 on v1

--- a/solution.py
+++ b/solution.py
@@ -140,7 +140,7 @@
         y = lax.axis_index("y")
         if first:
             acc_ref[...] = jnp.zeros_like(acc_ref)
-        else:
+        elif last:
             acc_ref[...] = dq_in[...]
         dk_ref[...] = jnp.zeros_like(dk_ref)
         dv_ref[...] = jnp.zeros_like(dv_ref)
@@ -205,7 +205,8 @@
     ] + [pltpu.VMEM((2 * B, ROWS), BF16)] * 4
     if last:
         scratch.append(pltpu.VMEM((4, HD, ROWS), F32))
-    return call(kernel, (kv, kv, *dq), 0, 4 if first else 5, scratch)
+    aliases = None if first or last else {4: 2}
+    return call(kernel, (kv, kv, *dq), 0, 4 if first else 5, scratch, aliases)
 
 
 def sibling_kernel(len_ref, p_ref, stat_ref, mark_ref, dq_in, *refs):
@@ -215,7 +216,7 @@
     y = lax.axis_index("y")
     shard = 2 * lax.axis_index("x") + lax.axis_index("c")
     length = len_ref[thinker]
-    acc_ref[...] = dq_in[...]
+    del dq_in
     dcur[...] = jnp.zeros_like(dcur)
     dprev[...] = jnp.zeros_like(dprev)
     step = (shard == 0).astype(jnp.int32)
@@ -323,7 +324,8 @@
         sibling_mask.reshape(3), queries[0], forward_out[0], logsumexp.reshape(4, GROUP, B)
     )
     qo = [qo_sent[0]] + [ring(qo_sent[d], "y", d, 4) for d in dists]
-    near = [kv_own] + [ring(kv_own, "x", d, 4) for d in dists]
+    near = {0: kv_own, 1: ring(kv_own, "x", 1, 4), 3: ring(kv_own, "x", -1, 4)}
+    near[2] = ring(near[3], "x", -1, 4)
     cur = [ring(kv_own, "z", d, 4) for d in dists]
     dealt = call(deal, shape((128, 16, HD), BF16), 0, 1, [pltpu.VMEM((128, 16, HD), F32)])(
         upstream.reshape(128, 2048)
@@ -344,20 +346,22 @@
     trio = shape((3, 4, 2, B, HD), BF16)
     scratch = [pltpu.VMEM((16, 2 * B, HD), BF16)] * 2 + [pltpu.SMEM((16,), jnp.int32)]
     scratch += [pltpu.VMEM((2 * B, ROWS), BF16)] * 4
-    sibling = call(sibling_kernel, (trio, trio, shape((4, HD, ROWS), F32)), 1, 10, scratch)
+    sibling = call(sibling_kernel, (trio, trio, shape((4, HD, ROWS), F32)), 1, 10, scratch, {4: 2})
     dcur, dprev, dq = sibling(lengths, pay, stat, mark, dq, *cur, *prev)
     mine[3], other[3], dq = make_own(3, False, False)(pay, stat, near[3], far[3], dq)
     mine[1], other[1], *dq_sent = make_own(1, False, True)(pay, stat, near[1], far[1], dq)
     terms = [mine[0], ring(other[0], "c", 1, 2)]
-    for d in (2, 1, 3):
-        both = mine[d].astype(F32) + ring(other[d], "c", 1, 2).astype(F32)
-        terms.append(ring(both.astype(BF16), "x", -d, 4))
+    both = {d: mine[d].astype(F32) + ring(other[d], "c", 1, 2).astype(F32) for d in dists}
+    passing = ring(both[2].astype(BF16), "x", 1, 4)
+    joined = (both[3] + passing.astype(F32)).astype(BF16)
+    terms.append(ring(joined, "x", 1, 4))
+    terms.append(ring(both[1].astype(BF16), "x", -1, 4))
     late = ring(dprev, core, -1, 8)
     merged = call(merge, (kv,) * 3, 0, 2)(dcur, late)
     terms += [ring(merged[d - 1], "z", -d, 4) for d in dists]
     dq_got = [dq_sent[0]] + [ring(dq_sent[d], "y", -d, 4) for d in dists]
     q_grad = call(finish_q, (shape((B, 2048), BF16),), 0, 4)(*dq_got)[0]
-    kv_out = call(gather_terms, (piece,) * 4, 0, 8)(*terms)
+    kv_out = call(gather_terms, (piece,) * 4, 0, 7)(*terms)
     kv_got = [kv_out[0]] + [ring(kv_out[d], "y", -d, 4) for d in dists]
     k_grad, v_grad = call(finish_kv, (row, row), 0, 4)(*kv_got)
     return q_grad[None], k_grad[None], v_grad[None]

time: 116 us -> 124 us (1.069)
  starting transfers between devices: 50.4 us -> 58.6 us
  waiting for transfers between devices: 33.7 us -> 35.7 us
  local copies, waits for them, and re-layouts: 6.27 us -> 4.55 us
    ppermute x36, waiting for transfers between devices: 23.3 us -> 35.7 us  [ring(): lax.ppermute(x, axis, [(j, (j + step) % count) for j in range(count)])]
    all_to_all x1, waiting for transfers between devices: 10.5 us -> 0.01 us  [step(): arrived = lax.all_to_all(dealt, ('z', 'y', 'x', 'c'), 0, 0, tiled=True)]
    ppermute x36, starting transfers between devices: 43.8 us -> 50.7 us  [ring(): lax.ppermute(x, axis, [(j, (j + step) % count) for j in range(count)])]
    unnamed x22 -> x16, local copies, waits for them, and re-layouts: 6.27 us -> 4.55 us
    all_to_all x1, starting transfers between devices: 6.67 us -> 7.97 us  [step(): arrived = lax.all_to_all(dealt, ('z', 'y', 'x', 'c'), 0, 0, tiled=True)]
  transfers between devices with their start and end apart: 37 -> 37, of which waited for: 11 -> 10; matrix products, arithmetic and copies ran while one was open for 0% -> 0% of each run, Pallas kernels for 20% -> 18%
where the time goes in v2:
time: 124 us; the launch traced here: 123 us
  starting transfers between devices  58.6 us (47%)
  waiting for transfers between devices  35.7 us (29%)
  Pallas kernels  23.3 us (19%)
  local copies, waits for them, and re-layouts  4.55 us (4%)
    ppermute x36, starting transfers between devices, ring(): lax.ppermute(x, axis, [(j, (j + step) % count) for j in range(count)])  50.7 us
    ppermute x36, waiting for transfers between devices, ring(): lax.ppermute(x, axis, [(j, (j + step) % count) for j in range(count)])  35.7 us
    all_to_all x1, starting transfers between devices, step(): arrived = lax.all_to_all(dealt, ('z', 'y', 'x', 'c'), 0, 0, tiled=True)  7.97 us
    pallas_call x1, Pallas kernels, step(): mine[0], other[0], dq = make_own(0, True, False)(pay, stat, near[0], far[0])  4.65 us
    unnamed x16, local copies, waits for them, and re-layouts  4.55 us
    pallas_call x1, Pallas kernels, step(): make_own(2, False, False)(pay, stat, near[2], far[2], dq)  3.75 us
    pallas_call x1, Pallas kernels, step(): make_own(1, False, True)(pay, stat, near[1], far[1], dq)  3.18 us
    pallas_call x1, Pallas kernels, step(): make_own(3, False, False)(pay, stat, near[3], far[3], dq)  2.8 us
  transfers between devices with their start and end apart: 37, of which 10 were waited for; matrix products, arithmetic and copies ran while one was open for 0% of the time, Pallas kernels for 18%

profile of v2, /device:TPU:0, one launch (start us, length us, event | category | flops | bytes accessed | tf_op | source)
XLA Modules:
  0.0 123.3 jit_solution(8977642109944691685)
XLA Ops:
  2.5 3.2 %collective-permute-start.5 = (bf16[2,128,128]{2,1,0:T(8,128)(2,1)S(1)}, bf16[2,128,128]{2,1,0:T(8,128)(2,1)S(1)}, u32[]{:S(2)}, u32[]{:S(2)}) collective-permute-start(bf16[2,128,128]{2,1,0:T(8,128)(2,1)S(1)} %get-tuple-element.50), channel_id=1, source_target_pairs={{0,24},{8,0},{16,8},{24,16},{1,25},{9,1},{17,9},{25,17},{2,26},{10... | collective-permute-start | bytes 196616 | tf_op jit(solution)/shard_map/ppermute | solution.py:312
  5.7 2.2 %collective-permute-start.4 = (bf16[2,128,128]{2,1,0:T(8,128)(2,1)S(1)}, bf16[2,128,128]{2,1,0:T(8,128)(2,1)S(1)}, u32[]{:S(2)}, u32[]{:S(2)}) collective-permute-start(bf16[2,128,128]{2,1,0:T(8,128)(2,1)S(1)} %get-tuple-element.49), channel_id=1, source_target_pairs={{0,16},{8,24},{16,0},{24,8},{1,17},{9,25},{17,1},{25,9},{2,18},{10... | collective-permute-start | bytes 196616 | tf_op jit(solution)/shard_map/ppermute | solution.py:312
  14.2 2.8 %collective-permute-start.8 = (bf16[4,2,128,128]{3,2,1,0:T(8,128)(2,1)S(1)}, bf16[4,2,128,128]{3,2,1,0:T(8,128)(2,1)S(1)}, u32[]{:S(2)}, u32[]{:S(2)}) collective-permute-start(bf16[4,2,128,128]{3,2,1,0:T(8,128)(2,1)S(1)} %pad_maximum_fusion.km_ref), channel_id=1, source_target_pairs={{0,6},{2,0},{4,2},{6,4},{1,7},{3,1},{5,3},{7,5},{8,14},{10,8},{12,... | collective-permute-start | bytes 786440 | tf_op jit(solution)/shard_map/ppermute | solution.py:312
  17.7 2.1 %collective-permute-start.2 = (bf16[1040,128]{1,0:T(8,128)(2,1)}, bf16[1040,128]{1,0:T(8,128)(2,1)S(1)}, u32[]{:S(2)}, u32[]{:S(2)}) collective-permute-start(bf16[1040,128]{1,0:T(8,128)(2,1)} %get-tuple-element.44), channel_id=1, source_target_pairs={{0,24},{8,0},{16,8},{24,16},{1,25},{9,1},{17,9},{25,17},{2,26},{10... | collective-permute-start | bytes 798728 | tf_op jit(solution)/shard_map/ppermute | solution.py:312
  21.5 3.7 %collective-permute-start.10 = (bf16[4,2,128,128]{3,2,1,0:T(8,128)(2,1)S(1)}, bf16[4,2,128,128]{3,2,1,0:T(8,128)(2,1)S(1)}, u32[]{:S(2)}, u32[]{:S(2)}) collective-permute-start(bf16[4,2,128,128]{3,2,1,0:T(8,128)(2,1)S(1)} %collective-permute-done.8.km_ref), channel_id=1, source_target_pairs={{0,6},{2,0},{4,2},{6,4},{1,7},{3,1},{5,3},{7,5},{8,14},{10,8},{12,... | collective-permute-start | bytes 786440 | tf_op jit(solution)/shard_map/ppermute | solution.py:312
  26.5 1.9 %collective-permute-start.13 = (bf16[4,2,128,128]{3,2,1,0:T(8,128)(2,1)S(1)}, bf16[4,2,128,128]{3,2,1,0:T(8,128)(2,1)S(1)}, u32[]{:S(2)}, u32[]{:S(2)}) collective-permute-start(bf16[4,2,128,128]{3,2,1,0:T(8,128)(2,1)S(1)} %pad_maximum_fusion.km_ref), channel_id=1, source_target_pairs={{0,32},{32,64},{64,96},{96,0},{1,33},{33,65},{65,97},{97,1},{2,34}... | collective-permute-start | bytes 786440 | tf_op jit(solution)/shard_map/ppermute | solution.py:312
  29.8 8.0 %all-to-all-start = ((bf16[128,16,128]{2,1,0:T(8,128)(2,1)}), bf16[128,16,128]{2,1,0:T(8,128)(2,1)S(1)}, u32[]{:S(2)}, u32[]{:S(2)}) async-start(bf16[128,16,128]{2,1,0:T(8,128)(2,1)} %shard_map.103), calls=%async_computation | async-start | bytes 1048576 | tf_op jit(solution)/shard_map/all_to_all | solution.py:333
  37.8 2.9 %collective-permute-start.14 = (bf16[4,2,128,128]{3,2,1,0:T(8,128)(2,1)S(1)}, bf16[4,2,128,128]{3,2,1,0:T(8,128)(2,1)S(1)}, u32[]{:S(2)}, u32[]{:S(2)}) collective-permute-start(bf16[4,2,128,128]{3,2,1,0:T(8,128)(2,1)S(1)} %pad_maximum_fusion.km_ref), channel_id=1, source_target_pairs={{0,64},{32,96},{64,0},{96,32},{1,65},{33,97},{65,1},{97,33},{2,66}... | collective-permute-start | bytes 786440 | tf_op jit(solution)/shard_map/ppermute | solution.py:312
  43.7 9.0 %collective-permute-done.14.refs_1_ = bf16[4,2,128,128]{3,2,1,0:T(8,128)(2,1)S(1)} collective-permute-done((bf16[4,2,128,128]{3,2,1,0:T(8,128)(2,1)S(1)}, bf16[4,2,128,128]{3,2,1,0:T(8,128)(2,1)S(1)}, u32[]{:S(2)}, u32[]{:S(2)}) %collective-permute-start.14) | collective-permute-done | bytes 262176 | tf_op jit(solution)/shard_map/ppermute | solution.py:312
  52.7 5.2 %collective-permute-done.15.refs_2_ = bf16[4,2,128,128]{3,2,1,0:T(8,128)(2,1)} collective-permute-done((bf16[4,2,128,128]{3,2,1,0:T(8,128)(2,1)S(1)}, bf16[4,2,128,128]{3,2,1,0:T(8,128)(2,1)}, u32[]{:S(2)}, u32[]{:S(2)}) %collective-permute-start.15) | collective-permute-done | bytes 262176 | tf_op jit(solution)/shard_map/ppermute | solution.py:312
  58.0 2.0 %shard_map.105 = (bf16[4,1024,128]{2,1,0:T(8,128)(2,1)S(1)}, f32[4,2,512]{2,1,0:T(2,128)S(1)}, f32[4,8,128]{2,1,0:T(8,128)S(1)}) custom-call(s32[4]{0:T(128)S(1)} %copy-done.6, bf16[128,16,128]{2,1,0:T(8,128)(2,1)S(1)} %all-to-all-done.g_ref, bf16[1040,128]{1,0:T(8,128)(2,1)S(1)} %get-tuple-element.41.refs_0_, ...), custom_call_target="tpu_custom_call" | custom-call | tf_op jit(solution)/shard_map/pallas_call | solution.py:336
  61.4 4.6 %shard_map.107 = (bf16[4,2,128,128]{3,2,1,0:T(8,128)(2,1)S(1)}, bf16[4,2,128,128]{3,2,1,0:T(8,128)(2,1)S(1)}, f32[4,128,512]{2,1,0:T(8,128)S(1)}) custom-call(bf16[4,1024,128]{2,1,0:T(8,128)(2,1)S(1)} %get-tuple-element.45.p_ref, f32[4,2,512]{2,1,0:T(2,128)S(1)} %get-tuple-element.46.stat_ref, bf16[4,2,128,128]{3,2,1,0:T(8,128)(2,1)S(1)} %pad_maximum_fusion.km_ref, ...), custom_call_target="tpu_custom_call" | custom-call | tf_op jit(solution)/shard_map/pallas_call | solution.py:344
  66.1 3.8 %shard_map.108 = (bf16[4,2,128,128]{3,2,1,0:T(8,128)(2,1)S(1)}, bf16[4,2,128,128]{3,2,1,0:T(8,128)(2,1)S(1)}, f32[4,128,512]{2,1,0:T(8,128)S(1)}) custom-call(bf16[4,1024,128]{2,1,0:T(8,128)(2,1)S(1)} %get-tuple-element.45.p_ref, f32[4,2,512]{2,1,0:T(2,128)S(1)} %get-tuple-element.46.stat_ref, ...), custom_call_target="tpu_custom_call", output_to_operand_aliasing={{2}: (4, {})} | custom-call | tf_op jit(solution)/shard_map/pallas_call | solution.py:345
  72.1 3.4 %collective-permute-start.29 = (bf16[3,4,2,128,128]{4,3,2,1,0:T(8,128)(2,1)S(1)}, bf16[3,4,2,128,128]{4,3,2,1,0:T(8,128)(2,1)S(1)}, u32[]{:S(2)}, u32[]{:S(2)}) collective-permute-start(bf16[3,4,2,128,128]{4,3,2,1,0:T(8,128)(2,1)S(1)} %get-tuple-element.69), channel_id=1, source_target_pairs={{0,7},{1,0},{2,1},{3,2},{4,3},{5,4},{6,5},{7,6},{8,15},{9,8},{10,9... | collective-permute-start | bytes 2359304 | tf_op jit(solution)/shard_map/ppermute | solution.py:312
  75.5 2.8 %shard_map.110 = (bf16[4,2,128,128]{3,2,1,0:T(8,128)(2,1)S(1)}, bf16[4,2,128,128]{3,2,1,0:T(8,128)(2,1)S(1)}, f32[4,128,512]{2,1,0:T(8,128)S(1)}) custom-call(bf16[4,1024,128]{2,1,0:T(8,128)(2,1)S(1)} %get-tuple-element.45.p_ref, f32[4,2,512]{2,1,0:T(2,128)S(1)} %get-tuple-element.46.stat_ref, ...), custom_call_target="tpu_custom_call", output_to_operand_aliasing={{2}: (4, {})} | custom-call | tf_op jit(solution)/shard_map/pallas_call | solution.py:351
  78.3 3.2 %shard_map.111 = (bf16[4,2,128,128]{3,2,1,0:T(8,128)(2,1)S(1)}, bf16[4,2,128,128]{3,2,1,0:T(8,128)(2,1)S(1)}, bf16[512,128]{1,0:T(8,128)(2,1)S(1)}, bf16[512,128...) custom-call(bf16[4,1024,128]{2,1,0:T(8,128)(2,1)S(1)} %get-tuple-element.45.p_ref, ...), custom_call_target="tpu_custom_call" | custom-call | tf_op jit(solution)/shard_map/pallas_call | solution.py:352
  83.6 3.9 %collective-permute-start.28 = (bf16[4,2,128,128]{3,2,1,0:T(8,128)(2,1)S(1)}, bf16[4,2,128,128]{3,2,1,0:T(8,128)(2,1)S(1)}, u32[]{:S(2)}, u32[]{:S(2)}) collective-permute-start(bf16[4,2,128,128]{3,2,1,0:T(8,128)(2,1)S(1)} %add_convert_fusion), channel_id=1, source_target_pairs={{0,6},{2,0},{4,2},{6,4},{1,7},{3,1},{5,3},{7,5},{8,14},{10,8},{12,... | collective-permute-start | bytes 786440 | tf_op jit(solution)/shard_map/ppermute | solution.py:312
  87.5 5.5 %collective-permute-done.25 = bf16[4,2,128,128]{3,2,1,0:T(8,128)(2,1)S(1)} collective-permute-done((bf16[4,2,128,128]{3,2,1,0:T(8,128)(2,1)S(1)}, bf16[4,2,128,128]{3,2,1,0:T(8,128)(2,1)S(1)}, u32[]{:S(2)}, u32[]{:S(2)}) %collective-permute-start.25) | collective-permute-done | bytes 262176 | tf_op jit(solution)/shard_map/ppermute | solution.py:312
  93.5 5.2 %collective-permute-start.30 = (bf16[4,2,128,128]{3,2,1,0:T(8,128)(2,1)S(1)}, bf16[4,2,128,128]{3,2,1,0:T(8,128)(2,1)S(1)}, u32[]{:S(2)}, u32[]{:S(2)}) collective-permute-start(bf16[4,2,128,128]{3,2,1,0:T(8,128)(2,1)S(1)} %get-tuple-element.70), channel_id=1, source_target_pairs={{0,96},{32,0},{64,32},{96,64},{1,97},{33,1},{65,33},{97,65},{2,98}... | collective-permute-start | bytes 786440 | tf_op jit(solution)/shard_map/ppermute | solution.py:312
  100.8 2.2 %collective-permute-start.19 = (bf16[512,128]{1,0:T(8,128)(2,1)S(1)}, bf16[512,128]{1,0:T(8,128)(2,1)S(1)}, u32[]{:S(2)}, u32[]{:S(2)}) collective-permute-start(bf16[512,128]{1,0:T(8,128)(2,1)S(1)} %get-tuple-element.57), channel_id=1, source_target_pairs={{0,24},{8,0},{16,8},{24,16},{1,25},{9,1},{17,9},{25,17},{2,26},{10... | collective-permute-start | bytes 393224 | tf_op jit(solution)/shard_map/ppermute | solution.py:312
  104.1 5.8 %collective-permute-done.30.refs_4_ = bf16[4,2,128,128]{3,2,1,0:T(8,128)(2,1)S(1)} collective-permute-done((bf16[4,2,128,128]{3,2,1,0:T(8,128)(2,1)S(1)}, bf16[4,2,128,128]{3,2,1,0:T(8,128)(2,1)S(1)}, u32[]{:S(2)}, u32[]{:S(2)}) %collective-permute-start.30) | collective-permute-done | bytes 262176 | tf_op jit(solution)/shard_map/ppermute | solution.py:312
  110.9 2.7 %collective-permute-done.32.refs_6_ = bf16[4,2,128,128]{3,2,1,0:T(8,128)(2,1)S(1)} collective-permute-done((bf16[4,2,128,128]{3,2,1,0:T(8,128)(2,1)S(1)}, bf16[4,2,128,128]{3,2,1,0:T(8,128)(2,1)S(1)}, u32[]{:S(2)}, u32[]{:S(2)}) %collective-permute-start.32) | collective-permute-done | bytes 262176 | tf_op jit(solution)/shard_map/ppermute | solution.py:312
  113.8 2.1 %collective-permute-start.33 = (bf16[2,128,128]{2,1,0:T(8,128)(2,1)S(1)}, bf16[2,128,128]{2,1,0:T(8,128)(2,1)S(1)}, u32[]{:S(2)}, u32[]{:S(2)}) collective-permute-start(bf16[2,128,128]{2,1,0:T(8,128)(2,1)S(1)} %get-tuple-element.74), channel_id=1, source_target_pairs={{0,24},{8,0},{16,8},{24,16},{1,25},{9,1},{17,9},{25,17},{2,26},{10... | collective-permute-start | bytes 196616 | tf_op jit(solution)/shard_map/ppermute | solution.py:312
  119.0 2.9 %collective-permute-done.34.d2 = bf16[2,128,128]{2,1,0:T(8,128)(2,1)S(1)} collective-permute-done((bf16[2,128,128]{2,1,0:T(8,128)(2,1)S(1)}, bf16[2,128,128]{2,1,0:T(8,128)(2,1)S(1)}, u32[]{:S(2)}, u32[]{:S(2)}) %collective-permute-start.34) | collective-permute-done | bytes 65568 | tf_op jit(solution)/shard_map/ppermute | solution.py:312
  (83 shorter events, 31.2 us)
Async XLA Ops:
  12.3 14.2 %collective-permute-start = (bf16[1040,128]{1,0:T(8,128)(2,1)S(1)}, bf16[1040,128]{1,0:T(8,128)(2,1)S(1)}, u32[]{:S(2)}, u32[]{:S(2)}) collective-permute-start(bf16[1040,128]{1,0:T(8,128)(2,1)S(1)} %get-tuple-element.42), channel_id=1, source_target_pairs={{0,8},{8,16},{16,24},{24,0},{1,9},{9,17},{17,25},{25,1},{2,10},{10... | collective-permute-start | bytes 798728 | tf_op jit(solution)/shard_map/ppermute | solution.py:312
  17.1 20.8 %collective-permute-start.1 = (bf16[1040,128]{1,0:T(8,128)(2,1)}, bf16[1040,128]{1,0:T(8,128)(2,1)S(1)}, u32[]{:S(2)}, u32[]{:S(2)}) collective-permute-start(bf16[1040,128]{1,0:T(8,128)(2,1)} %get-tuple-element.43), channel_id=1, source_target_pairs={{0,16},{8,24},{16,0},{24,8},{1,17},{9,25},{17,1},{25,9},{2,18},{10... | collective-permute-start | bytes 798728 | tf_op jit(solution)/shard_map/ppermute | solution.py:312
  17.7 23.1 %collective-permute-start.2 = (bf16[1040,128]{1,0:T(8,128)(2,1)}, bf16[1040,128]{1,0:T(8,128)(2,1)S(1)}, u32[]{:S(2)}, u32[]{:S(2)}) collective-permute-start(bf16[1040,128]{1,0:T(8,128)(2,1)} %get-tuple-element.44), channel_id=1, source_target_pairs={{0,24},{8,0},{16,8},{24,16},{1,25},{9,1},{17,9},{25,17},{2,26},{10... | collective-permute-start | bytes 798728 | tf_op jit(solution)/shard_map/ppermute | solution.py:312
  19.8 21.9 %collective-permute-start.12 = (bf16[4,2,128,128]{3,2,1,0:T(8,128)(2,1)S(1)}, bf16[4,2,128,128]{3,2,1,0:T(8,128)(2,1)S(1)}, u32[]{:S(2)}, u32[]{:S(2)}) collective-permute-start(bf16[4,2,128,128]{3,2,1,0:T(8,128)(2,1)S(1)} %pad_maximum_fusion.km_ref), channel_id=1, source_target_pairs={{0,1},{1,0},{2,3},{3,2},{4,5},{5,4},{6,7},{7,6},{8,9},{9,8},{10,11... | collective-permute-start | bytes 786440 | tf_op jit(solution)/shard_map/ppermute | solution.py:312
  21.5 21.7 %collective-permute-start.10 = (bf16[4,2,128,128]{3,2,1,0:T(8,128)(2,1)S(1)}, bf16[4,2,128,128]{3,2,1,0:T(8,128)(2,1)S(1)}, u32[]{:S(2)}, u32[]{:S(2)}) collective-permute-start(bf16[4,2,128,128]{3,2,1,0:T(8,128)(2,1)S(1)} %collective-permute-done.8.km_ref), channel_id=1, source_target_pairs={{0,6},{2,0},{4,2},{6,4},{1,7},{3,1},{5,3},{7,5},{8,14},{10,8},{12,... | collective-permute-start | bytes 786440 | tf_op jit(solution)/shard_map/ppermute | solution.py:312
  26.5 16.7 %collective-permute-start.13 = (bf16[4,2,128,128]{3,2,1,0:T(8,128)(2,1)S(1)}, bf16[4,2,128,128]{3,2,1,0:T(8,128)(2,1)S(1)}, u32[]{:S(2)}, u32[]{:S(2)}) collective-permute-start(bf16[4,2,128,128]{3,2,1,0:T(8,128)(2,1)S(1)} %pad_maximum_fusion.km_ref), channel_id=1, source_target_pairs={{0,32},{32,64},{64,96},{96,0},{1,33},{33,65},{65,97},{97,1},{2,34}... | collective-permute-start | bytes 786440 | tf_op jit(solution)/shard_map/ppermute | solution.py:312
  29.8 28.1 %all-to-all-start = ((bf16[128,16,128]{2,1,0:T(8,128)(2,1)}), bf16[128,16,128]{2,1,0:T(8,128)(2,1)S(1)}, u32[]{:S(2)}, u32[]{:S(2)}) async-start(bf16[128,16,128]{2,1,0:T(8,128)(2,1)} %shard_map.103), calls=%async_computation | async-start | bytes 1048576 | tf_op jit(solution)/shard_map/all_to_all | solution.py:333
  37.8 14.9 %collective-permute-start.14 = (bf16[4,2,128,128]{3,2,1,0:T(8,128)(2,1)S(1)}, bf16[4,2,128,128]{3,2,1,0:T(8,128)(2,1)S(1)}, u32[]{:S(2)}, u32[]{:S(2)}) collective-permute-start(bf16[4,2,128,128]{3,2,1,0:T(8,128)(2,1)S(1)} %pad_maximum_fusion.km_ref), channel_id=1, source_target_pairs={{0,64},{32,96},{64,0},{96,32},{1,65},{33,97},{65,1},{97,33},{2,66}... | collective-permute-start | bytes 786440 | tf_op jit(solution)/shard_map/ppermute | solution.py:312
  40.8 17.2 %collective-permute-start.15 = (bf16[4,2,128,128]{3,2,1,0:T(8,128)(2,1)S(1)}, bf16[4,2,128,128]{3,2,1,0:T(8,128)(2,1)}, u32[]{:S(2)}, u32[]{:S(2)}) collective-permute-start(bf16[4,2,128,128]{3,2,1,0:T(8,128)(2,1)S(1)} %pad_maximum_fusion.km_ref), channel_id=1, source_target_pairs={{0,96},{32,0},{64,32},{96,64},{1,97},{33,1},{65,33},{97,65},{2,98}... | collective-permute-start | bytes 786440 | tf_op jit(solution)/shard_map/ppermute | solution.py:312
  41.7 18.3 %collective-permute-start.6 = (bf16[4,2,128,128]{3,2,1,0:T(8,128)(2,1)S(1)}, bf16[4,2,128,128]{3,2,1,0:T(8,128)(2,1)S(1)}, u32[]{:S(2)}, u32[]{:S(2)}) collective-permute-start(bf16[4,2,128,128]{3,2,1,0:T(8,128)(2,1)S(1)} %pad_maximum_fusion.km_ref), channel_id=1, source_target_pairs={{0,2},{2,4},{4,6},{6,0},{1,3},{3,5},{5,7},{7,1},{8,10},{10,12},{12... | collective-permute-start | bytes 786440 | tf_op jit(solution)/shard_map/ppermute | solution.py:312
  43.2 18.2 %collective-permute-start.11 = (bf16[4,2,128,128]{3,2,1,0:T(8,128)(2,1)S(1)}, bf16[4,2,128,128]{3,2,1,0:T(8,128)(2,1)}, u32[]{:S(2)}, u32[]{:S(2)}) collective-permute-start(bf16[4,2,128,128]{3,2,1,0:T(8,128)(2,1)S(1)} %collective-permute-done.10.km_ref), channel_id=1, source_target_pairs={{0,1},{1,0},{2,3},{3,2},{4,5},{5,4},{6,7},{7,6},{8,9},{9,8},{10,11... | collective-permute-start | bytes 786440 | tf_op jit(solution)/shard_map/ppermute | solution.py:312
  43.2 26.7 %collective-permute-start.16 = (bf16[4,2,128,128]{3,2,1,0:T(8,128)(2,1)S(1)}, bf16[4,2,128,128]{3,2,1,0:T(8,128)(2,1)}, u32[]{:S(2)}, u32[]{:S(2)}) collective-permute-start(bf16[4,2,128,128]{3,2,1,0:T(8,128)(2,1)S(1)} %collective-permute-done.13.refs_0_), channel_id=1, source_target_pairs={{0,1},{1,2},{2,3},{3,4},{4,5},{5,6},{6,7},{7,0},{8,9},{9,10},{10,1... | collective-permute-start | bytes 786440 | tf_op jit(solution)/shard_map/ppermute | solution.py:312
  52.7 17.6 %collective-permute-start.17 = (bf16[4,2,128,128]{3,2,1,0:T(8,128)(2,1)S(1)}, bf16[4,2,128,128]{3,2,1,0:T(8,128)(2,1)}, u32[]{:S(2)}, u32[]{:S(2)}) collective-permute-start(bf16[4,2,128,128]{3,2,1,0:T(8,128)(2,1)S(1)} %collective-permute-done.14.refs_1_), channel_id=1, source_target_pairs={{0,1},{1,2},{2,3},{3,4},{4,5},{5,6},{6,7},{7,0},{8,9},{9,10},{10,1... | collective-permute-start | bytes 786440 | tf_op jit(solution)/shard_map/ppermute | solution.py:312
  58.0 12.4 %collective-permute-start.18 = (bf16[4,2,128,128]{3,2,1,0:T(8,128)(2,1)}, bf16[4,2,128,128]{3,2,1,0:T(8,128)(2,1)}, u32[]{:S(2)}, u32[]{:S(2)}) collective-permute-start(bf16[4,2,128,128]{3,2,1,0:T(8,128)(2,1)} %collective-permute-done.15.refs_2_), channel_id=1, source_target_pairs={{0,1},{1,2},{2,3},{3,4},{4,5},{5,6},{6,7},{7,0},{8,9},{9,10},{10,1... | collective-permute-start | bytes 786440 | tf_op jit(solution)/shard_map/ppermute | solution.py:312
  60.0 15.5 %collective-permute-start.9 = (bf16[4,2,128,128]{3,2,1,0:T(8,128)(2,1)S(1)}, bf16[4,2,128,128]{3,2,1,0:T(8,128)(2,1)S(1)}, u32[]{:S(2)}, u32[]{:S(2)}) collective-permute-start(bf16[4,2,128,128]{3,2,1,0:T(8,128)(2,1)S(1)} %collective-permute-done.8.km_ref), channel_id=1, source_target_pairs={{0,1},{1,0},{2,3},{3,2},{4,5},{5,4},{6,7},{7,6},{8,9},{9,8},{10,11... | collective-permute-start | bytes 786440 | tf_op jit(solution)/shard_map/ppermute | solution.py:312
  61.3 17.0 %collective-permute-start.7 = (bf16[4,2,128,128]{3,2,1,0:T(8,128)(2,1)S(1)}, bf16[4,2,128,128]{3,2,1,0:T(8,128)(2,1)S(1)}, u32[]{:S(2)}, u32[]{:S(2)}) collective-permute-start(bf16[4,2,128,128]{3,2,1,0:T(8,128)(2,1)S(1)} %collective-permute-done.6.km_ref), channel_id=1, source_target_pairs={{0,1},{1,0},{2,3},{3,2},{4,5},{5,4},{6,7},{7,6},{8,9},{9,8},{10,11... | collective-permute-start | bytes 786440 | tf_op jit(solution)/shard_map/ppermute | solution.py:312
  69.8 12.2 %collective-permute-start.24 = (bf16[4,2,128,128]{3,2,1,0:T(8,128)(2,1)S(1)}, bf16[4,2,128,128]{3,2,1,0:T(8,128)(2,1)S(1)}, u32[]{:S(2)}, u32[]{:S(2)}) collective-permute-start(bf16[4,2,128,128]{3,2,1,0:T(8,128)(2,1)S(1)} %get-tuple-element.65), channel_id=1, source_target_pairs={{0,1},{1,0},{2,3},{3,2},{4,5},{5,4},{6,7},{7,6},{8,9},{9,8},{10,11... | collective-permute-start | bytes 786440 | tf_op jit(solution)/shard_map/ppermute | solution.py:312
  72.1 21.2 %collective-permute-start.29 = (bf16[3,4,2,128,128]{4,3,2,1,0:T(8,128)(2,1)S(1)}, bf16[3,4,2,128,128]{4,3,2,1,0:T(8,128)(2,1)S(1)}, u32[]{:S(2)}, u32[]{:S(2)}) collective-permute-start(bf16[3,4,2,128,128]{4,3,2,1,0:T(8,128)(2,1)S(1)} %get-tuple-element.69), channel_id=1, source_target_pairs={{0,7},{1,0},{2,1},{3,2},{4,3},{5,4},{6,5},{7,6},{8,15},{9,8},{10,9... | collective-permute-start | bytes 2359304 | tf_op jit(solution)/shard_map/ppermute | solution.py:312
  83.5 16.2 %collective-permute-start.22 = (bf16[4,2,128,128]{3,2,1,0:T(8,128)(2,1)S(1)}, bf16[4,2,128,128]{3,2,1,0:T(8,128)(2,1)S(1)}, u32[]{:S(2)}, u32[]{:S(2)}) collective-permute-start(bf16[4,2,128,128]{3,2,1,0:T(8,128)(2,1)S(1)} %get-tuple-element.61), channel_id=1, source_target_pairs={{0,1},{1,0},{2,3},{3,2},{4,5},{5,4},{6,7},{7,6},{8,9},{9,8},{10,11... | collective-permute-start | bytes 786440 | tf_op jit(solution)/shard_map/ppermute | solution.py:312
  83.6 17.3 %collective-permute-start.28 = (bf16[4,2,128,128]{3,2,1,0:T(8,128)(2,1)S(1)}, bf16[4,2,128,128]{3,2,1,0:T(8,128)(2,1)S(1)}, u32[]{:S(2)}, u32[]{:S(2)}) collective-permute-start(bf16[4,2,128,128]{3,2,1,0:T(8,128)(2,1)S(1)} %add_convert_fusion), channel_id=1, source_target_pairs={{0,6},{2,0},{4,2},{6,4},{1,7},{3,1},{5,3},{7,5},{8,14},{10,8},{12,... | collective-permute-start | bytes 786440 | tf_op jit(solution)/shard_map/ppermute | solution.py:312
  93.5 16.4 %collective-permute-start.30 = (bf16[4,2,128,128]{3,2,1,0:T(8,128)(2,1)S(1)}, bf16[4,2,128,128]{3,2,1,0:T(8,128)(2,1)S(1)}, u32[]{:S(2)}, u32[]{:S(2)}) collective-permute-start(bf16[4,2,128,128]{3,2,1,0:T(8,128)(2,1)S(1)} %get-tuple-element.70), channel_id=1, source_target_pairs={{0,96},{32,0},{64,32},{96,64},{1,97},{33,1},{65,33},{97,65},{2,98}... | collective-permute-start | bytes 786440 | tf_op jit(solution)/shard_map/ppermute | solution.py:312
  99.7 13.9 %collective-permute-start.32 = (bf16[4,2,128,128]{3,2,1,0:T(8,128)(2,1)S(1)}, bf16[4,2,128,128]{3,2,1,0:T(8,128)(2,1)S(1)}, u32[]{:S(2)}, u32[]{:S(2)}) collective-permute-start(bf16[4,2,128,128]{3,2,1,0:T(8,128)(2,1)S(1)} %get-tuple-element.72), channel_id=1, source_target_pairs={{0,32},{32,64},{64,96},{96,0},{1,33},{33,65},{65,97},{97,1},{2,34}... | collective-permute-start | bytes 786440 | tf_op jit(solution)/shard_map/ppermute | solution.py:312
  100.8 16.1 %collective-permute-start.19 = (bf16[512,128]{1,0:T(8,128)(2,1)S(1)}, bf16[512,128]{1,0:T(8,128)(2,1)S(1)}, u32[]{:S(2)}, u32[]{:S(2)}) collective-permute-start(bf16[512,128]{1,0:T(8,128)(2,1)S(1)} %get-tuple-element.57), channel_id=1, source_target_pairs={{0,24},{8,0},{16,8},{24,16},{1,25},{9,1},{17,9},{25,17},{2,26},{10... | collective-permute-start | bytes 393224 | tf_op jit(solution)/shard_map/ppermute | solution.py:312
  103.0 14.4 %collective-permute-start.20 = (bf16[512,128]{1,0:T(8,128)(2,1)S(1)}, bf16[512,128]{1,0:T(8,128)(2,1)S(1)}, u32[]{:S(2)}, u32[]{:S(2)}) collective-permute-start(bf16[512,128]{1,0:T(8,128)(2,1)S(1)} %get-tuple-element.58), channel_id=1, source_target_pairs={{0,16},{8,24},{16,0},{24,8},{1,17},{9,25},{17,1},{25,9},{2,18},{10... | collective-permute-start | bytes 393224 | tf_op jit(solution)/shard_map/ppermute | solution.py:312
  (21 other events, 147.2 us)

commit v3 on v2

--- a/solution.py
+++ b/solution.py
@@ -341,15 +341,15 @@
         [pltpu.VMEM((128, 16, HD), F32)],
     )(lengths, arrived, *qo)
     mine, other, dq = {}, {}, None
-    mine[0], other[0], dq = make_own(0, True, False)(pay, stat, near[0], far[0])
+    mine[3], other[3], dq = make_own(3, True, False)(pay, stat, near[3], far[3])
     mine[2], other[2], dq = make_own(2, False, False)(pay, stat, near[2], far[2], dq)
     trio = shape((3, 4, 2, B, HD), BF16)
     scratch = [pltpu.VMEM((16, 2 * B, HD), BF16)] * 2 + [pltpu.SMEM((16,), jnp.int32)]
     scratch += [pltpu.VMEM((2 * B, ROWS), BF16)] * 4
     sibling = call(sibling_kernel, (trio, trio, shape((4, HD, ROWS), F32)), 1, 10, scratch, {4: 2})
     dcur, dprev, dq = sibling(lengths, pay, stat, mark, dq, *cur, *prev)
-    mine[3], other[3], dq = make_own(3, False, False)(pay, stat, near[3], far[3], dq)
-    mine[1], other[1], *dq_sent = make_own(1, False, True)(pay, stat, near[1], far[1], dq)
+    mine[1], other[1], dq = make_own(1, False, False)(pay, stat, near[1], far[1], dq)
+    mine[0], other[0], *dq_sent = make_own(0, False, True)(pay, stat, near[0], far[0], dq)
     terms = [mine[0], ring(other[0], "c", 1, 2)]
     both = {d: mine[d].astype(F32) + ring(other[d], "c", 1, 2).astype(F32) for d in dists}
     passing = ring(both[2].astype(BF16), "x", 1, 4)

time: 124 us -> 116 us (0.935)
  waiting for transfers between devices: 35.7 us -> 31 us
  starting transfers between devices: 58.6 us -> 55.4 us
    ppermute x36, waiting for transfers between devices: 35.7 us -> 31 us  [ring(): lax.ppermute(x, axis, [(j, (j + step) % count) for j in range(count)])]
    ppermute x36, starting transfers between devices: 50.7 us -> 47.9 us  [ring(): lax.ppermute(x, axis, [(j, (j + step) % count) for j in range(count)])]
  transfers between devices with their start and end apart: 37 -> 37, of which waited for: 10 -> 10; matrix products, arithmetic and copies ran while one was open for 0% -> 0% of each run, Pallas kernels for 18% -> 20%
where the time goes in v3:
time: 116 us; the launch traced here: 115 us
  starting transfers between devices  55.4 us (48%)
  waiting for transfers between devices  31 us (27%)
  Pallas kernels  24.2 us (21%)
  local copies, waits for them, and re-layouts  3.57 us (3%)
    ppermute x36, starting transfers between devices, ring(): lax.ppermute(x, axis, [(j, (j + step) % count) for j in range(count)])  47.9 us
    ppermute x36, waiting for transfers between devices, ring(): lax.ppermute(x, axis, [(j, (j + step) % count) for j in range(count)])  31 us
    all_to_all x1, starting transfers between devices, step(): arrived = lax.all_to_all(dealt, ('z', 'y', 'x', 'c'), 0, 0, tiled=True)  7.47 us
    pallas_call x1, Pallas kernels, step(): make_own(0, False, True)(pay, stat, near[0], far[0], dq)  5.03 us
    pallas_call x1, Pallas kernels, step(): mine[3], other[3], dq = make_own(3, True, False)(pay, stat, near[3], far[3])  3.79 us
    pallas_call x1, Pallas kernels, step(): make_own(2, False, False)(pay, stat, near[2], far[2], dq)  3.75 us
    unnamed x16, local copies, waits for them, and re-layouts  3.57 us
    pallas_call x1, Pallas kernels, step(): make_own(1, False, False)(pay, stat, near[1], far[1], dq)  2.8 us
  transfers between devices with their start and end apart: 37, of which 10 were waited for; matrix products, arithmetic and copies ran while one was open for 0% of the time, Pallas kernels for 20%

profile of v3, /device:TPU:0, one launch (start us, length us, event | category | flops | bytes accessed | tf_op | source)
XLA Modules:
  0.0 115.3 jit_solution(5855644929949827108)
XLA Ops:
  2.6 3.2 %collective-permute-start.5 = (bf16[2,128,128]{2,1,0:T(8,128)(2,1)S(1)}, bf16[2,128,128]{2,1,0:T(8,128)(2,1)S(1)}, u32[]{:S(2)}, u32[]{:S(2)}) collective-permute-start(bf16[2,128,128]{2,1,0:T(8,128)(2,1)S(1)} %get-tuple-element.50), channel_id=1, source_target_pairs={{0,24},{8,0},{16,8},{24,16},{1,25},{9,1},{17,9},{25,17},{2,26},{10... | collective-permute-start | bytes 196616 | tf_op jit(solution)/shard_map/ppermute | solution.py:312
  5.8 2.2 %collective-permute-start.4 = (bf16[2,128,128]{2,1,0:T(8,128)(2,1)S(1)}, bf16[2,128,128]{2,1,0:T(8,128)(2,1)S(1)}, u32[]{:S(2)}, u32[]{:S(2)}) collective-permute-start(bf16[2,128,128]{2,1,0:T(8,128)(2,1)S(1)} %get-tuple-element.49), channel_id=1, source_target_pairs={{0,16},{8,24},{16,0},{24,8},{1,17},{9,25},{17,1},{25,9},{2,18},{10... | collective-permute-start | bytes 196616 | tf_op jit(solution)/shard_map/ppermute | solution.py:312
  8.0 4.1 %collective-permute-done.3 = bf16[2,128,128]{2,1,0:T(8,128)(2,1)S(1)} collective-permute-done((bf16[2,128,128]{2,1,0:T(8,128)(2,1)S(1)}, bf16[2,128,128]{2,1,0:T(8,128)(2,1)S(1)}, u32[]{:S(2)}, u32[]{:S(2)}) %collective-permute-start.3) | collective-permute-done | bytes 65568 | tf_op jit(solution)/shard_map/ppermute | solution.py:312
  12.1 2.8 %collective-permute-start.9 = (bf16[4,2,128,128]{3,2,1,0:T(8,128)(2,1)S(1)}, bf16[4,2,128,128]{3,2,1,0:T(8,128)(2,1)S(1)}, u32[]{:S(2)}, u32[]{:S(2)}) collective-permute-start(bf16[4,2,128,128]{3,2,1,0:T(8,128)(2,1)S(1)} %pad_maximum_fusion.km_ref), channel_id=1, source_target_pairs={{0,6},{2,0},{4,2},{6,4},{1,7},{3,1},{5,3},{7,5},{8,14},{10,8},{12,... | collective-permute-start | bytes 786440 | tf_op jit(solution)/shard_map/ppermute | solution.py:312
  18.3 4.1 %collective-permute-start.1 = (bf16[1040,128]{1,0:T(8,128)(2,1)}, bf16[1040,128]{1,0:T(8,128)(2,1)S(1)}, u32[]{:S(2)}, u32[]{:S(2)}) collective-permute-start(bf16[1040,128]{1,0:T(8,128)(2,1)} %get-tuple-element.43), channel_id=1, source_target_pairs={{0,16},{8,24},{16,0},{24,8},{1,17},{9,25},{17,1},{25,9},{2,18},{10... | collective-permute-start | bytes 798728 | tf_op jit(solution)/shard_map/ppermute | solution.py:312
  22.6 1.9 %collective-permute-start.13 = (bf16[4,2,128,128]{3,2,1,0:T(8,128)(2,1)S(1)}, bf16[4,2,128,128]{3,2,1,0:T(8,128)(2,1)S(1)}, u32[]{:S(2)}, u32[]{:S(2)}) collective-permute-start(bf16[4,2,128,128]{3,2,1,0:T(8,128)(2,1)S(1)} %pad_maximum_fusion.km_ref), channel_id=1, source_target_pairs={{0,32},{32,64},{64,96},{96,0},{1,33},{33,65},{65,97},{97,1},{2,34}... | collective-permute-start | bytes 786440 | tf_op jit(solution)/shard_map/ppermute | solution.py:312
  26.7 7.5 %all-to-all-start = ((bf16[128,16,128]{2,1,0:T(8,128)(2,1)}), bf16[128,16,128]{2,1,0:T(8,128)(2,1)S(1)}, u32[]{:S(2)}, u32[]{:S(2)}) async-start(bf16[128,16,128]{2,1,0:T(8,128)(2,1)} %shard_map.103), calls=%async_computation | async-start | bytes 1048576 | tf_op jit(solution)/shard_map/all_to_all | solution.py:333
  34.2 2.9 %collective-permute-start.14 = (bf16[4,2,128,128]{3,2,1,0:T(8,128)(2,1)S(1)}, bf16[4,2,128,128]{3,2,1,0:T(8,128)(2,1)S(1)}, u32[]{:S(2)}, u32[]{:S(2)}) collective-permute-start(bf16[4,2,128,128]{3,2,1,0:T(8,128)(2,1)S(1)} %pad_maximum_fusion.km_ref), channel_id=1, source_target_pairs={{0,64},{32,96},{64,0},{96,32},{1,65},{33,97},{65,1},{97,33},{2,66}... | collective-permute-start | bytes 786440 | tf_op jit(solution)/shard_map/ppermute | solution.py:312
  40.1 9.0 %collective-permute-done.14.refs_1_ = bf16[4,2,128,128]{3,2,1,0:T(8,128)(2,1)S(1)} collective-permute-done((bf16[4,2,128,128]{3,2,1,0:T(8,128)(2,1)S(1)}, bf16[4,2,128,128]{3,2,1,0:T(8,128)(2,1)S(1)}, u32[]{:S(2)}, u32[]{:S(2)}) %collective-permute-start.14) | collective-permute-done | bytes 262176 | tf_op jit(solution)/shard_map/ppermute | solution.py:312
  49.1 5.1 %collective-permute-done.15.refs_2_ = bf16[4,2,128,128]{3,2,1,0:T(8,128)(2,1)S(1)} collective-permute-done((bf16[4,2,128,128]{3,2,1,0:T(8,128)(2,1)S(1)}, bf16[4,2,128,128]{3,2,1,0:T(8,128)(2,1)S(1)}, u32[]{:S(2)}, u32[]{:S(2)}) %collective-permute-start.15) | collective-permute-done | bytes 262176 | tf_op jit(solution)/shard_map/ppermute | solution.py:312
  55.5 2.0 %shard_map.105 = (bf16[4,1024,128]{2,1,0:T(8,128)(2,1)S(1)}, f32[4,2,512]{2,1,0:T(2,128)S(1)}, f32[4,8,128]{2,1,0:T(8,128)S(1)}) custom-call(s32[4]{0:T(128)S(1)} %copy-done.6, bf16[128,16,128]{2,1,0:T(8,128)(2,1)S(1)} %all-to-all-done.g_ref, bf16[1040,128]{1,0:T(8,128)(2,1)S(1)} %get-tuple-element.41.refs_0_, ...), custom_call_target="tpu_custom_call" | custom-call | tf_op jit(solution)/shard_map/pallas_call | solution.py:336
  57.7 3.8 %shard_map.107 = (bf16[4,2,128,128]{3,2,1,0:T(8,128)(2,1)S(1)}, bf16[4,2,128,128]{3,2,1,0:T(8,128)(2,1)S(1)}, f32[4,128,512]{2,1,0:T(8,128)S(1)}) custom-call(bf16[4,1024,128]{2,1,0:T(8,128)(2,1)S(1)} %get-tuple-element.45.p_ref, f32[4,2,512]{2,1,0:T(2,128)S(1)} %get-tuple-element.46.stat_ref, bf16[4,2,128,128]{3,2,1,0:T(8,128)(2,1)S(1)} %collective-permute-done.9.km_ref, ...), custom_call_target="tpu_custom_call" | custom-call | tf_op jit(solution)/shard_map/pallas_call | solution.py:344
  61.5 3.8 %shard_map.108 = (bf16[4,2,128,128]{3,2,1,0:T(8,128)(2,1)S(1)}, bf16[4,2,128,128]{3,2,1,0:T(8,128)(2,1)S(1)}, f32[4,128,512]{2,1,0:T(8,128)S(1)}) custom-call(bf16[4,1024,128]{2,1,0:T(8,128)(2,1)S(1)} %get-tuple-element.45.p_ref, f32[4,2,512]{2,1,0:T(2,128)S(1)} %get-tuple-element.46.stat_ref, ...), custom_call_target="tpu_custom_call", output_to_operand_aliasing={{2}: (4, {})} | custom-call | tf_op jit(solution)/shard_map/pallas_call | solution.py:345
  67.4 5.0 %collective-permute-start.29 = (bf16[3,4,2,128,128]{4,3,2,1,0:T(8,128)(2,1)S(1)}, bf16[3,4,2,128,128]{4,3,2,1,0:T(8,128)(2,1)S(1)}, u32[]{:S(2)}, u32[]{:S(2)}) collective-permute-start(bf16[3,4,2,128,128]{4,3,2,1,0:T(8,128)(2,1)S(1)} %get-tuple-element.69), channel_id=1, source_target_pairs={{0,7},{1,0},{2,1},{3,2},{4,3},{5,4},{6,5},{7,6},{8,15},{9,8},{10,9... | collective-permute-start | bytes 2359304 | tf_op jit(solution)/shard_map/ppermute | solution.py:312
  72.5 2.8 %shard_map.110 = (bf16[4,2,128,128]{3,2,1,0:T(8,128)(2,1)S(1)}, bf16[4,2,128,128]{3,2,1,0:T(8,128)(2,1)S(1)}, f32[4,128,512]{2,1,0:T(8,128)S(1)}) custom-call(bf16[4,1024,128]{2,1,0:T(8,128)(2,1)S(1)} %get-tuple-element.45.p_ref, f32[4,2,512]{2,1,0:T(2,128)S(1)} %get-tuple-element.46.stat_ref, ...), custom_call_target="tpu_custom_call", output_to_operand_aliasing={{2}: (4, {})} | custom-call | tf_op jit(solution)/shard_map/pallas_call | solution.py:351
  76.1 5.0 %shard_map.111 = (bf16[4,2,128,128]{3,2,1,0:T(8,128)(2,1)S(1)}, bf16[4,2,128,128]{3,2,1,0:T(8,128)(2,1)S(1)}, bf16[512,128]{1,0:T(8,128)(2,1)S(1)}, bf16[512,128...) custom-call(bf16[4,1024,128]{2,1,0:T(8,128)(2,1)S(1)} %get-tuple-element.45.p_ref, ...), custom_call_target="tpu_custom_call" | custom-call | tf_op jit(solution)/shard_map/pallas_call | solution.py:352
  81.8 3.0 %collective-permute-start.28 = (bf16[4,2,128,128]{3,2,1,0:T(8,128)(2,1)S(1)}, bf16[4,2,128,128]{3,2,1,0:T(8,128)(2,1)S(1)}, u32[]{:S(2)}, u32[]{:S(2)}) collective-permute-start(bf16[4,2,128,128]{3,2,1,0:T(8,128)(2,1)S(1)} %add_convert_fusion), channel_id=1, source_target_pairs={{0,6},{2,0},{4,2},{6,4},{1,7},{3,1},{5,3},{7,5},{8,14},{10,8},{12,... | collective-permute-start | bytes 786440 | tf_op jit(solution)/shard_map/ppermute | solution.py:312
  86.4 4.6 %collective-permute-start.30 = (bf16[4,2,128,128]{3,2,1,0:T(8,128)(2,1)S(1)}, bf16[4,2,128,128]{3,2,1,0:T(8,128)(2,1)S(1)}, u32[]{:S(2)}, u32[]{:S(2)}) collective-permute-start(bf16[4,2,128,128]{3,2,1,0:T(8,128)(2,1)S(1)} %get-tuple-element.70), channel_id=1, source_target_pairs={{0,96},{32,0},{64,32},{96,64},{1,97},{33,1},{65,33},{97,65},{2,98}... | collective-permute-start | bytes 786440 | tf_op jit(solution)/shard_map/ppermute | solution.py:312
  91.0 2.3 %collective-permute-start.31 = (bf16[4,2,128,128]{3,2,1,0:T(8,128)(2,1)S(1)}, bf16[4,2,128,128]{3,2,1,0:T(8,128)(2,1)S(1)}, u32[]{:S(2)}, u32[]{:S(2)}) collective-permute-start(bf16[4,2,128,128]{3,2,1,0:T(8,128)(2,1)S(1)} %get-tuple-element.71), channel_id=1, source_target_pairs={{0,64},{32,96},{64,0},{96,32},{1,65},{33,97},{65,1},{97,33},{2,66}... | collective-permute-start | bytes 786440 | tf_op jit(solution)/shard_map/ppermute | solution.py:312
  93.3 2.4 %collective-permute-start.19 = (bf16[512,128]{1,0:T(8,128)(2,1)S(1)}, bf16[512,128]{1,0:T(8,128)(2,1)S(1)}, u32[]{:S(2)}, u32[]{:S(2)}) collective-permute-start(bf16[512,128]{1,0:T(8,128)(2,1)S(1)} %get-tuple-element.57), channel_id=1, source_target_pairs={{0,24},{8,0},{16,8},{24,16},{1,25},{9,1},{17,9},{25,17},{2,26},{10... | collective-permute-start | bytes 393224 | tf_op jit(solution)/shard_map/ppermute | solution.py:312
  99.5 2.2 %collective-permute-done.31.refs_5_ = bf16[4,2,128,128]{3,2,1,0:T(8,128)(2,1)S(1)} collective-permute-done((bf16[4,2,128,128]{3,2,1,0:T(8,128)(2,1)S(1)}, bf16[4,2,128,128]{3,2,1,0:T(8,128)(2,1)S(1)}, u32[]{:S(2)}, u32[]{:S(2)}) %collective-permute-start.31) | collective-permute-done | bytes 262176 | tf_op jit(solution)/shard_map/ppermute | solution.py:312
  101.7 3.8 %collective-permute-done.32.refs_6_ = bf16[4,2,128,128]{3,2,1,0:T(8,128)(2,1)S(1)} collective-permute-done((bf16[4,2,128,128]{3,2,1,0:T(8,128)(2,1)S(1)}, bf16[4,2,128,128]{3,2,1,0:T(8,128)(2,1)S(1)}, u32[]{:S(2)}, u32[]{:S(2)}) %collective-permute-start.32) | collective-permute-done | bytes 262176 | tf_op jit(solution)/shard_map/ppermute | solution.py:312
  105.8 2.1 %collective-permute-start.33 = (bf16[2,128,128]{2,1,0:T(8,128)(2,1)S(1)}, bf16[2,128,128]{2,1,0:T(8,128)(2,1)S(1)}, u32[]{:S(2)}, u32[]{:S(2)}) collective-permute-start(bf16[2,128,128]{2,1,0:T(8,128)(2,1)S(1)} %get-tuple-element.74), channel_id=1, source_target_pairs={{0,24},{8,0},{16,8},{24,16},{1,25},{9,1},{17,9},{25,17},{2,26},{10... | collective-permute-start | bytes 196616 | tf_op jit(solution)/shard_map/ppermute | solution.py:312
  110.9 2.9 %collective-permute-done.34.d2 = bf16[2,128,128]{2,1,0:T(8,128)(2,1)S(1)} collective-permute-done((bf16[2,128,128]{2,1,0:T(8,128)(2,1)S(1)}, bf16[2,128,128]{2,1,0:T(8,128)(2,1)S(1)}, u32[]{:S(2)}, u32[]{:S(2)}) %collective-permute-start.34) | collective-permute-done | bytes 65568 | tf_op jit(solution)/shard_map/ppermute | solution.py:312
  (83 shorter events, 25.8 us)
Async XLA Ops:
  12.1 12.4 %collective-permute-start.9 = (bf16[4,2,128,128]{3,2,1,0:T(8,128)(2,1)S(1)}, bf16[4,2,128,128]{3,2,1,0:T(8,128)(2,1)S(1)}, u32[]{:S(2)}, u32[]{:S(2)}) collective-permute-start(bf16[4,2,128,128]{3,2,1,0:T(8,128)(2,1)S(1)} %pad_maximum_fusion.km_ref), channel_id=1, source_target_pairs={{0,6},{2,0},{4,2},{6,4},{1,7},{3,1},{5,3},{7,5},{8,14},{10,8},{12,... | collective-permute-start | bytes 786440 | tf_op jit(solution)/shard_map/ppermute | solution.py:312
  18.2 16.0 %collective-permute-start = (bf16[1040,128]{1,0:T(8,128)(2,1)S(1)}, bf16[1040,128]{1,0:T(8,128)(2,1)S(1)}, u32[]{:S(2)}, u32[]{:S(2)}) collective-permute-start(bf16[1040,128]{1,0:T(8,128)(2,1)S(1)} %get-tuple-element.42), channel_id=1, source_target_pairs={{0,8},{8,16},{16,24},{24,0},{1,9},{9,17},{17,25},{25,1},{2,10},{10... | collective-permute-start | bytes 798728 | tf_op jit(solution)/shard_map/ppermute | solution.py:312
  18.3 18.9 %collective-permute-start.1 = (bf16[1040,128]{1,0:T(8,128)(2,1)}, bf16[1040,128]{1,0:T(8,128)(2,1)S(1)}, u32[]{:S(2)}, u32[]{:S(2)}) collective-permute-start(bf16[1040,128]{1,0:T(8,128)(2,1)} %get-tuple-element.43), channel_id=1, source_target_pairs={{0,16},{8,24},{16,0},{24,8},{1,17},{9,25},{17,1},{25,9},{2,18},{10... | collective-permute-start | bytes 798728 | tf_op jit(solution)/shard_map/ppermute | solution.py:312
  22.4 15.6 %collective-permute-start.2 = (bf16[1040,128]{1,0:T(8,128)(2,1)}, bf16[1040,128]{1,0:T(8,128)(2,1)S(1)}, u32[]{:S(2)}, u32[]{:S(2)}) collective-permute-start(bf16[1040,128]{1,0:T(8,128)(2,1)} %get-tuple-element.44), channel_id=1, source_target_pairs={{0,24},{8,0},{16,8},{24,16},{1,25},{9,1},{17,9},{25,17},{2,26},{10... | collective-permute-start | bytes 798728 | tf_op jit(solution)/shard_map/ppermute | solution.py:312
  22.6 17.0 %collective-permute-start.13 = (bf16[4,2,128,128]{3,2,1,0:T(8,128)(2,1)S(1)}, bf16[4,2,128,128]{3,2,1,0:T(8,128)(2,1)S(1)}, u32[]{:S(2)}, u32[]{:S(2)}) collective-permute-start(bf16[4,2,128,128]{3,2,1,0:T(8,128)(2,1)S(1)} %pad_maximum_fusion.km_ref), channel_id=1, source_target_pairs={{0,32},{32,64},{64,96},{96,0},{1,33},{33,65},{65,97},{97,1},{2,34}... | collective-permute-start | bytes 786440 | tf_op jit(solution)/shard_map/ppermute | solution.py:312
  24.5 15.1 %collective-permute-start.10 = (bf16[4,2,128,128]{3,2,1,0:T(8,128)(2,1)S(1)}, bf16[4,2,128,128]{3,2,1,0:T(8,128)(2,1)S(1)}, u32[]{:S(2)}, u32[]{:S(2)}) collective-permute-start(bf16[4,2,128,128]{3,2,1,0:T(8,128)(2,1)S(1)} %collective-permute-done.9.km_ref), channel_id=1, source_target_pairs={{0,6},{2,0},{4,2},{6,4},{1,7},{3,1},{5,3},{7,5},{8,14},{10,8},{12,... | collective-permute-start | bytes 786440 | tf_op jit(solution)/shard_map/ppermute | solution.py:312
  26.7 28.8 %all-to-all-start = ((bf16[128,16,128]{2,1,0:T(8,128)(2,1)}), bf16[128,16,128]{2,1,0:T(8,128)(2,1)S(1)}, u32[]{:S(2)}, u32[]{:S(2)}) async-start(bf16[128,16,128]{2,1,0:T(8,128)(2,1)} %shard_map.103), calls=%async_computation | async-start | bytes 1048576 | tf_op jit(solution)/shard_map/all_to_all | solution.py:333
  34.2 14.9 %collective-permute-start.14 = (bf16[4,2,128,128]{3,2,1,0:T(8,128)(2,1)S(1)}, bf16[4,2,128,128]{3,2,1,0:T(8,128)(2,1)S(1)}, u32[]{:S(2)}, u32[]{:S(2)}) collective-permute-start(bf16[4,2,128,128]{3,2,1,0:T(8,128)(2,1)S(1)} %pad_maximum_fusion.km_ref), channel_id=1, source_target_pairs={{0,64},{32,96},{64,0},{96,32},{1,65},{33,97},{65,1},{97,33},{2,66}... | collective-permute-start | bytes 786440 | tf_op jit(solution)/shard_map/ppermute | solution.py:312
  37.2 17.1 %collective-permute-start.15 = (bf16[4,2,128,128]{3,2,1,0:T(8,128)(2,1)S(1)}, bf16[4,2,128,128]{3,2,1,0:T(8,128)(2,1)S(1)}, u32[]{:S(2)}, u32[]{:S(2)}) collective-permute-start(bf16[4,2,128,128]{3,2,1,0:T(8,128)(2,1)S(1)} %pad_maximum_fusion.km_ref), channel_id=1, source_target_pairs={{0,96},{32,0},{64,32},{96,64},{1,97},{33,1},{65,33},{97,65},{2,98}... | collective-permute-start | bytes 786440 | tf_op jit(solution)/shard_map/ppermute | solution.py:312
  38.1 16.3 %collective-permute-start.7 = (bf16[4,2,128,128]{3,2,1,0:T(8,128)(2,1)S(1)}, bf16[4,2,128,128]{3,2,1,0:T(8,128)(2,1)S(1)}, u32[]{:S(2)}, u32[]{:S(2)}) collective-permute-start(bf16[4,2,128,128]{3,2,1,0:T(8,128)(2,1)S(1)} %pad_maximum_fusion.km_ref), channel_id=1, source_target_pairs={{0,2},{2,4},{4,6},{6,0},{1,3},{3,5},{5,7},{7,1},{8,10},{10,12},{12... | collective-permute-start | bytes 786440 | tf_op jit(solution)/shard_map/ppermute | solution.py:312
  39.6 18.0 %collective-permute-start.12 = (bf16[4,2,128,128]{3,2,1,0:T(8,128)(2,1)S(1)}, bf16[4,2,128,128]{3,2,1,0:T(8,128)(2,1)}, u32[]{:S(2)}, u32[]{:S(2)}) collective-permute-start(bf16[4,2,128,128]{3,2,1,0:T(8,128)(2,1)S(1)} %collective-permute-done.9.km_ref), channel_id=1, source_target_pairs={{0,1},{1,0},{2,3},{3,2},{4,5},{5,4},{6,7},{7,6},{8,9},{9,8},{10,11... | collective-permute-start | bytes 786440 | tf_op jit(solution)/shard_map/ppermute | solution.py:312
  39.6 21.9 %collective-permute-start.11 = (bf16[4,2,128,128]{3,2,1,0:T(8,128)(2,1)S(1)}, bf16[4,2,128,128]{3,2,1,0:T(8,128)(2,1)}, u32[]{:S(2)}, u32[]{:S(2)}) collective-permute-start(bf16[4,2,128,128]{3,2,1,0:T(8,128)(2,1)S(1)} %collective-permute-done.10.km_ref), channel_id=1, source_target_pairs={{0,1},{1,0},{2,3},{3,2},{4,5},{5,4},{6,7},{7,6},{8,9},{9,8},{10,11... | collective-permute-start | bytes 786440 | tf_op jit(solution)/shard_map/ppermute | solution.py:312
  49.1 16.7 %collective-permute-start.16 = (bf16[4,2,128,128]{3,2,1,0:T(8,128)(2,1)S(1)}, bf16[4,2,128,128]{3,2,1,0:T(8,128)(2,1)}, u32[]{:S(2)}, u32[]{:S(2)}) collective-permute-start(bf16[4,2,128,128]{3,2,1,0:T(8,128)(2,1)S(1)} %collective-permute-done.13.refs_0_), channel_id=1, source_target_pairs={{0,1},{1,2},{2,3},{3,4},{4,5},{5,6},{6,7},{7,0},{8,9},{9,10},{10,1... | collective-permute-start | bytes 786440 | tf_op jit(solution)/shard_map/ppermute | solution.py:312
  54.3 11.5 %collective-permute-start.17 = (bf16[4,2,128,128]{3,2,1,0:T(8,128)(2,1)S(1)}, bf16[4,2,128,128]{3,2,1,0:T(8,128)(2,1)}, u32[]{:S(2)}, u32[]{:S(2)}) collective-permute-start(bf16[4,2,128,128]{3,2,1,0:T(8,128)(2,1)S(1)} %collective-permute-done.14.refs_1_), channel_id=1, source_target_pairs={{0,1},{1,2},{2,3},{3,4},{4,5},{5,6},{6,7},{7,0},{8,9},{9,10},{10,1... | collective-permute-start | bytes 786440 | tf_op jit(solution)/shard_map/ppermute | solution.py:312
  54.4 11.4 %collective-permute-start.18 = (bf16[4,2,128,128]{3,2,1,0:T(8,128)(2,1)S(1)}, bf16[4,2,128,128]{3,2,1,0:T(8,128)(2,1)}, u32[]{:S(2)}, u32[]{:S(2)}) collective-permute-start(bf16[4,2,128,128]{3,2,1,0:T(8,128)(2,1)S(1)} %collective-permute-done.15.refs_2_), channel_id=1, source_target_pairs={{0,1},{1,2},{2,3},{3,4},{4,5},{5,6},{6,7},{7,0},{8,9},{9,10},{10,1... | collective-permute-start | bytes 786440 | tf_op jit(solution)/shard_map/ppermute | solution.py:312
  57.5 14.9 %collective-permute-start.8 = (bf16[4,2,128,128]{3,2,1,0:T(8,128)(2,1)S(1)}, bf16[4,2,128,128]{3,2,1,0:T(8,128)(2,1)S(1)}, u32[]{:S(2)}, u32[]{:S(2)}) collective-permute-start(bf16[4,2,128,128]{3,2,1,0:T(8,128)(2,1)S(1)} %collective-permute-done.7.km_ref), channel_id=1, source_target_pairs={{0,1},{1,0},{2,3},{3,2},{4,5},{5,4},{6,7},{7,6},{8,9},{9,8},{10,11... | collective-permute-start | bytes 786440 | tf_op jit(solution)/shard_map/ppermute | solution.py:312
  67.4 18.7 %collective-permute-start.29 = (bf16[3,4,2,128,128]{4,3,2,1,0:T(8,128)(2,1)S(1)}, bf16[3,4,2,128,128]{4,3,2,1,0:T(8,128)(2,1)S(1)}, u32[]{:S(2)}, u32[]{:S(2)}) collective-permute-start(bf16[3,4,2,128,128]{4,3,2,1,0:T(8,128)(2,1)S(1)} %get-tuple-element.69), channel_id=1, source_target_pairs={{0,7},{1,0},{2,1},{3,2},{4,3},{5,4},{6,5},{7,6},{8,15},{9,8},{10,9... | collective-permute-start | bytes 2359304 | tf_op jit(solution)/shard_map/ppermute | solution.py:312
  81.2 12.1 %collective-permute-start.22 = (bf16[4,2,128,128]{3,2,1,0:T(8,128)(2,1)S(1)}, bf16[4,2,128,128]{3,2,1,0:T(8,128)(2,1)S(1)}, u32[]{:S(2)}, u32[]{:S(2)}) collective-permute-start(bf16[4,2,128,128]{3,2,1,0:T(8,128)(2,1)S(1)} %get-tuple-element.61), channel_id=1, source_target_pairs={{0,1},{1,0},{2,3},{3,2},{4,5},{5,4},{6,7},{7,6},{8,9},{9,8},{10,11... | collective-permute-start | bytes 786440 | tf_op jit(solution)/shard_map/ppermute | solution.py:312
  81.8 11.6 %collective-permute-start.28 = (bf16[4,2,128,128]{3,2,1,0:T(8,128)(2,1)S(1)}, bf16[4,2,128,128]{3,2,1,0:T(8,128)(2,1)S(1)}, u32[]{:S(2)}, u32[]{:S(2)}) collective-permute-start(bf16[4,2,128,128]{3,2,1,0:T(8,128)(2,1)S(1)} %add_convert_fusion), channel_id=1, source_target_pairs={{0,6},{2,0},{4,2},{6,4},{1,7},{3,1},{5,3},{7,5},{8,14},{10,8},{12,... | collective-permute-start | bytes 786440 | tf_op jit(solution)/shard_map/ppermute | solution.py:312
  86.4 12.1 %collective-permute-start.30 = (bf16[4,2,128,128]{3,2,1,0:T(8,128)(2,1)S(1)}, bf16[4,2,128,128]{3,2,1,0:T(8,128)(2,1)S(1)}, u32[]{:S(2)}, u32[]{:S(2)}) collective-permute-start(bf16[4,2,128,128]{3,2,1,0:T(8,128)(2,1)S(1)} %get-tuple-element.70), channel_id=1, source_target_pairs={{0,96},{32,0},{64,32},{96,64},{1,97},{33,1},{65,33},{97,65},{2,98}... | collective-permute-start | bytes 786440 | tf_op jit(solution)/shard_map/ppermute | solution.py:312
  93.3 12.2 %collective-permute-start.32 = (bf16[4,2,128,128]{3,2,1,0:T(8,128)(2,1)S(1)}, bf16[4,2,128,128]{3,2,1,0:T(8,128)(2,1)S(1)}, u32[]{:S(2)}, u32[]{:S(2)}) collective-permute-start(bf16[4,2,128,128]{3,2,1,0:T(8,128)(2,1)S(1)} %get-tuple-element.72), channel_id=1, source_target_pairs={{0,32},{32,64},{64,96},{96,0},{1,33},{33,65},{65,97},{97,1},{2,34}... | collective-permute-start | bytes 786440 | tf_op jit(solution)/shard_map/ppermute | solution.py:312
  93.3 15.6 %collective-permute-start.19 = (bf16[512,128]{1,0:T(8,128)(2,1)S(1)}, bf16[512,128]{1,0:T(8,128)(2,1)S(1)}, u32[]{:S(2)}, u32[]{:S(2)}) collective-permute-start(bf16[512,128]{1,0:T(8,128)(2,1)S(1)} %get-tuple-element.57), channel_id=1, source_target_pairs={{0,24},{8,0},{16,8},{24,16},{1,25},{9,1},{17,9},{25,17},{2,26},{10... | collective-permute-start | bytes 393224 | tf_op jit(solution)/shard_map/ppermute | solution.py:312
  95.7 13.6 %collective-permute-start.20 = (bf16[512,128]{1,0:T(8,128)(2,1)S(1)}, bf16[512,128]{1,0:T(8,128)(2,1)S(1)}, u32[]{:S(2)}, u32[]{:S(2)}) collective-permute-start(bf16[512,128]{1,0:T(8,128)(2,1)S(1)} %get-tuple-element.58), channel_id=1, source_target_pairs={{0,16},{8,24},{16,0},{24,8},{1,17},{9,25},{17,1},{25,9},{2,18},{10... | collective-permute-start | bytes 393224 | tf_op jit(solution)/shard_map/ppermute | solution.py:312
  98.4 10.9 %collective-permute-start.21 = (bf16[512,128]{1,0:T(8,128)(2,1)S(1)}, bf16[512,128]{1,0:T(8,128)(2,1)S(1)}, u32[]{:S(2)}, u32[]{:S(2)}) collective-permute-start(bf16[512,128]{1,0:T(8,128)(2,1)S(1)} %get-tuple-element.59), channel_id=1, source_target_pairs={{0,8},{8,16},{16,24},{24,0},{1,9},{9,17},{17,25},{25,1},{2,10},{10... | collective-permute-start | bytes 393224 | tf_op jit(solution)/shard_map/ppermute | solution.py:312
  (21 other events, 145.3 us)

commit v4 on v3

--- a/solution.py
+++ b/solution.py
@@ -86,33 +86,37 @@
     out_ref[...] = wide_ref[...].astype(BF16)
 
 
-def prepare(len_ref, g_ref, *refs):
-    pieces, (p_ref, stat_ref, mark_ref, wide_ref) = refs[:4], refs[4:]
+def unpack(g_ref, grad_ref, wide_ref):
+    wide_ref[...] = g_ref[...].astype(F32)
+    for n in range(16):
+        g = n % GROUP
+        grad_ref[n // GROUP, g * B : (g + 1) * B, :] = wide_ref[:, n, :].astype(BF16)
+
+
+def prepare(len_ref, grad_ref, *refs):
+    pieces, (q_ref, stat_ref, mark_ref) = refs[:4], refs[4:]
     y = lax.axis_index("y")
     length = len_ref[lax.axis_index("z")]
     shard = 2 * lax.axis_index("x") + lax.axis_index("c")
     lane = lax.broadcasted_iota(jnp.int32, (GROUP, B), 1)
-    wide_ref[...] = g_ref[...].astype(F32)
-    for n in range(16):
-        p_ref[n // GROUP, ROWS + (n % GROUP) * B : ROWS + (n % GROUP + 1) * B, :] = wide_ref[:, n, :].astype(BF16)
     for d in range(4):
         i = lax.rem(y + 4 - d, 4)
-        p_ref[i, 0:ROWS, :] = pieces[d][0:ROWS, :]
+        q_ref[i] = pieces[d][0:ROWS, :]
         raw = pieces[d][2 * ROWS : QO, :].astype(F32)
         lse = raw[0:4] + raw[4:8] + raw[8:12]
         lse = jnp.where((8 * i + shard) * B + lane < length, lse * LOG2E, DEAD)
         mark_ref[i] = raw[8:16]
         for g in range(GROUP):
-            grad = p_ref[i, ROWS + g * B : ROWS + (g + 1) * B, :]
+            rows = slice(g * B, (g + 1) * B)
             out = pieces[d][ROWS + g * B : ROWS + (g + 1) * B, :]
-            prod = grad.astype(F32) * out.astype(F32)
-            stat_ref[i, 0:1, g * B : (g + 1) * B] = jnp.sum(prod.T, axis=0, keepdims=True)
-            stat_ref[i, 1:2, g * B : (g + 1) * B] = lse[g : g + 1]
-
-
-def weigh(keys, vals, p_ref, stat_ref, i, allow, prob_ref, ds_ref):
-    q = p_ref[i, 0:ROWS, :]
-    grad = p_ref[i, ROWS : 2 * ROWS, :]
+            prod = grad_ref[i, rows, :].astype(F32) * out.astype(F32)
+            stat_ref[i, 0:1, rows] = jnp.sum(prod.T, axis=0, keepdims=True)
+            stat_ref[i, 1:2, rows] = lse[g : g + 1]
+
+
+def weigh(keys, vals, q_ref, grad_ref, stat_ref, i, allow, prob_ref, ds_ref):
+    q = q_ref[i]
+    grad = grad_ref[i]
     prob = jnp.exp2(nt(keys, q) * SCALE - stat_ref[i, 1:2, :])
     if allow is not None:
         prob = jnp.where(allow, prob, 0.0)
@@ -126,7 +130,7 @@
 
 
 def make_own(dist, first, last):
-    def kernel(p_ref, stat_ref, km_ref, ko_ref, *refs):
+    def kernel(q_ref, grad_ref, stat_ref, km_ref, ko_ref, *refs):
         if not first:
             dq_in, refs = refs[0], refs[1:]
         dm_ref, do_ref, refs = refs[0], refs[1], refs[2:]
@@ -167,12 +171,12 @@
                 col = lax.broadcasted_iota(jnp.int32, (1, ROWS), 1)
                 row = jnp.where(core == 0, row, row ^ B)
                 allow = row <= core * B + col % B + jnp.where(i > m, 4 * B, 0)
-            weigh(keys, vals, p_ref, stat_ref, i, allow, prob_ref, ds_ref)
+            weigh(keys, vals, q_ref, grad_ref, stat_ref, i, allow, prob_ref, ds_ref)
 
         def after(t, prob_ref, ds_ref):
             _, i, slot = which(t)
-            dv_ref[slot] += nn(prob_ref[...], p_ref[i, ROWS : 2 * ROWS, :])
-            dk_ref[slot] += nn(ds_ref[...], p_ref[i, 0:ROWS, :])
+            dv_ref[slot] += nn(prob_ref[...], grad_ref[i])
+            dk_ref[slot] += nn(ds_ref[...], q_ref[i])
             acc_ref[i] += nn(kt_ref[slot], ds_ref[...])
 
         before(0, p0, s0)
@@ -205,11 +209,11 @@
     ] + [pltpu.VMEM((2 * B, ROWS), BF16)] * 4
     if last:
         scratch.append(pltpu.VMEM((4, HD, ROWS), F32))
-    aliases = None if first or last else {4: 2}
-    return call(kernel, (kv, kv, *dq), 0, 4 if first else 5, scratch, aliases)
-
-
-def sibling_kernel(len_ref, p_ref, stat_ref, mark_ref, dq_in, *refs):
+    aliases = None if first or last else {5: 2}
+    return call(kernel, (kv, kv, *dq), 0, 5 if first else 6, scratch, aliases)
+
+
+def sibling_kernel(len_ref, q_ref, grad_ref, stat_ref, mark_ref, dq_in, *refs):
     cur, prev, refs = refs[0:3], refs[3:6], refs[6:]
     dcur, dprev, acc_ref, k_ref, v_ref, list_ref, p0, s0, p1, s1 = refs
     thinker = lax.axis_index("z")
@@ -249,15 +253,15 @@
         row = lax.broadcasted_iota(jnp.int32, (2 * B, ROWS), 0)
         col = lax.broadcasted_iota(jnp.int32, (1, ROWS), 1) % B
         allow = (row > jnp.maximum(col, low - 1)) & (row <= jnp.minimum(col + B, top - 1))
-        weigh(k_ref[code], v_ref[code], p_ref, stat_ref, i, allow, prob_ref, ds_ref)
+        weigh(k_ref[code], v_ref[code], q_ref, grad_ref, stat_ref, i, allow, prob_ref, ds_ref)
 
     def after(t, prob_ref, ds_ref):
         code = list_ref[t]
         i, n = code // 4, code & 3
         slot = (y - i) & 3
         old = (slot + step) & 3
-        dv = nn(prob_ref[...], p_ref[i, ROWS : 2 * ROWS, :])
-        dk = nn(ds_ref[...], p_ref[i, 0:ROWS, :]) * FACTOR
+        dv = nn(prob_ref[...], grad_ref[i])
+        dk = nn(ds_ref[...], q_ref[i]) * FACTOR
         acc_ref[i] += nn(k_ref[code].T, ds_ref[...])
         for kind, grad in ((0, dk), (1, dv)):
             dprev[n, old, kind] = (dprev[n, old, kind].astype(F32) + grad[:B]).astype(BF16)
@@ -333,29 +337,29 @@
     arrived = lax.all_to_all(dealt, ("z", "y", "x", "c"), 0, 0, tiled=True)
     far = [ring(near[d], "c", 1, 2) for d in range(4)]
     prev = [ring(k, core, 1, 8) for k in cur]
-    pay, stat, mark = call(
-        prepare,
-        (shape((4, 2 * ROWS, HD), BF16), shape((4, 2, ROWS), F32), shape((4, 8, HD), F32)),
-        1,
-        5,
-        [pltpu.VMEM((128, 16, HD), F32)],
-    )(lengths, arrived, *qo)
+    rows4 = shape((4, ROWS, HD), BF16)
+    grads = call(unpack, rows4, 0, 1, [pltpu.VMEM((128, 16, HD), F32)])(arrived)
+    query, stat, mark = call(
+        prepare, (rows4, shape((4, 2, ROWS), F32), shape((4, 8, HD), F32)), 1, 5
+    )(lengths, grads, *qo)
+    rows_in = (query, grads, stat)
     mine, other, dq = {}, {}, None
-    mine[3], other[3], dq = make_own(3, True, False)(pay, stat, near[3], far[3])
-    mine[2], other[2], dq = make_own(2, False, False)(pay, stat, near[2], far[2], dq)
+    mine[3], other[3], dq = make_own(3, True, False)(*rows_in, near[3], far[3])
+    mine[2], other[2], dq = make_own(2, False, False)(*rows_in, near[2], far[2], dq)
     trio = shape((3, 4, 2, B, HD), BF16)
     scratch = [pltpu.VMEM((16, 2 * B, HD), BF16)] * 2 + [pltpu.SMEM((16,), jnp.int32)]
     scratch += [pltpu.VMEM((2 * B, ROWS), BF16)] * 4
-    sibling = call(sibling_kernel, (trio, trio, shape((4, HD, ROWS), F32)), 1, 10, scratch, {4: 2})
-    dcur, dprev, dq = sibling(lengths, pay, stat, mark, dq, *cur, *prev)
-    mine[1], other[1], dq = make_own(1, False, False)(pay, stat, near[1], far[1], dq)
-    mine[0], other[0], *dq_sent = make_own(0, False, True)(pay, stat, near[0], far[0], dq)
+    sibling = call(sibling_kernel, (trio, trio, shape((4, HD, ROWS), F32)), 1, 11, scratch, {5: 2})
+    dcur, dprev, dq = sibling(lengths, *rows_in, mark, dq, *cur, *prev)
+    mine[1], other[1], dq = make_own(1, False, False)(*rows_in, near[1], far[1], dq)
+    mine[0], other[0], *dq_sent = make_own(0, False, True)(*rows_in, near[0], far[0], dq)
     terms = [mine[0], ring(other[0], "c", 1, 2)]
-    both = {d: mine[d].astype(F32) + ring(other[d], "c", 1, 2).astype(F32) for d in dists}
-    passing = ring(both[2].astype(BF16), "x", 1, 4)
-    joined = (both[3] + passing.astype(F32)).astype(BF16)
+    moved = {d: ring(other[d], "c", 1, 2).astype(F32) for d in dists}
+    passing = ring((mine[2].astype(F32) + moved[2]).astype(BF16), "x", 1, 4)
+    joined = (mine[3].astype(F32) + moved[3] + passing.astype(F32)).astype(BF16)
+    nearest = (mine[1].astype(F32) + moved[1]).astype(BF16)
     terms.append(ring(joined, "x", 1, 4))
-    terms.append(ring(both[1].astype(BF16), "x", -1, 4))
+    terms.append(ring(nearest, "x", -1, 4))
     late = ring(dprev, core, -1, 8)
     merged = call(merge, (kv,) * 3, 0, 2)(dcur, late)
     terms += [ring(merged[d - 1], "z", -d, 4) for d in dists]

time: 116 us -> 117 us (level)
    pallas_call x6 -> x7, Pallas kernels: 19 us -> 19.2 us  [the longest x1 4.97 us: step(): make_own(0, False, True)(*rows_in, near[0], far[0], dq)]
where the time goes in v4:
time: 117 us; the launch traced here: 116 us
  starting transfers between devices  55.4 us (47%)
  waiting for transfers between devices  31 us (26%)
  Pallas kernels  24.4 us (21%)
  local copies, waits for them, and re-layouts  4.21 us (4%)
    ppermute x36, starting transfers between devices, ring(): lax.ppermute(x, axis, [(j, (j + step) % count) for j in range(count)])  48 us
    ppermute x36, waiting for transfers between devices, ring(): lax.ppermute(x, axis, [(j, (j + step) % count) for j in range(count)])  31 us
    all_to_all x1, starting transfers between devices, step(): arrived = lax.all_to_all(dealt, ('z', 'y', 'x', 'c'), 0, 0, tiled=True)  7.47 us
    pallas_call x1, Pallas kernels, step(): make_own(0, False, True)(*rows_in, near[0], far[0], dq)  4.97 us
    unnamed x16, local copies, waits for them, and re-layouts  4.21 us
    pallas_call x1, Pallas kernels, step(): mine[3], other[3], dq = make_own(3, True, False)(*rows_in, near[3], far[3])  3.77 us
    pallas_call x1, Pallas kernels, step(): make_own(2, False, False)(*rows_in, near[2], far[2], dq)  3.73 us
    pallas_call x1, Pallas kernels, step(): make_own(1, False, False)(*rows_in, near[1], far[1], dq)  2.77 us
  transfers between devices with their start and end apart: 37, of which 10 were waited for; matrix products, arithmetic and copies ran while one was open for 0% of the time, Pallas kernels for 20%

profile of v4, /device:TPU:0, one launch (start us, length us, event | category | flops | bytes accessed | tf_op | source)
XLA Modules:
  0.0 116.2 jit_solution(3260698991210791722)
XLA Ops:
  2.6 3.2 %collective-permute-start.5 = (bf16[2,128,128]{2,1,0:T(8,128)(2,1)S(1)}, bf16[2,128,128]{2,1,0:T(8,128)(2,1)S(1)}, u32[]{:S(2)}, u32[]{:S(2)}) collective-permute-start(bf16[2,128,128]{2,1,0:T(8,128)(2,1)S(1)} %get-tuple-element.50), channel_id=1, source_target_pairs={{0,24},{8,0},{16,8},{24,16},{1,25},{9,1},{17,9},{25,17},{2,26},{10... | collective-permute-start | bytes 196616 | tf_op jit(solution)/shard_map/ppermute | solution.py:316
  5.8 2.2 %collective-permute-start.4 = (bf16[2,128,128]{2,1,0:T(8,128)(2,1)S(1)}, bf16[2,128,128]{2,1,0:T(8,128)(2,1)S(1)}, u32[]{:S(2)}, u32[]{:S(2)}) collective-permute-start(bf16[2,128,128]{2,1,0:T(8,128)(2,1)S(1)} %get-tuple-element.49), channel_id=1, source_target_pairs={{0,16},{8,24},{16,0},{24,8},{1,17},{9,25},{17,1},{25,9},{2,18},{10... | collective-permute-start | bytes 196616 | tf_op jit(solution)/shard_map/ppermute | solution.py:316
  8.0 4.1 %collective-permute-done.3 = bf16[2,128,128]{2,1,0:T(8,128)(2,1)S(1)} collective-permute-done((bf16[2,128,128]{2,1,0:T(8,128)(2,1)S(1)}, bf16[2,128,128]{2,1,0:T(8,128)(2,1)S(1)}, u32[]{:S(2)}, u32[]{:S(2)}) %collective-permute-start.3) | collective-permute-done | bytes 65568 | tf_op jit(solution)/shard_map/ppermute | solution.py:316
  12.1 2.8 %collective-permute-start.9 = (bf16[4,2,128,128]{3,2,1,0:T(8,128)(2,1)S(1)}, bf16[4,2,128,128]{3,2,1,0:T(8,128)(2,1)S(1)}, u32[]{:S(2)}, u32[]{:S(2)}) collective-permute-start(bf16[4,2,128,128]{3,2,1,0:T(8,128)(2,1)S(1)} %pad_maximum_fusion.km_ref), channel_id=1, source_target_pairs={{0,6},{2,0},{4,2},{6,4},{1,7},{3,1},{5,3},{7,5},{8,14},{10,8},{12,... | collective-permute-start | bytes 786440 | tf_op jit(solution)/shard_map/ppermute | solution.py:316
  18.3 4.1 %collective-permute-start.1 = (bf16[1040,128]{1,0:T(8,128)(2,1)}, bf16[1040,128]{1,0:T(8,128)(2,1)S(1)}, u32[]{:S(2)}, u32[]{:S(2)}) collective-permute-start(bf16[1040,128]{1,0:T(8,128)(2,1)} %get-tuple-element.43), channel_id=1, source_target_pairs={{0,16},{8,24},{16,0},{24,8},{1,17},{9,25},{17,1},{25,9},{2,18},{10... | collective-permute-start | bytes 798728 | tf_op jit(solution)/shard_map/ppermute | solution.py:316
  22.6 1.9 %collective-permute-start.13 = (bf16[4,2,128,128]{3,2,1,0:T(8,128)(2,1)S(1)}, bf16[4,2,128,128]{3,2,1,0:T(8,128)(2,1)S(1)}, u32[]{:S(2)}, u32[]{:S(2)}) collective-permute-start(bf16[4,2,128,128]{3,2,1,0:T(8,128)(2,1)S(1)} %pad_maximum_fusion.km_ref), channel_id=1, source_target_pairs={{0,32},{32,64},{64,96},{96,0},{1,33},{33,65},{65,97},{97,1},{2,34}... | collective-permute-start | bytes 786440 | tf_op jit(solution)/shard_map/ppermute | solution.py:316
  26.7 7.5 %all-to-all-start = ((bf16[128,16,128]{2,1,0:T(8,128)(2,1)}), bf16[128,16,128]{2,1,0:T(8,128)(2,1)S(1)}, u32[]{:S(2)}, u32[]{:S(2)}) async-start(bf16[128,16,128]{2,1,0:T(8,128)(2,1)} %shard_map.103), calls=%async_computation | async-start | bytes 1048576 | tf_op jit(solution)/shard_map/all_to_all | solution.py:337
  34.2 2.9 %collective-permute-start.14 = (bf16[4,2,128,128]{3,2,1,0:T(8,128)(2,1)S(1)}, bf16[4,2,128,128]{3,2,1,0:T(8,128)(2,1)S(1)}, u32[]{:S(2)}, u32[]{:S(2)}) collective-permute-start(bf16[4,2,128,128]{3,2,1,0:T(8,128)(2,1)S(1)} %pad_maximum_fusion.km_ref), channel_id=1, source_target_pairs={{0,64},{32,96},{64,0},{96,32},{1,65},{33,97},{65,1},{97,33},{2,66}... | collective-permute-start | bytes 786440 | tf_op jit(solution)/shard_map/ppermute | solution.py:316
  40.1 9.0 %collective-permute-done.14.refs_1_ = bf16[4,2,128,128]{3,2,1,0:T(8,128)(2,1)S(1)} collective-permute-done((bf16[4,2,128,128]{3,2,1,0:T(8,128)(2,1)S(1)}, bf16[4,2,128,128]{3,2,1,0:T(8,128)(2,1)S(1)}, u32[]{:S(2)}, u32[]{:S(2)}) %collective-permute-start.14) | collective-permute-done | bytes 262176 | tf_op jit(solution)/shard_map/ppermute | solution.py:316
  49.1 5.1 %collective-permute-done.15.refs_2_ = bf16[4,2,128,128]{3,2,1,0:T(8,128)(2,1)S(1)} collective-permute-done((bf16[4,2,128,128]{3,2,1,0:T(8,128)(2,1)S(1)}, bf16[4,2,128,128]{3,2,1,0:T(8,128)(2,1)S(1)}, u32[]{:S(2)}, u32[]{:S(2)}) %collective-permute-start.15) | collective-permute-done | bytes 262176 | tf_op jit(solution)/shard_map/ppermute | solution.py:316
  58.7 3.8 %shard_map.108 = (bf16[4,2,128,128]{3,2,1,0:T(8,128)(2,1)S(1)}, bf16[4,2,128,128]{3,2,1,0:T(8,128)(2,1)S(1)}, f32[4,128,512]{2,1,0:T(8,128)S(1)}) custom-call(bf16[4,512,128]{2,1,0:T(8,128)(2,1)S(1)} %get-tuple-element.45.q_ref, bf16[4,512,128]{2,1,0:T(8,128)(2,1)S(1)} %shard_map.104.grad_ref, f32[4,2,512]{2,1,0:T(2,128)S(1)} %get-tuple-element.46.stat_ref, ...), custom_call_target="tpu_custom_call" | custom-call | tf_op jit(solution)/shard_map/pallas_call | solution.py:347
  62.5 3.7 %shard_map.109 = (bf16[4,2,128,128]{3,2,1,0:T(8,128)(2,1)S(1)}, bf16[4,2,128,128]{3,2,1,0:T(8,128)(2,1)S(1)}, f32[4,128,512]{2,1,0:T(8,128)S(1)}) custom-call(bf16[4,512,128]{2,1,0:T(8,128)(2,1)S(1)} %get-tuple-element.45.q_ref, bf16[4,512,128]{2,1,0:T(8,128)(2,1)S(1)} %shard_map.104.grad_ref, ...), custom_call_target="tpu_custom_call", output_to_operand_aliasing={{2}: (5, {})} | custom-call | tf_op jit(solution)/shard_map/pallas_call | solution.py:348
  66.8 1.6 %shard_map.110 = (bf16[3,4,2,128,128]{4,3,2,1,0:T(8,128)(2,1)S(1)}, bf16[3,4,2,128,128]{4,3,2,1,0:T(8,128)(2,1)S(1)}, f32[4,128,512]{2,1,0:T(8,128)S(1)}) custom-call(s32[4]{0:T(128)S(1)} %copy-done.6, bf16[4,512,128]{2,1,0:T(8,128)(2,1)S(1)} %get-tuple-element.45.q_ref, ...), custom_call_target="tpu_custom_call", output_to_operand_aliasing={{2}: (5, {})} | custom-call | tf_op jit(solution)/shard_map/pallas_call | solution.py:353
  68.4 5.0 %collective-permute-start.29 = (bf16[3,4,2,128,128]{4,3,2,1,0:T(8,128)(2,1)S(1)}, bf16[3,4,2,128,128]{4,3,2,1,0:T(8,128)(2,1)S(1)}, u32[]{:S(2)}, u32[]{:S(2)}) collective-permute-start(bf16[3,4,2,128,128]{4,3,2,1,0:T(8,128)(2,1)S(1)} %get-tuple-element.69), channel_id=1, source_target_pairs={{0,7},{1,0},{2,1},{3,2},{4,3},{5,4},{6,5},{7,6},{8,15},{9,8},{10,9... | collective-permute-start | bytes 2359304 | tf_op jit(solution)/shard_map/ppermute | solution.py:316
  73.4 2.8 %shard_map.111 = (bf16[4,2,128,128]{3,2,1,0:T(8,128)(2,1)S(1)}, bf16[4,2,128,128]{3,2,1,0:T(8,128)(2,1)S(1)}, f32[4,128,512]{2,1,0:T(8,128)S(1)}) custom-call(bf16[4,512,128]{2,1,0:T(8,128)(2,1)S(1)} %get-tuple-element.45.q_ref, bf16[4,512,128]{2,1,0:T(8,128)(2,1)S(1)} %shard_map.104.grad_ref, ...), custom_call_target="tpu_custom_call", output_to_operand_aliasing={{2}: (5, {})} | custom-call | tf_op jit(solution)/shard_map/pallas_call | solution.py:354
  77.1 5.0 %shard_map.112 = (bf16[4,2,128,128]{3,2,1,0:T(8,128)(2,1)S(1)}, bf16[4,2,128,128]{3,2,1,0:T(8,128)(2,1)S(1)}, bf16[512,128]{1,0:T(8,128)(2,1)S(1)}, bf16[512,128...) custom-call(bf16[4,512,128]{2,1,0:T(8,128)(2,1)S(1)} %get-tuple-element.45.q_ref, ...), custom_call_target="tpu_custom_call" | custom-call | tf_op jit(solution)/shard_map/pallas_call | solution.py:355
  82.6 3.0 %collective-permute-start.28 = (bf16[4,2,128,128]{3,2,1,0:T(8,128)(2,1)S(1)}, bf16[4,2,128,128]{3,2,1,0:T(8,128)(2,1)S(1)}, u32[]{:S(2)}, u32[]{:S(2)}) collective-permute-start(bf16[4,2,128,128]{3,2,1,0:T(8,128)(2,1)S(1)} %add_convert_fusion), channel_id=1, source_target_pairs={{0,6},{2,0},{4,2},{6,4},{1,7},{3,1},{5,3},{7,5},{8,14},{10,8},{12,... | collective-permute-start | bytes 786440 | tf_op jit(solution)/shard_map/ppermute | solution.py:316
  87.3 4.6 %collective-permute-start.30 = (bf16[4,2,128,128]{3,2,1,0:T(8,128)(2,1)S(1)}, bf16[4,2,128,128]{3,2,1,0:T(8,128)(2,1)S(1)}, u32[]{:S(2)}, u32[]{:S(2)}) collective-permute-start(bf16[4,2,128,128]{3,2,1,0:T(8,128)(2,1)S(1)} %get-tuple-element.70), channel_id=1, source_target_pairs={{0,96},{32,0},{64,32},{96,64},{1,97},{33,1},{65,33},{97,65},{2,98}... | collective-permute-start | bytes 786440 | tf_op jit(solution)/shard_map/ppermute | solution.py:316
  91.8 2.4 %collective-permute-start.31 = (bf16[4,2,128,128]{3,2,1,0:T(8,128)(2,1)S(1)}, bf16[4,2,128,128]{3,2,1,0:T(8,128)(2,1)S(1)}, u32[]{:S(2)}, u32[]{:S(2)}) collective-permute-start(bf16[4,2,128,128]{3,2,1,0:T(8,128)(2,1)S(1)} %get-tuple-element.71), channel_id=1, source_target_pairs={{0,64},{32,96},{64,0},{96,32},{1,65},{33,97},{65,1},{97,33},{2,66}... | collective-permute-start | bytes 786440 | tf_op jit(solution)/shard_map/ppermute | solution.py:316
  94.2 2.4 %collective-permute-start.19 = (bf16[512,128]{1,0:T(8,128)(2,1)S(1)}, bf16[512,128]{1,0:T(8,128)(2,1)S(1)}, u32[]{:S(2)}, u32[]{:S(2)}) collective-permute-start(bf16[512,128]{1,0:T(8,128)(2,1)S(1)} %get-tuple-element.57), channel_id=1, source_target_pairs={{0,24},{8,0},{16,8},{24,16},{1,25},{9,1},{17,9},{25,17},{2,26},{10... | collective-permute-start | bytes 393224 | tf_op jit(solution)/shard_map/ppermute | solution.py:316
  100.4 2.2 %collective-permute-done.31.refs_5_ = bf16[4,2,128,128]{3,2,1,0:T(8,128)(2,1)S(1)} collective-permute-done((bf16[4,2,128,128]{3,2,1,0:T(8,128)(2,1)S(1)}, bf16[4,2,128,128]{3,2,1,0:T(8,128)(2,1)S(1)}, u32[]{:S(2)}, u32[]{:S(2)}) %collective-permute-start.31) | collective-permute-done | bytes 262176 | tf_op jit(solution)/shard_map/ppermute | solution.py:316
  102.6 3.9 %collective-permute-done.32.refs_6_ = bf16[4,2,128,128]{3,2,1,0:T(8,128)(2,1)S(1)} collective-permute-done((bf16[4,2,128,128]{3,2,1,0:T(8,128)(2,1)S(1)}, bf16[4,2,128,128]{3,2,1,0:T(8,128)(2,1)S(1)}, u32[]{:S(2)}, u32[]{:S(2)}) %collective-permute-start.32) | collective-permute-done | bytes 262176 | tf_op jit(solution)/shard_map/ppermute | solution.py:316
  106.7 2.1 %collective-permute-start.33 = (bf16[2,128,128]{2,1,0:T(8,128)(2,1)S(1)}, bf16[2,128,128]{2,1,0:T(8,128)(2,1)S(1)}, u32[]{:S(2)}, u32[]{:S(2)}) collective-permute-start(bf16[2,128,128]{2,1,0:T(8,128)(2,1)S(1)} %get-tuple-element.74), channel_id=1, source_target_pairs={{0,24},{8,0},{16,8},{24,16},{1,25},{9,1},{17,9},{25,17},{2,26},{10... | collective-permute-start | bytes 196616 | tf_op jit(solution)/shard_map/ppermute | solution.py:316
  111.8 2.9 %collective-permute-done.34.d2 = bf16[2,128,128]{2,1,0:T(8,128)(2,1)S(1)} collective-permute-done((bf16[2,128,128]{2,1,0:T(8,128)(2,1)S(1)}, bf16[2,128,128]{2,1,0:T(8,128)(2,1)S(1)}, u32[]{:S(2)}, u32[]{:S(2)}) %collective-permute-start.34) | collective-permute-done | bytes 65568 | tf_op jit(solution)/shard_map/ppermute | solution.py:316
  (84 shorter events, 27.2 us)
Async XLA Ops:
  12.1 12.4 %collective-permute-start.9 = (bf16[4,2,128,128]{3,2,1,0:T(8,128)(2,1)S(1)}, bf16[4,2,128,128]{3,2,1,0:T(8,128)(2,1)S(1)}, u32[]{:S(2)}, u32[]{:S(2)}) collective-permute-start(bf16[4,2,128,128]{3,2,1,0:T(8,128)(2,1)S(1)} %pad_maximum_fusion.km_ref), channel_id=1, source_target_pairs={{0,6},{2,0},{4,2},{6,4},{1,7},{3,1},{5,3},{7,5},{8,14},{10,8},{12,... | collective-permute-start | bytes 786440 | tf_op jit(solution)/shard_map/ppermute | solution.py:316
  18.2 16.0 %collective-permute-start = (bf16[1040,128]{1,0:T(8,128)(2,1)S(1)}, bf16[1040,128]{1,0:T(8,128)(2,1)S(1)}, u32[]{:S(2)}, u32[]{:S(2)}) collective-permute-start(bf16[1040,128]{1,0:T(8,128)(2,1)S(1)} %get-tuple-element.42), channel_id=1, source_target_pairs={{0,8},{8,16},{16,24},{24,0},{1,9},{9,17},{17,25},{25,1},{2,10},{10... | collective-permute-start | bytes 798728 | tf_op jit(solution)/shard_map/ppermute | solution.py:316
  18.3 18.8 %collective-permute-start.1 = (bf16[1040,128]{1,0:T(8,128)(2,1)}, bf16[1040,128]{1,0:T(8,128)(2,1)S(1)}, u32[]{:S(2)}, u32[]{:S(2)}) collective-permute-start(bf16[1040,128]{1,0:T(8,128)(2,1)} %get-tuple-element.43), channel_id=1, source_target_pairs={{0,16},{8,24},{16,0},{24,8},{1,17},{9,25},{17,1},{25,9},{2,18},{10... | collective-permute-start | bytes 798728 | tf_op jit(solution)/shard_map/ppermute | solution.py:316
  22.4 15.6 %collective-permute-start.2 = (bf16[1040,128]{1,0:T(8,128)(2,1)}, bf16[1040,128]{1,0:T(8,128)(2,1)S(1)}, u32[]{:S(2)}, u32[]{:S(2)}) collective-permute-start(bf16[1040,128]{1,0:T(8,128)(2,1)} %get-tuple-element.44), channel_id=1, source_target_pairs={{0,24},{8,0},{16,8},{24,16},{1,25},{9,1},{17,9},{25,17},{2,26},{10... | collective-permute-start | bytes 798728 | tf_op jit(solution)/shard_map/ppermute | solution.py:316
  22.6 17.0 %collective-permute-start.13 = (bf16[4,2,128,128]{3,2,1,0:T(8,128)(2,1)S(1)}, bf16[4,2,128,128]{3,2,1,0:T(8,128)(2,1)S(1)}, u32[]{:S(2)}, u32[]{:S(2)}) collective-permute-start(bf16[4,2,128,128]{3,2,1,0:T(8,128)(2,1)S(1)} %pad_maximum_fusion.km_ref), channel_id=1, source_target_pairs={{0,32},{32,64},{64,96},{96,0},{1,33},{33,65},{65,97},{97,1},{2,34}... | collective-permute-start | bytes 786440 | tf_op jit(solution)/shard_map/ppermute | solution.py:316
  24.5 15.1 %collective-permute-start.10 = (bf16[4,2,128,128]{3,2,1,0:T(8,128)(2,1)S(1)}, bf16[4,2,128,128]{3,2,1,0:T(8,128)(2,1)S(1)}, u32[]{:S(2)}, u32[]{:S(2)}) collective-permute-start(bf16[4,2,128,128]{3,2,1,0:T(8,128)(2,1)S(1)} %collective-permute-done.9.km_ref), channel_id=1, source_target_pairs={{0,6},{2,0},{4,2},{6,4},{1,7},{3,1},{5,3},{7,5},{8,14},{10,8},{12,... | collective-permute-start | bytes 786440 | tf_op jit(solution)/shard_map/ppermute | solution.py:316
  26.7 28.8 %all-to-all-start = ((bf16[128,16,128]{2,1,0:T(8,128)(2,1)}), bf16[128,16,128]{2,1,0:T(8,128)(2,1)S(1)}, u32[]{:S(2)}, u32[]{:S(2)}) async-start(bf16[128,16,128]{2,1,0:T(8,128)(2,1)} %shard_map.103), calls=%async_computation | async-start | bytes 1048576 | tf_op jit(solution)/shard_map/all_to_all | solution.py:337
  34.2 14.9 %collective-permute-start.14 = (bf16[4,2,128,128]{3,2,1,0:T(8,128)(2,1)S(1)}, bf16[4,2,128,128]{3,2,1,0:T(8,128)(2,1)S(1)}, u32[]{:S(2)}, u32[]{:S(2)}) collective-permute-start(bf16[4,2,128,128]{3,2,1,0:T(8,128)(2,1)S(1)} %pad_maximum_fusion.km_ref), channel_id=1, source_target_pairs={{0,64},{32,96},{64,0},{96,32},{1,65},{33,97},{65,1},{97,33},{2,66}... | collective-permute-start | bytes 786440 | tf_op jit(solution)/shard_map/ppermute | solution.py:316
  37.2 17.1 %collective-permute-start.15 = (bf16[4,2,128,128]{3,2,1,0:T(8,128)(2,1)S(1)}, bf16[4,2,128,128]{3,2,1,0:T(8,128)(2,1)S(1)}, u32[]{:S(2)}, u32[]{:S(2)}) collective-permute-start(bf16[4,2,128,128]{3,2,1,0:T(8,128)(2,1)S(1)} %pad_maximum_fusion.km_ref), channel_id=1, source_target_pairs={{0,96},{32,0},{64,32},{96,64},{1,97},{33,1},{65,33},{97,65},{2,98}... | collective-permute-start | bytes 786440 | tf_op jit(solution)/shard_map/ppermute | solution.py:316
  38.1 16.3 %collective-permute-start.7 = (bf16[4,2,128,128]{3,2,1,0:T(8,128)(2,1)S(1)}, bf16[4,2,128,128]{3,2,1,0:T(8,128)(2,1)S(1)}, u32[]{:S(2)}, u32[]{:S(2)}) collective-permute-start(bf16[4,2,128,128]{3,2,1,0:T(8,128)(2,1)S(1)} %pad_maximum_fusion.km_ref), channel_id=1, source_target_pairs={{0,2},{2,4},{4,6},{6,0},{1,3},{3,5},{5,7},{7,1},{8,10},{10,12},{12... | collective-permute-start | bytes 786440 | tf_op jit(solution)/shard_map/ppermute | solution.py:316
  39.6 19.0 %collective-permute-start.12 = (bf16[4,2,128,128]{3,2,1,0:T(8,128)(2,1)S(1)}, bf16[4,2,128,128]{3,2,1,0:T(8,128)(2,1)}, u32[]{:S(2)}, u32[]{:S(2)}) collective-permute-start(bf16[4,2,128,128]{3,2,1,0:T(8,128)(2,1)S(1)} %collective-permute-done.9.km_ref), channel_id=1, source_target_pairs={{0,1},{1,0},{2,3},{3,2},{4,5},{5,4},{6,7},{7,6},{8,9},{9,8},{10,11... | collective-permute-start | bytes 786440 | tf_op jit(solution)/shard_map/ppermute | solution.py:316
  39.6 22.9 %collective-permute-start.11 = (bf16[4,2,128,128]{3,2,1,0:T(8,128)(2,1)S(1)}, bf16[4,2,128,128]{3,2,1,0:T(8,128)(2,1)}, u32[]{:S(2)}, u32[]{:S(2)}) collective-permute-start(bf16[4,2,128,128]{3,2,1,0:T(8,128)(2,1)S(1)} %collective-permute-done.10.km_ref), channel_id=1, source_target_pairs={{0,1},{1,0},{2,3},{3,2},{4,5},{5,4},{6,7},{7,6},{8,9},{9,8},{10,11... | collective-permute-start | bytes 786440 | tf_op jit(solution)/shard_map/ppermute | solution.py:316
  49.1 17.6 %collective-permute-start.16 = (bf16[4,2,128,128]{3,2,1,0:T(8,128)(2,1)S(1)}, bf16[4,2,128,128]{3,2,1,0:T(8,128)(2,1)}, u32[]{:S(2)}, u32[]{:S(2)}) collective-permute-start(bf16[4,2,128,128]{3,2,1,0:T(8,128)(2,1)S(1)} %collective-permute-done.13.refs_0_), channel_id=1, source_target_pairs={{0,1},{1,2},{2,3},{3,4},{4,5},{5,6},{6,7},{7,0},{8,9},{9,10},{10,1... | collective-permute-start | bytes 786440 | tf_op jit(solution)/shard_map/ppermute | solution.py:316
  54.3 12.5 %collective-permute-start.17 = (bf16[4,2,128,128]{3,2,1,0:T(8,128)(2,1)S(1)}, bf16[4,2,128,128]{3,2,1,0:T(8,128)(2,1)}, u32[]{:S(2)}, u32[]{:S(2)}) collective-permute-start(bf16[4,2,128,128]{3,2,1,0:T(8,128)(2,1)S(1)} %collective-permute-done.14.refs_1_), channel_id=1, source_target_pairs={{0,1},{1,2},{2,3},{3,4},{4,5},{5,6},{6,7},{7,0},{8,9},{9,10},{10,1... | collective-permute-start | bytes 786440 | tf_op jit(solution)/shard_map/ppermute | solution.py:316
  54.4 12.4 %collective-permute-start.18 = (bf16[4,2,128,128]{3,2,1,0:T(8,128)(2,1)S(1)}, bf16[4,2,128,128]{3,2,1,0:T(8,128)(2,1)}, u32[]{:S(2)}, u32[]{:S(2)}) collective-permute-start(bf16[4,2,128,128]{3,2,1,0:T(8,128)(2,1)S(1)} %collective-permute-done.15.refs_2_), channel_id=1, source_target_pairs={{0,1},{1,2},{2,3},{3,4},{4,5},{5,6},{6,7},{7,0},{8,9},{9,10},{10,1... | collective-permute-start | bytes 786440 | tf_op jit(solution)/shard_map/ppermute | solution.py:316
  58.5 14.9 %collective-permute-start.8 = (bf16[4,2,128,128]{3,2,1,0:T(8,128)(2,1)S(1)}, bf16[4,2,128,128]{3,2,1,0:T(8,128)(2,1)S(1)}, u32[]{:S(2)}, u32[]{:S(2)}) collective-permute-start(bf16[4,2,128,128]{3,2,1,0:T(8,128)(2,1)S(1)} %collective-permute-done.7.km_ref), channel_id=1, source_target_pairs={{0,1},{1,0},{2,3},{3,2},{4,5},{5,4},{6,7},{7,6},{8,9},{9,8},{10,11... | collective-permute-start | bytes 786440 | tf_op jit(solution)/shard_map/ppermute | solution.py:316
  68.4 18.7 %collective-permute-start.29 = (bf16[3,4,2,128,128]{4,3,2,1,0:T(8,128)(2,1)S(1)}, bf16[3,4,2,128,128]{4,3,2,1,0:T(8,128)(2,1)S(1)}, u32[]{:S(2)}, u32[]{:S(2)}) collective-permute-start(bf16[3,4,2,128,128]{4,3,2,1,0:T(8,128)(2,1)S(1)} %get-tuple-element.69), channel_id=1, source_target_pairs={{0,7},{1,0},{2,1},{3,2},{4,3},{5,4},{6,5},{7,6},{8,15},{9,8},{10,9... | collective-permute-start | bytes 2359304 | tf_op jit(solution)/shard_map/ppermute | solution.py:316
  82.0 12.2 %collective-permute-start.22 = (bf16[4,2,128,128]{3,2,1,0:T(8,128)(2,1)S(1)}, bf16[4,2,128,128]{3,2,1,0:T(8,128)(2,1)S(1)}, u32[]{:S(2)}, u32[]{:S(2)}) collective-permute-start(bf16[4,2,128,128]{3,2,1,0:T(8,128)(2,1)S(1)} %get-tuple-element.61), channel_id=1, source_target_pairs={{0,1},{1,0},{2,3},{3,2},{4,5},{5,4},{6,7},{7,6},{8,9},{9,8},{10,11... | collective-permute-start | bytes 786440 | tf_op jit(solution)/shard_map/ppermute | solution.py:316
  82.6 11.6 %collective-permute-start.28 = (bf16[4,2,128,128]{3,2,1,0:T(8,128)(2,1)S(1)}, bf16[4,2,128,128]{3,2,1,0:T(8,128)(2,1)S(1)}, u32[]{:S(2)}, u32[]{:S(2)}) collective-permute-start(bf16[4,2,128,128]{3,2,1,0:T(8,128)(2,1)S(1)} %add_convert_fusion), channel_id=1, source_target_pairs={{0,6},{2,0},{4,2},{6,4},{1,7},{3,1},{5,3},{7,5},{8,14},{10,8},{12,... | collective-permute-start | bytes 786440 | tf_op jit(solution)/shard_map/ppermute | solution.py:316
  87.3 12.0 %collective-permute-start.30 = (bf16[4,2,128,128]{3,2,1,0:T(8,128)(2,1)S(1)}, bf16[4,2,128,128]{3,2,1,0:T(8,128)(2,1)S(1)}, u32[]{:S(2)}, u32[]{:S(2)}) collective-permute-start(bf16[4,2,128,128]{3,2,1,0:T(8,128)(2,1)S(1)} %get-tuple-element.70), channel_id=1, source_target_pairs={{0,96},{32,0},{64,32},{96,64},{1,97},{33,1},{65,33},{97,65},{2,98}... | collective-permute-start | bytes 786440 | tf_op jit(solution)/shard_map/ppermute | solution.py:316
  94.2 12.2 %collective-permute-start.32 = (bf16[4,2,128,128]{3,2,1,0:T(8,128)(2,1)S(1)}, bf16[4,2,128,128]{3,2,1,0:T(8,128)(2,1)S(1)}, u32[]{:S(2)}, u32[]{:S(2)}) collective-permute-start(bf16[4,2,128,128]{3,2,1,0:T(8,128)(2,1)S(1)} %get-tuple-element.72), channel_id=1, source_target_pairs={{0,32},{32,64},{64,96},{96,0},{1,33},{33,65},{65,97},{97,1},{2,34}... | collective-permute-start | bytes 786440 | tf_op jit(solution)/shard_map/ppermute | solution.py:316
  94.2 15.6 %collective-permute-start.19 = (bf16[512,128]{1,0:T(8,128)(2,1)S(1)}, bf16[512,128]{1,0:T(8,128)(2,1)S(1)}, u32[]{:S(2)}, u32[]{:S(2)}) collective-permute-start(bf16[512,128]{1,0:T(8,128)(2,1)S(1)} %get-tuple-element.57), channel_id=1, source_target_pairs={{0,24},{8,0},{16,8},{24,16},{1,25},{9,1},{17,9},{25,17},{2,26},{10... | collective-permute-start | bytes 393224 | tf_op jit(solution)/shard_map/ppermute | solution.py:316
  96.6 13.7 %collective-permute-start.20 = (bf16[512,128]{1,0:T(8,128)(2,1)S(1)}, bf16[512,128]{1,0:T(8,128)(2,1)S(1)}, u32[]{:S(2)}, u32[]{:S(2)}) collective-permute-start(bf16[512,128]{1,0:T(8,128)(2,1)S(1)} %get-tuple-element.58), channel_id=1, source_target_pairs={{0,16},{8,24},{16,0},{24,8},{1,17},{9,25},{17,1},{25,9},{2,18},{10... | collective-permute-start | bytes 393224 | tf_op jit(solution)/shard_map/ppermute | solution.py:316
  99.3 11.0 %collective-permute-start.21 = (bf16[512,128]{1,0:T(8,128)(2,1)S(1)}, bf16[512,128]{1,0:T(8,128)(2,1)S(1)}, u32[]{:S(2)}, u32[]{:S(2)}) collective-permute-start(bf16[512,128]{1,0:T(8,128)(2,1)S(1)} %get-tuple-element.59), channel_id=1, source_target_pairs={{0,8},{8,16},{16,24},{24,0},{1,9},{9,17},{17,25},{25,1},{2,10},{10... | collective-permute-start | bytes 393224 | tf_op jit(solution)/shard_map/ppermute | solution.py:316
  (21 other events, 124.5 us)

commit v5 on v4

--- a/solution.py
+++ b/solution.py
@@ -76,13 +76,12 @@
 
 
 def deal(up_ref, out_ref, wide_ref):
-    for t in range(4):
-        for c in range(4):
-            for i in range(4):
-                for g in range(GROUP):
-                    cols = slice((c * GROUP + g) * HD, (c * GROUP + g + 1) * HD)
-                    block = up_ref[(t * 4 + i) * 8 : (t * 4 + i + 1) * 8, cols]
-                    wide_ref[(t * 4 + c) * 8 : (t * 4 + c + 1) * 8, i * GROUP + g, :] = block.astype(F32)
+    for c in range(4):
+        for i in range(4):
+            for g in range(GROUP):
+                cols = slice((c * GROUP + g) * HD, (c * GROUP + g + 1) * HD)
+                block = up_ref[i * 8 : (i + 1) * 8, cols]
+                wide_ref[c * 8 : (c + 1) * 8, i * GROUP + g, :] = block.astype(F32)
     out_ref[...] = wide_ref[...].astype(BF16)
 
 
@@ -331,9 +330,15 @@
     near = {0: kv_own, 1: ring(kv_own, "x", 1, 4), 3: ring(kv_own, "x", -1, 4)}
     near[2] = ring(near[3], "x", -1, 4)
     cur = [ring(kv_own, "z", d, 4) for d in dists]
-    dealt = call(deal, shape((128, 16, HD), BF16), 0, 1, [pltpu.VMEM((128, 16, HD), F32)])(
-        upstream.reshape(128, 2048)
-    )
+    dealt = pl.pallas_call(
+        deal,
+        grid=(4,),
+        out_shape=shape((128, 16, HD), BF16),
+        in_specs=[pl.BlockSpec((32, 2048), lambda t: (t, 0))],
+        out_specs=pl.BlockSpec((32, 16, HD), lambda t: (t, 0, 0)),
+        scratch_shapes=[pltpu.VMEM((32, 16, HD), F32)],
+        name="deal",
+    )(upstream.reshape(128, 2048))
     arrived = lax.all_to_all(dealt, ("z", "y", "x", "c"), 0, 0, tiled=True)
     far = [ring(near[d], "c", 1, 2) for d in range(4)]
     prev = [ring(k, core, 1, 8) for k in cur]

time: 117 us -> 119 us (1.017)
  Pallas kernels: 24.4 us -> 26.4 us
    pallas_call x1, Pallas kernels: 1.42 us -> 3.45 us  [step(): pl.pallas_call(deal, grid=(4,), out_shape=shape((128, 16, HD), BF16), in_...]
    unnamed x16 -> x14, local copies, waits for them, and re-layouts: 4.21 us -> 4.21 us
  transfers between devices with their start and end apart: 37 -> 37, of which waited for: 10 -> 10; matrix products, arithmetic and copies ran while one was open for 0% -> 0% of each run, Pallas kernels for 20% -> 22%
where the time goes in v5:
time: 119 us; the launch traced here: 118 us
  starting transfers between devices  55.4 us (47%)
  waiting for transfers between devices  31 us (26%)
  Pallas kernels  26.4 us (22%)
  local copies, waits for them, and re-layouts  4.21 us (4%)
    ppermute x36, starting transfers between devices, ring(): lax.ppermute(x, axis, [(j, (j + step) % count) for j in range(count)])  48 us
    ppermute x36, waiting for transfers between devices, ring(): lax.ppermute(x, axis, [(j, (j + step) % count) for j in range(count)])  31 us
    all_to_all x1, starting transfers between devices, step(): arrived = lax.all_to_all(dealt, ('z', 'y', 'x', 'c'), 0, 0, tiled=True)  7.47 us
    pallas_call x1, Pallas kernels, step(): make_own(0, False, True)(*rows_in, near[0], far[0], dq)  4.97 us
    unnamed x14, local copies, waits for them, and re-layouts  4.21 us
    pallas_call x1, Pallas kernels, step(): mine[3], other[3], dq = make_own(3, True, False)(*rows_in, near[3], far[3])  3.77 us
    pallas_call x1, Pallas kernels, step(): make_own(2, False, False)(*rows_in, near[2], far[2], dq)  3.73 us
    pallas_call x1, Pallas kernels, step(): pl.pallas_call(deal, grid=(4,), out_shape=shape((128, 16, HD), BF16), in_...  3.45 us
  transfers between devices with their start and end apart: 37, of which 10 were waited for; matrix products, arithmetic and copies ran while one was open for 0% of the time, Pallas kernels for 22%

profile of v5, /device:TPU:0, one launch (start us, length us, event | category | flops | bytes accessed | tf_op | source)
XLA Modules:
  0.0 118.2 jit_solution(17109485756691688381)
XLA Ops:
  2.6 3.2 %collective-permute-start.5 = (bf16[2,128,128]{2,1,0:T(8,128)(2,1)S(1)}, bf16[2,128,128]{2,1,0:T(8,128)(2,1)S(1)}, u32[]{:S(2)}, u32[]{:S(2)}) collective-permute-start(bf16[2,128,128]{2,1,0:T(8,128)(2,1)S(1)} %get-tuple-element.50), channel_id=1, source_target_pairs={{0,24},{8,0},{16,8},{24,16},{1,25},{9,1},{17,9},{25,17},{2,26},{10... | collective-permute-start | bytes 196616 | tf_op jit(solution)/shard_map/ppermute | solution.py:315
  5.8 2.2 %collective-permute-start.4 = (bf16[2,128,128]{2,1,0:T(8,128)(2,1)S(1)}, bf16[2,128,128]{2,1,0:T(8,128)(2,1)S(1)}, u32[]{:S(2)}, u32[]{:S(2)}) collective-permute-start(bf16[2,128,128]{2,1,0:T(8,128)(2,1)S(1)} %get-tuple-element.49), channel_id=1, source_target_pairs={{0,16},{8,24},{16,0},{24,8},{1,17},{9,25},{17,1},{25,9},{2,18},{10... | collective-permute-start | bytes 196616 | tf_op jit(solution)/shard_map/ppermute | solution.py:315
  8.0 4.1 %collective-permute-done.3 = bf16[2,128,128]{2,1,0:T(8,128)(2,1)S(1)} collective-permute-done((bf16[2,128,128]{2,1,0:T(8,128)(2,1)S(1)}, bf16[2,128,128]{2,1,0:T(8,128)(2,1)S(1)}, u32[]{:S(2)}, u32[]{:S(2)}) %collective-permute-start.3) | collective-permute-done | bytes 65568 | tf_op jit(solution)/shard_map/ppermute | solution.py:315
  12.1 2.8 %collective-permute-start.9 = (bf16[4,2,128,128]{3,2,1,0:T(8,128)(2,1)S(1)}, bf16[4,2,128,128]{3,2,1,0:T(8,128)(2,1)S(1)}, u32[]{:S(2)}, u32[]{:S(2)}) collective-permute-start(bf16[4,2,128,128]{3,2,1,0:T(8,128)(2,1)S(1)} %pad_maximum_fusion.km_ref), channel_id=1, source_target_pairs={{0,6},{2,0},{4,2},{6,4},{1,7},{3,1},{5,3},{7,5},{8,14},{10,8},{12,... | collective-permute-start | bytes 786440 | tf_op jit(solution)/shard_map/ppermute | solution.py:315
  18.3 4.1 %collective-permute-start.1 = (bf16[1040,128]{1,0:T(8,128)(2,1)}, bf16[1040,128]{1,0:T(8,128)(2,1)S(1)}, u32[]{:S(2)}, u32[]{:S(2)}) collective-permute-start(bf16[1040,128]{1,0:T(8,128)(2,1)} %get-tuple-element.43), channel_id=1, source_target_pairs={{0,16},{8,24},{16,0},{24,8},{1,17},{9,25},{17,1},{25,9},{2,18},{10... | collective-permute-start | bytes 798728 | tf_op jit(solution)/shard_map/ppermute | solution.py:315
  22.6 1.9 %collective-permute-start.13 = (bf16[4,2,128,128]{3,2,1,0:T(8,128)(2,1)S(1)}, bf16[4,2,128,128]{3,2,1,0:T(8,128)(2,1)S(1)}, u32[]{:S(2)}, u32[]{:S(2)}) collective-permute-start(bf16[4,2,128,128]{3,2,1,0:T(8,128)(2,1)S(1)} %pad_maximum_fusion.km_ref), channel_id=1, source_target_pairs={{0,32},{32,64},{64,96},{96,0},{1,33},{33,65},{65,97},{97,1},{2,34}... | collective-permute-start | bytes 786440 | tf_op jit(solution)/shard_map/ppermute | solution.py:315
  25.3 3.5 %deal.1 = bf16[128,16,128]{2,1,0:T(8,128)(2,1)} custom-call(bf16[128,2048]{1,0:T(8,128)(2,1)} %bitcast.21), custom_call_target="tpu_custom_call" | custom-call | tf_op jit(solution)/shard_map/deal/pallas_call | solution.py:333
  28.8 7.5 %all-to-all-start = ((bf16[128,16,128]{2,1,0:T(8,128)(2,1)}), bf16[128,16,128]{2,1,0:T(8,128)(2,1)S(1)}, u32[]{:S(2)}, u32[]{:S(2)}) async-start(bf16[128,16,128]{2,1,0:T(8,128)(2,1)} %deal.1), calls=%async_computation | async-start | bytes 1048576 | tf_op jit(solution)/shard_map/all_to_all | solution.py:342
  36.3 2.9 %collective-permute-start.14 = (bf16[4,2,128,128]{3,2,1,0:T(8,128)(2,1)S(1)}, bf16[4,2,128,128]{3,2,1,0:T(8,128)(2,1)S(1)}, u32[]{:S(2)}, u32[]{:S(2)}) collective-permute-start(bf16[4,2,128,128]{3,2,1,0:T(8,128)(2,1)S(1)} %pad_maximum_fusion.km_ref), channel_id=1, source_target_pairs={{0,64},{32,96},{64,0},{96,32},{1,65},{33,97},{65,1},{97,33},{2,66}... | collective-permute-start | bytes 786440 | tf_op jit(solution)/shard_map/ppermute | solution.py:315
  42.1 9.0 %collective-permute-done.14.refs_1_ = bf16[4,2,128,128]{3,2,1,0:T(8,128)(2,1)S(1)} collective-permute-done((bf16[4,2,128,128]{3,2,1,0:T(8,128)(2,1)S(1)}, bf16[4,2,128,128]{3,2,1,0:T(8,128)(2,1)S(1)}, u32[]{:S(2)}, u32[]{:S(2)}) %collective-permute-start.14) | collective-permute-done | bytes 262176 | tf_op jit(solution)/shard_map/ppermute | solution.py:315
  51.1 5.1 %collective-permute-done.15.refs_2_ = bf16[4,2,128,128]{3,2,1,0:T(8,128)(2,1)S(1)} collective-permute-done((bf16[4,2,128,128]{3,2,1,0:T(8,128)(2,1)S(1)}, bf16[4,2,128,128]{3,2,1,0:T(8,128)(2,1)S(1)}, u32[]{:S(2)}, u32[]{:S(2)}) %collective-permute-start.15) | collective-permute-done | bytes 262176 | tf_op jit(solution)/shard_map/ppermute | solution.py:315
  60.7 3.8 %shard_map.107 = (bf16[4,2,128,128]{3,2,1,0:T(8,128)(2,1)S(1)}, bf16[4,2,128,128]{3,2,1,0:T(8,128)(2,1)S(1)}, f32[4,128,512]{2,1,0:T(8,128)S(1)}) custom-call(bf16[4,512,128]{2,1,0:T(8,128)(2,1)S(1)} %get-tuple-element.45.q_ref, bf16[4,512,128]{2,1,0:T(8,128)(2,1)S(1)} %shard_map.103.grad_ref, f32[4,2,512]{2,1,0:T(2,128)S(1)} %get-tuple-element.46.stat_ref, ...), custom_call_target="tpu_custom_call" | custom-call | tf_op jit(solution)/shard_map/pallas_call | solution.py:352
  64.5 3.7 %shard_map.108 = (bf16[4,2,128,128]{3,2,1,0:T(8,128)(2,1)S(1)}, bf16[4,2,128,128]{3,2,1,0:T(8,128)(2,1)S(1)}, f32[4,128,512]{2,1,0:T(8,128)S(1)}) custom-call(bf16[4,512,128]{2,1,0:T(8,128)(2,1)S(1)} %get-tuple-element.45.q_ref, bf16[4,512,128]{2,1,0:T(8,128)(2,1)S(1)} %shard_map.103.grad_ref, ...), custom_call_target="tpu_custom_call", output_to_operand_aliasing={{2}: (5, {})} | custom-call | tf_op jit(solution)/shard_map/pallas_call | solution.py:353
  70.4 5.0 %collective-permute-start.29 = (bf16[3,4,2,128,128]{4,3,2,1,0:T(8,128)(2,1)S(1)}, bf16[3,4,2,128,128]{4,3,2,1,0:T(8,128)(2,1)S(1)}, u32[]{:S(2)}, u32[]{:S(2)}) collective-permute-start(bf16[3,4,2,128,128]{4,3,2,1,0:T(8,128)(2,1)S(1)} %get-tuple-element.69), channel_id=1, source_target_pairs={{0,7},{1,0},{2,1},{3,2},{4,3},{5,4},{6,5},{7,6},{8,15},{9,8},{10,9... | collective-permute-start | bytes 2359304 | tf_op jit(solution)/shard_map/ppermute | solution.py:315
  75.4 2.8 %shard_map.110 = (bf16[4,2,128,128]{3,2,1,0:T(8,128)(2,1)S(1)}, bf16[4,2,128,128]{3,2,1,0:T(8,128)(2,1)S(1)}, f32[4,128,512]{2,1,0:T(8,128)S(1)}) custom-call(bf16[4,512,128]{2,1,0:T(8,128)(2,1)S(1)} %get-tuple-element.45.q_ref, bf16[4,512,128]{2,1,0:T(8,128)(2,1)S(1)} %shard_map.103.grad_ref, ...), custom_call_target="tpu_custom_call", output_to_operand_aliasing={{2}: (5, {})} | custom-call | tf_op jit(solution)/shard_map/pallas_call | solution.py:359
  79.1 5.0 %shard_map.111 = (bf16[4,2,128,128]{3,2,1,0:T(8,128)(2,1)S(1)}, bf16[4,2,128,128]{3,2,1,0:T(8,128)(2,1)S(1)}, bf16[512,128]{1,0:T(8,128)(2,1)S(1)}, bf16[512,128...) custom-call(bf16[4,512,128]{2,1,0:T(8,128)(2,1)S(1)} %get-tuple-element.45.q_ref, ...), custom_call_target="tpu_custom_call" | custom-call | tf_op jit(solution)/shard_map/pallas_call | solution.py:360
  84.6 3.0 %collective-permute-start.28 = (bf16[4,2,128,128]{3,2,1,0:T(8,128)(2,1)S(1)}, bf16[4,2,128,128]{3,2,1,0:T(8,128)(2,1)S(1)}, u32[]{:S(2)}, u32[]{:S(2)}) collective-permute-start(bf16[4,2,128,128]{3,2,1,0:T(8,128)(2,1)S(1)} %add_convert_fusion), channel_id=1, source_target_pairs={{0,6},{2,0},{4,2},{6,4},{1,7},{3,1},{5,3},{7,5},{8,14},{10,8},{12,... | collective-permute-start | bytes 786440 | tf_op jit(solution)/shard_map/ppermute | solution.py:315
  89.3 4.6 %collective-permute-start.30 = (bf16[4,2,128,128]{3,2,1,0:T(8,128)(2,1)S(1)}, bf16[4,2,128,128]{3,2,1,0:T(8,128)(2,1)S(1)}, u32[]{:S(2)}, u32[]{:S(2)}) collective-permute-start(bf16[4,2,128,128]{3,2,1,0:T(8,128)(2,1)S(1)} %get-tuple-element.70), channel_id=1, source_target_pairs={{0,96},{32,0},{64,32},{96,64},{1,97},{33,1},{65,33},{97,65},{2,98}... | collective-permute-start | bytes 786440 | tf_op jit(solution)/shard_map/ppermute | solution.py:315
  93.9 2.4 %collective-permute-start.31 = (bf16[4,2,128,128]{3,2,1,0:T(8,128)(2,1)S(1)}, bf16[4,2,128,128]{3,2,1,0:T(8,128)(2,1)S(1)}, u32[]{:S(2)}, u32[]{:S(2)}) collective-permute-start(bf16[4,2,128,128]{3,2,1,0:T(8,128)(2,1)S(1)} %get-tuple-element.71), channel_id=1, source_target_pairs={{0,64},{32,96},{64,0},{96,32},{1,65},{33,97},{65,1},{97,33},{2,66}... | collective-permute-start | bytes 786440 | tf_op jit(solution)/shard_map/ppermute | solution.py:315
  96.3 2.3 %collective-permute-start.19 = (bf16[512,128]{1,0:T(8,128)(2,1)S(1)}, bf16[512,128]{1,0:T(8,128)(2,1)S(1)}, u32[]{:S(2)}, u32[]{:S(2)}) collective-permute-start(bf16[512,128]{1,0:T(8,128)(2,1)S(1)} %get-tuple-element.57), channel_id=1, source_target_pairs={{0,24},{8,0},{16,8},{24,16},{1,25},{9,1},{17,9},{25,17},{2,26},{10... | collective-permute-start | bytes 393224 | tf_op jit(solution)/shard_map/ppermute | solution.py:315
  102.4 2.2 %collective-permute-done.31.refs_5_ = bf16[4,2,128,128]{3,2,1,0:T(8,128)(2,1)S(1)} collective-permute-done((bf16[4,2,128,128]{3,2,1,0:T(8,128)(2,1)S(1)}, bf16[4,2,128,128]{3,2,1,0:T(8,128)(2,1)S(1)}, u32[]{:S(2)}, u32[]{:S(2)}) %collective-permute-start.31) | collective-permute-done | bytes 262176 | tf_op jit(solution)/shard_map/ppermute | solution.py:315
  104.6 3.9 %collective-permute-done.32.refs_6_ = bf16[4,2,128,128]{3,2,1,0:T(8,128)(2,1)S(1)} collective-permute-done((bf16[4,2,128,128]{3,2,1,0:T(8,128)(2,1)S(1)}, bf16[4,2,128,128]{3,2,1,0:T(8,128)(2,1)S(1)}, u32[]{:S(2)}, u32[]{:S(2)}) %collective-permute-start.32) | collective-permute-done | bytes 262176 | tf_op jit(solution)/shard_map/ppermute | solution.py:315
  108.7 2.1 %collective-permute-start.33 = (bf16[2,128,128]{2,1,0:T(8,128)(2,1)S(1)}, bf16[2,128,128]{2,1,0:T(8,128)(2,1)S(1)}, u32[]{:S(2)}, u32[]{:S(2)}) collective-permute-start(bf16[2,128,128]{2,1,0:T(8,128)(2,1)S(1)} %get-tuple-element.74), channel_id=1, source_target_pairs={{0,24},{8,0},{16,8},{24,16},{1,25},{9,1},{17,9},{25,17},{2,26},{10... | collective-permute-start | bytes 196616 | tf_op jit(solution)/shard_map/ppermute | solution.py:315
  113.9 2.9 %collective-permute-done.34.d2 = bf16[2,128,128]{2,1,0:T(8,128)(2,1)S(1)} collective-permute-done((bf16[2,128,128]{2,1,0:T(8,128)(2,1)S(1)}, bf16[2,128,128]{2,1,0:T(8,128)(2,1)S(1)}, u32[]{:S(2)}, u32[]{:S(2)}) %collective-permute-start.34) | collective-permute-done | bytes 65568 | tf_op jit(solution)/shard_map/ppermute | solution.py:315
  (82 shorter events, 27.4 us)
Async XLA Ops:
  12.1 12.4 %collective-permute-start.9 = (bf16[4,2,128,128]{3,2,1,0:T(8,128)(2,1)S(1)}, bf16[4,2,128,128]{3,2,1,0:T(8,128)(2,1)S(1)}, u32[]{:S(2)}, u32[]{:S(2)}) collective-permute-start(bf16[4,2,128,128]{3,2,1,0:T(8,128)(2,1)S(1)} %pad_maximum_fusion.km_ref), channel_id=1, source_target_pairs={{0,6},{2,0},{4,2},{6,4},{1,7},{3,1},{5,3},{7,5},{8,14},{10,8},{12,... | collective-permute-start | bytes 786440 | tf_op jit(solution)/shard_map/ppermute | solution.py:315
  18.2 18.0 %collective-permute-start = (bf16[1040,128]{1,0:T(8,128)(2,1)S(1)}, bf16[1040,128]{1,0:T(8,128)(2,1)S(1)}, u32[]{:S(2)}, u32[]{:S(2)}) collective-permute-start(bf16[1040,128]{1,0:T(8,128)(2,1)S(1)} %get-tuple-element.42), channel_id=1, source_target_pairs={{0,8},{8,16},{16,24},{24,0},{1,9},{9,17},{17,25},{25,1},{2,10},{10... | collective-permute-start | bytes 798728 | tf_op jit(solution)/shard_map/ppermute | solution.py:315
  18.3 20.9 %collective-permute-start.1 = (bf16[1040,128]{1,0:T(8,128)(2,1)}, bf16[1040,128]{1,0:T(8,128)(2,1)S(1)}, u32[]{:S(2)}, u32[]{:S(2)}) collective-permute-start(bf16[1040,128]{1,0:T(8,128)(2,1)} %get-tuple-element.43), channel_id=1, source_target_pairs={{0,16},{8,24},{16,0},{24,8},{1,17},{9,25},{17,1},{25,9},{2,18},{10... | collective-permute-start | bytes 798728 | tf_op jit(solution)/shard_map/ppermute | solution.py:315
  22.4 17.7 %collective-permute-start.2 = (bf16[1040,128]{1,0:T(8,128)(2,1)}, bf16[1040,128]{1,0:T(8,128)(2,1)S(1)}, u32[]{:S(2)}, u32[]{:S(2)}) collective-permute-start(bf16[1040,128]{1,0:T(8,128)(2,1)} %get-tuple-element.44), channel_id=1, source_target_pairs={{0,24},{8,0},{16,8},{24,16},{1,25},{9,1},{17,9},{25,17},{2,26},{10... | collective-permute-start | bytes 798728 | tf_op jit(solution)/shard_map/ppermute | solution.py:315
  22.6 19.0 %collective-permute-start.13 = (bf16[4,2,128,128]{3,2,1,0:T(8,128)(2,1)S(1)}, bf16[4,2,128,128]{3,2,1,0:T(8,128)(2,1)S(1)}, u32[]{:S(2)}, u32[]{:S(2)}) collective-permute-start(bf16[4,2,128,128]{3,2,1,0:T(8,128)(2,1)S(1)} %pad_maximum_fusion.km_ref), channel_id=1, source_target_pairs={{0,32},{32,64},{64,96},{96,0},{1,33},{33,65},{65,97},{97,1},{2,34}... | collective-permute-start | bytes 786440 | tf_op jit(solution)/shard_map/ppermute | solution.py:315
  24.5 17.1 %collective-permute-start.10 = (bf16[4,2,128,128]{3,2,1,0:T(8,128)(2,1)S(1)}, bf16[4,2,128,128]{3,2,1,0:T(8,128)(2,1)S(1)}, u32[]{:S(2)}, u32[]{:S(2)}) collective-permute-start(bf16[4,2,128,128]{3,2,1,0:T(8,128)(2,1)S(1)} %collective-permute-done.9.km_ref), channel_id=1, source_target_pairs={{0,6},{2,0},{4,2},{6,4},{1,7},{3,1},{5,3},{7,5},{8,14},{10,8},{12,... | collective-permute-start | bytes 786440 | tf_op jit(solution)/shard_map/ppermute | solution.py:315
  28.8 28.8 %all-to-all-start = ((bf16[128,16,128]{2,1,0:T(8,128)(2,1)}), bf16[128,16,128]{2,1,0:T(8,128)(2,1)S(1)}, u32[]{:S(2)}, u32[]{:S(2)}) async-start(bf16[128,16,128]{2,1,0:T(8,128)(2,1)} %deal.1), calls=%async_computation | async-start | bytes 1048576 | tf_op jit(solution)/shard_map/all_to_all | solution.py:342
  36.3 14.9 %collective-permute-start.14 = (bf16[4,2,128,128]{3,2,1,0:T(8,128)(2,1)S(1)}, bf16[4,2,128,128]{3,2,1,0:T(8,128)(2,1)S(1)}, u32[]{:S(2)}, u32[]{:S(2)}) collective-permute-start(bf16[4,2,128,128]{3,2,1,0:T(8,128)(2,1)S(1)} %pad_maximum_fusion.km_ref), channel_id=1, source_target_pairs={{0,64},{32,96},{64,0},{96,32},{1,65},{33,97},{65,1},{97,33},{2,66}... | collective-permute-start | bytes 786440 | tf_op jit(solution)/shard_map/ppermute | solution.py:315
  39.2 17.1 %collective-permute-start.15 = (bf16[4,2,128,128]{3,2,1,0:T(8,128)(2,1)S(1)}, bf16[4,2,128,128]{3,2,1,0:T(8,128)(2,1)S(1)}, u32[]{:S(2)}, u32[]{:S(2)}) collective-permute-start(bf16[4,2,128,128]{3,2,1,0:T(8,128)(2,1)S(1)} %pad_maximum_fusion.km_ref), channel_id=1, source_target_pairs={{0,96},{32,0},{64,32},{96,64},{1,97},{33,1},{65,33},{97,65},{2,98}... | collective-permute-start | bytes 786440 | tf_op jit(solution)/shard_map/ppermute | solution.py:315
  40.1 16.3 %collective-permute-start.7 = (bf16[4,2,128,128]{3,2,1,0:T(8,128)(2,1)S(1)}, bf16[4,2,128,128]{3,2,1,0:T(8,128)(2,1)S(1)}, u32[]{:S(2)}, u32[]{:S(2)}) collective-permute-start(bf16[4,2,128,128]{3,2,1,0:T(8,128)(2,1)S(1)} %pad_maximum_fusion.km_ref), channel_id=1, source_target_pairs={{0,2},{2,4},{4,6},{6,0},{1,3},{3,5},{5,7},{7,1},{8,10},{10,12},{12... | collective-permute-start | bytes 786440 | tf_op jit(solution)/shard_map/ppermute | solution.py:315
  41.6 19.0 %collective-permute-start.12 = (bf16[4,2,128,128]{3,2,1,0:T(8,128)(2,1)S(1)}, bf16[4,2,128,128]{3,2,1,0:T(8,128)(2,1)}, u32[]{:S(2)}, u32[]{:S(2)}) collective-permute-start(bf16[4,2,128,128]{3,2,1,0:T(8,128)(2,1)S(1)} %collective-permute-done.9.km_ref), channel_id=1, source_target_pairs={{0,1},{1,0},{2,3},{3,2},{4,5},{5,4},{6,7},{7,6},{8,9},{9,8},{10,11... | collective-permute-start | bytes 786440 | tf_op jit(solution)/shard_map/ppermute | solution.py:315
  41.6 22.9 %collective-permute-start.11 = (bf16[4,2,128,128]{3,2,1,0:T(8,128)(2,1)S(1)}, bf16[4,2,128,128]{3,2,1,0:T(8,128)(2,1)}, u32[]{:S(2)}, u32[]{:S(2)}) collective-permute-start(bf16[4,2,128,128]{3,2,1,0:T(8,128)(2,1)S(1)} %collective-permute-done.10.km_ref), channel_id=1, source_target_pairs={{0,1},{1,0},{2,3},{3,2},{4,5},{5,4},{6,7},{7,6},{8,9},{9,8},{10,11... | collective-permute-start | bytes 786440 | tf_op jit(solution)/shard_map/ppermute | solution.py:315
  51.1 17.6 %collective-permute-start.16 = (bf16[4,2,128,128]{3,2,1,0:T(8,128)(2,1)S(1)}, bf16[4,2,128,128]{3,2,1,0:T(8,128)(2,1)}, u32[]{:S(2)}, u32[]{:S(2)}) collective-permute-start(bf16[4,2,128,128]{3,2,1,0:T(8,128)(2,1)S(1)} %collective-permute-done.13.refs_0_), channel_id=1, source_target_pairs={{0,1},{1,2},{2,3},{3,4},{4,5},{5,6},{6,7},{7,0},{8,9},{9,10},{10,1... | collective-permute-start | bytes 786440 | tf_op jit(solution)/shard_map/ppermute | solution.py:315
  56.3 12.5 %collective-permute-start.17 = (bf16[4,2,128,128]{3,2,1,0:T(8,128)(2,1)S(1)}, bf16[4,2,128,128]{3,2,1,0:T(8,128)(2,1)}, u32[]{:S(2)}, u32[]{:S(2)}) collective-permute-start(bf16[4,2,128,128]{3,2,1,0:T(8,128)(2,1)S(1)} %collective-permute-done.14.refs_1_), channel_id=1, source_target_pairs={{0,1},{1,2},{2,3},{3,4},{4,5},{5,6},{6,7},{7,0},{8,9},{9,10},{10,1... | collective-permute-start | bytes 786440 | tf_op jit(solution)/shard_map/ppermute | solution.py:315
  56.4 12.4 %collective-permute-start.18 = (bf16[4,2,128,128]{3,2,1,0:T(8,128)(2,1)S(1)}, bf16[4,2,128,128]{3,2,1,0:T(8,128)(2,1)}, u32[]{:S(2)}, u32[]{:S(2)}) collective-permute-start(bf16[4,2,128,128]{3,2,1,0:T(8,128)(2,1)S(1)} %collective-permute-done.15.refs_2_), channel_id=1, source_target_pairs={{0,1},{1,2},{2,3},{3,4},{4,5},{5,6},{6,7},{7,0},{8,9},{9,10},{10,1... | collective-permute-start | bytes 786440 | tf_op jit(solution)/shard_map/ppermute | solution.py:315
  60.6 14.9 %collective-permute-start.8 = (bf16[4,2,128,128]{3,2,1,0:T(8,128)(2,1)S(1)}, bf16[4,2,128,128]{3,2,1,0:T(8,128)(2,1)S(1)}, u32[]{:S(2)}, u32[]{:S(2)}) collective-permute-start(bf16[4,2,128,128]{3,2,1,0:T(8,128)(2,1)S(1)} %collective-permute-done.7.km_ref), channel_id=1, source_target_pairs={{0,1},{1,0},{2,3},{3,2},{4,5},{5,4},{6,7},{7,6},{8,9},{9,8},{10,11... | collective-permute-start | bytes 786440 | tf_op jit(solution)/shard_map/ppermute | solution.py:315
  70.4 18.6 %collective-permute-start.29 = (bf16[3,4,2,128,128]{4,3,2,1,0:T(8,128)(2,1)S(1)}, bf16[3,4,2,128,128]{4,3,2,1,0:T(8,128)(2,1)S(1)}, u32[]{:S(2)}, u32[]{:S(2)}) collective-permute-start(bf16[3,4,2,128,128]{4,3,2,1,0:T(8,128)(2,1)S(1)} %get-tuple-element.69), channel_id=1, source_target_pairs={{0,7},{1,0},{2,1},{3,2},{4,3},{5,4},{6,5},{7,6},{8,15},{9,8},{10,9... | collective-permute-start | bytes 2359304 | tf_op jit(solution)/shard_map/ppermute | solution.py:315
  84.0 12.2 %collective-permute-start.22 = (bf16[4,2,128,128]{3,2,1,0:T(8,128)(2,1)S(1)}, bf16[4,2,128,128]{3,2,1,0:T(8,128)(2,1)S(1)}, u32[]{:S(2)}, u32[]{:S(2)}) collective-permute-start(bf16[4,2,128,128]{3,2,1,0:T(8,128)(2,1)S(1)} %get-tuple-element.61), channel_id=1, source_target_pairs={{0,1},{1,0},{2,3},{3,2},{4,5},{5,4},{6,7},{7,6},{8,9},{9,8},{10,11... | collective-permute-start | bytes 786440 | tf_op jit(solution)/shard_map/ppermute | solution.py:315
  84.6 11.6 %collective-permute-start.28 = (bf16[4,2,128,128]{3,2,1,0:T(8,128)(2,1)S(1)}, bf16[4,2,128,128]{3,2,1,0:T(8,128)(2,1)S(1)}, u32[]{:S(2)}, u32[]{:S(2)}) collective-permute-start(bf16[4,2,128,128]{3,2,1,0:T(8,128)(2,1)S(1)} %add_convert_fusion), channel_id=1, source_target_pairs={{0,6},{2,0},{4,2},{6,4},{1,7},{3,1},{5,3},{7,5},{8,14},{10,8},{12,... | collective-permute-start | bytes 786440 | tf_op jit(solution)/shard_map/ppermute | solution.py:315
  89.3 12.1 %collective-permute-start.30 = (bf16[4,2,128,128]{3,2,1,0:T(8,128)(2,1)S(1)}, bf16[4,2,128,128]{3,2,1,0:T(8,128)(2,1)S(1)}, u32[]{:S(2)}, u32[]{:S(2)}) collective-permute-start(bf16[4,2,128,128]{3,2,1,0:T(8,128)(2,1)S(1)} %get-tuple-element.70), channel_id=1, source_target_pairs={{0,96},{32,0},{64,32},{96,64},{1,97},{33,1},{65,33},{97,65},{2,98}... | collective-permute-start | bytes 786440 | tf_op jit(solution)/shard_map/ppermute | solution.py:315
  96.2 12.2 %collective-permute-start.32 = (bf16[4,2,128,128]{3,2,1,0:T(8,128)(2,1)S(1)}, bf16[4,2,128,128]{3,2,1,0:T(8,128)(2,1)S(1)}, u32[]{:S(2)}, u32[]{:S(2)}) collective-permute-start(bf16[4,2,128,128]{3,2,1,0:T(8,128)(2,1)S(1)} %get-tuple-element.72), channel_id=1, source_target_pairs={{0,32},{32,64},{64,96},{96,0},{1,33},{33,65},{65,97},{97,1},{2,34}... | collective-permute-start | bytes 786440 | tf_op jit(solution)/shard_map/ppermute | solution.py:315
  96.3 15.6 %collective-permute-start.19 = (bf16[512,128]{1,0:T(8,128)(2,1)S(1)}, bf16[512,128]{1,0:T(8,128)(2,1)S(1)}, u32[]{:S(2)}, u32[]{:S(2)}) collective-permute-start(bf16[512,128]{1,0:T(8,128)(2,1)S(1)} %get-tuple-element.57), channel_id=1, source_target_pairs={{0,24},{8,0},{16,8},{24,16},{1,25},{9,1},{17,9},{25,17},{2,26},{10... | collective-permute-start | bytes 393224 | tf_op jit(solution)/shard_map/ppermute | solution.py:315
  98.6 13.7 %collective-permute-start.20 = (bf16[512,128]{1,0:T(8,128)(2,1)S(1)}, bf16[512,128]{1,0:T(8,128)(2,1)S(1)}, u32[]{:S(2)}, u32[]{:S(2)}) collective-permute-start(bf16[512,128]{1,0:T(8,128)(2,1)S(1)} %get-tuple-element.58), channel_id=1, source_target_pairs={{0,16},{8,24},{16,0},{24,8},{1,17},{9,25},{17,1},{25,9},{2,18},{10... | collective-permute-start | bytes 393224 | tf_op jit(solution)/shard_map/ppermute | solution.py:315
  101.3 11.0 %collective-permute-start.21 = (bf16[512,128]{1,0:T(8,128)(2,1)S(1)}, bf16[512,128]{1,0:T(8,128)(2,1)S(1)}, u32[]{:S(2)}, u32[]{:S(2)}) collective-permute-start(bf16[512,128]{1,0:T(8,128)(2,1)S(1)} %get-tuple-element.59), channel_id=1, source_target_pairs={{0,8},{8,16},{16,24},{24,0},{1,9},{9,17},{17,25},{25,1},{2,10},{10... | collective-permute-start | bytes 393224 | tf_op jit(solution)/shard_map/ppermute | solution.py:315
  (20 other events, 115.7 us)
